TPU v7x, 32 devices: a whole 2x2x4 slice. The times are simulated.
32 devices in a mesh: lat: 4 (over x, core), lon: 8 (over z, y).
Axes of the slice: x: 2, y: 2, z: 4, core: 2. Of those that a mesh axis runs over, the one named last changes fastest.
Arguments:
- ensemble: float32 [48, 384, 4, 128], P('lat', 'lon'), may hold values from -6 to 6
- grad_increment: float32 [48, 384, 128], P('lat', 'lon'), may hold values from -6 to 6
- normalization: float32 [48, 384], P('lat', 'lon'), may hold values from 12 to 48
- lon_diffusion: float32 [48, 384], P('lat', 'lon'), may hold values from 1152 to 4608
- lat_diffusion: float32 [48, 384], P('lat', 'lon'), may hold values from 288 to 1152
- vert_diag: float32 [128], replicated, may hold values from 1 to 2
- vert_sub: float32 [127], replicated, may hold values from -0.8 to -0.3
Outputs:
- grad_alpha: float32 [48, 384, 4, 128], P('lat', 'lon')
All inputs are finite; a program needn't handle non-finite values.
Results may differ from a plain program's by a relative error of at most 0.0003.
Values sent between devices are 32-bit elements; how exact they have to be, the bound alone decides.
No kernel may reach another device: no remote copies, remote signals or barrier semaphores. Data moves between devices by JAX's collectives and lax.ppermute only.
A program may use at most 64 MiB of HBM per device.

v0:
```python
import jax
import jax.numpy as jnp
from jax import lax
from jax.sharding import PartitionSpec as P

HIGHEST = lax.Precision.HIGHEST


def shifted(value, axis, steps):
    count = lax.axis_size(axis)
    pairs = [(source, (source + steps) % count) for source in range(count)]
    return lax.ppermute(value, axis, pairs)


def shifted_2(value, axis, steps):
    count = lax.axis_size(axis)
    initial, last = (max(0, -steps), min(count, count - steps))
    return lax.ppermute(value, axis, [(source, source + steps) for source in range(initial, last)])


def block_inverse(edges, base_vals):
    block_len = edges.shape[-1]
    row_ids = lax.broadcasted_iota(jnp.int32, (block_len, block_len), 0)
    col_ids = lax.broadcasted_iota(jnp.int32, (block_len, block_len), 1)
    leading = jnp.arange(block_len) == 0
    earlier = jnp.concatenate([jnp.zeros_like(edges[:, :1]), edges[:, :-1]], axis=1)
    diagonal = jnp.where(leading[None, :], 1.0, base_vals + earlier + edges)
    couple_vals = jnp.where(leading[None, :], 0.0, -edges)
    upper_mask = (col_ids == row_ids + 1).astype(jnp.float32)
    eye_mask = (col_ids == row_ids).astype(jnp.float32)
    matrix = (
        diagonal[:, :, None] * eye_mask
        + couple_vals[:, :, None] * upper_mask
        + couple_vals[:, None, :] * upper_mask.T
    )
    factor = jnp.linalg.cholesky(matrix)
    identity = jnp.broadcast_to(eye_mask, matrix.shape)
    inverse = jax.scipy.linalg.cho_solve((factor, True), identity)
    corner = ((row_ids == 0) & (col_ids == 0)).astype(jnp.float32)
    return inverse - corner


def interface_values(inverse, edges, base_vals, first_row, last_row, sep_rhs):
    block_len = inverse.shape[-1]
    left_edge = edges[:, 0]
    right_edge = edges[:, block_len - 1]
    own_diag = base_vals[:, 0] + left_edge - left_edge * left_edge * inverse[:, 1, 1]
    next_diag = right_edge - right_edge * right_edge * inverse[:, block_len - 1, block_len - 1]
    coupling = -left_edge * right_edge * inverse[:, 1, block_len - 1]
    own_rhs = sep_rhs + left_edge[:, None] * first_row
    next_rhs = right_edge[:, None] * last_row
    return (own_diag, next_diag, coupling, own_rhs, next_rhs)


def interface_solve(diag_sum, coupling, rhs_sum):
    part_count = diag_sum.shape[0]
    row_ids = lax.broadcasted_iota(jnp.int32, (part_count, part_count), 0)
    col_ids = lax.broadcasted_iota(jnp.int32, (part_count, part_count), 1)
    follow = (col_ids == (row_ids + 1) % part_count).astype(jnp.float32)
    eye_mask = (col_ids == row_ids).astype(jnp.float32)
    diag_t = diag_sum.T
    couple_t = coupling.T
    system = (
        diag_t[:, :, None] * eye_mask
        + couple_t[:, :, None] * follow
        + couple_t[:, None, :] * follow.T
    )
    factor = jnp.linalg.cholesky(system)
    inverse = jax.scipy.linalg.cho_solve((factor, True), jnp.broadcast_to(eye_mask, system.shape))
    return jnp.einsum("bqp,pbx->qbx", inverse, rhs_sum, precision=HIGHEST)


def spike_columns(inverse, edges):
    block_len = inverse.shape[-1]
    leading = (jnp.arange(block_len) == 0).astype(jnp.float32)
    spike_first = edges[:, 0:1] * inverse[:, :, 1] + leading[None, :]
    spike_last = edges[:, block_len - 1 : block_len] * inverse[:, :, block_len - 1]
    return (spike_first, spike_last)


def lon_blocks_solve(blocks, edges):
    block_len = blocks.shape[1]
    unit_base = jnp.ones_like(edges)
    inverse = block_inverse(edges, unit_base)
    interior = jnp.einsum("bij,bjx->bix", inverse, blocks, precision=HIGHEST)
    values = interface_values(
        inverse, edges, unit_base, interior[:, 1], interior[:, block_len - 1], blocks[:, 0]
    )
    return (inverse, interior, values)


def lon_finish(interior, inverse, edges, sep_own, sep_next):
    spike_first, spike_last = spike_columns(inverse, edges)
    return (
        interior
        + spike_first[:, :, None] * sep_own[:, None, :]
        + spike_last[:, :, None] * sep_next[:, None, :]
    )


def longitude_split(weighted, lon_diffusion):
    inverse, interior, values = lon_blocks_solve(weighted, lon_diffusion)
    own_diag, next_diag, coupling, own_rhs, next_rhs = values
    prior_rhs = shifted(next_rhs, "lon", 1)
    gathered = (
        lax.all_gather(own_diag[None], "lon", axis=0, tiled=True),
        lax.all_gather(next_diag[None], "lon", axis=0, tiled=True),
        lax.all_gather(coupling[None], "lon", axis=0, tiled=True),
        lax.all_gather((own_rhs + prior_rhs)[None], "lon", axis=0, tiled=True),
    )
    diag_sum = gathered[0] + jnp.roll(gathered[1], 1, axis=0)
    separators = interface_solve(diag_sum, gathered[2], gathered[3])
    part_count = lax.axis_size("lon")
    cycle_pos = lax.axis_index("lon")
    sep_own = lax.dynamic_index_in_dim(separators, cycle_pos, 0, keepdims=False)
    sep_next = lax.dynamic_index_in_dim(separators, (cycle_pos + 1) % part_count, 0, keepdims=False)
    return lon_finish(interior, inverse, lon_diffusion, sep_own, sep_next)


def latitude_split(along_lon, lat_diffusion):
    part_count = lax.axis_size("lat")
    band_pos = lax.axis_index("lat")
    block_len = along_lon.shape[0]
    lat_total = part_count * block_len
    global_rows = band_pos * block_len + jnp.arange(block_len, dtype=jnp.int32)
    latitude = -jnp.pi / 2 + (global_rows.astype(jnp.float32) + 0.5) * jnp.pi / lat_total
    cosine = jnp.cos(latitude)
    edge_keep = (global_rows < lat_total - 1).astype(jnp.float32)
    edges = jnp.transpose(lat_diffusion * edge_keep[:, None])
    base_vals = jnp.broadcast_to(cosine[None, :], edges.shape)
    inverse = block_inverse(edges, base_vals)
    interior = jnp.einsum("bij,jbx->ibx", inverse, along_lon, precision=HIGHEST)
    values = interface_values(
        inverse, edges, base_vals, interior[1], interior[block_len - 1], along_lon[0]
    )
    own_diag, next_diag, coupling, own_rhs, next_rhs = values
    prior_rhs = shifted_2(next_rhs, "lat", 1)
    gathered = (
        lax.all_gather(own_diag[None], "lat", axis=0, tiled=True),
        lax.all_gather(next_diag[None], "lat", axis=0, tiled=True),
        lax.all_gather(coupling[None], "lat", axis=0, tiled=True),
        lax.all_gather((own_rhs + prior_rhs)[None], "lat", axis=0, tiled=True),
    )
    diag_sum = gathered[0] + jnp.roll(gathered[1], 1, axis=0)
    separators = interface_solve(diag_sum, gathered[2], gathered[3])
    sep_own = lax.dynamic_index_in_dim(separators, band_pos, 0, keepdims=False)
    sep_next = lax.dynamic_index_in_dim(separators, (band_pos + 1) % part_count, 0, keepdims=False)
    spike_first, spike_last = spike_columns(inverse, edges)
    solved = (
        interior
        + spike_first.T[:, :, None] * sep_own[None]
        + spike_last.T[:, :, None] * sep_next[None]
    )
    return cosine[:, None, None] * solved


def shards(
    ensemble, grad_increment, normalization, lon_diffusion, lat_diffusion, vert_diag, vert_sub
):
    lat_rows, lon_cols, members, levels = ensemble.shape
    weighted = normalization[:, :, None, None] * ensemble * grad_increment[:, :, None, :]
    weighted = weighted.reshape(lat_rows, lon_cols, members * levels)
    along_lon = longitude_split(weighted, lon_diffusion)
    along_lat = latitude_split(along_lon, lat_diffusion)
    along_lat = along_lat.reshape(lat_rows, lon_cols, members, levels)
    factor = jnp.diag(vert_diag) + jnp.diag(vert_sub, -1)
    identity = jnp.eye(levels, dtype=jnp.float32)
    vert_inv = jax.scipy.linalg.cho_solve((factor, True), identity)
    return jnp.einsum("abml,lk->abmk", along_lat, vert_inv, precision=HIGHEST)


def solution(mesh):
    in_specs = (
        P("lat", "lon", None, None),
        P("lat", "lon", None),
        P("lat", "lon"),
        P("lat", "lon"),
        P("lat", "lon"),
        P(),
        P(),
    )
    out_specs = P("lat", "lon", None, None)
    return jax.shard_map(shards, mesh=mesh, in_specs=in_specs, out_specs=out_specs, check_vma=False)
```

profile of v0, /device:TPU:0, one launch (start us, length us, event | category | flops | bytes accessed | tf_op | source)
XLA Modules:
  0.0 350.6 jit_solution(8453644844362742854)
XLA Ops:
  0.0 0.5 iota_compare_fusion.22
  0.6 1.5 slice_reduce_fusion.4
  2.2 0.9 negate_select_fusion.1
  3.3 52.8 %custom-call.51 = f32[12,48,48]{2,1,0:T(8,128)S(1)} custom-call(f32[12,48,48]{2,1,0:T(8,128)S(1)} %fusion.10), custom_call_target="Cholesky" | custom-call | tf_op jit(solution)/shard_map/jit(cholesky)/cholesky | solution.py:36
  56.4 44.3 %custom-call.52 = f32[12,1,48,48]{2,3,1,0:T(8,128)S(1)} custom-call(f32[12,1,48,48]{3,2,1,0:T(8,128)S(1)} %select_bitcast_fusion), custom_call_target="InvertDiagBlocksLowerTriangular" | custom-call | tf_op jit(solution)/shard_map/jit(_cho_solve)/vmap()/triangular_solve | solution.py:38
  100.7 0.7 fusion.12
  101.4 0.8 multiply_multiply_fusion
  102.2 0.5 reshape.798
  102.6 0.6 convolution_subtract_fusion.1
  103.2 1.2 fusion.76
  104.4 0.6 fusion.74
  105.1 0.7 bitcast_multiply_fusion
  105.7 3.0 collective-permute-start
  108.8 0.6 add_cosine_fusion
  109.4 0.6 compare_and_fusion
  110.0 0.6 iota_compare_fusion.20
  110.5 0.6 iota_compare_fusion.19
  111.1 0.6 iota_compare_fusion.17
  111.7 0.6 iota_compare_fusion.16
  112.3 0.5 iota_compare_fusion.21
  112.8 0.6 compare_select_fusion
  113.4 0.6 fusion.57
  114.0 0.3 slice_reduce_fusion.5
  114.5 0.5 slice_bitcast_fusion.8
  115.4 0.3 fusion.6
  115.6 52.8 %custom-call.55 = f32[48,12,12]{2,1,0:T(8,128)S(1)} custom-call(f32[48,12,12]{2,1,0:T(8,128)S(1)} %fusion.6), custom_call_target="Cholesky" | custom-call | tf_op jit(solution)/shard_map/jit(cholesky)/cholesky | solution.py:36
  168.9 1.6 custom-call.56
  170.7 0.8 fusion.16
  171.6 0.5 convolution_subtract_fusion
  172.1 1.4 slice_reduce_fusion
  173.8 9.8 %custom-call.59 = f32[1,128,128]{1,2,0:T(8,128)S(1)} custom-call(f32[1,128,128]{2,1,0:T(8,128)S(1)} %add_select_fusion), custom_call_target="InvertDiagBlocksLowerTriangular" | custom-call | tf_op jit(solution)/shard_map/jit(_cho_solve)/triangular_solve | solution.py:168
  183.6 0.9 fusion.26
  184.5 19.3 %all-gather.5 = f32[8,1,12]{2,1,0:T(1,128)S(1)} all-gather(f32[1,1,12]{2,1,0:T(1,128)S(1)} %get-tuple-element.39), channel_id=1, replica_groups=mesh['lat'=4,'lon'=8] {'lon'}, dimensions={0}, use_global_device_ids=true | all-gather | bytes 432 | tf_op jit(solution)/shard_map/all_gather | solution.py:108
  203.8 16.3 %all-gather.3 = f32[8,1,12]{2,1,0:T(1,128)S(1)} all-gather(f32[1,1,12]{2,1,0:T(1,128)S(1)} %fusion.70), channel_id=1, replica_groups=mesh['lat'=4,'lon'=8] {'lon'}, dimensions={0}, use_global_device_ids=true | all-gather | bytes 432 | tf_op jit(solution)/shard_map/all_gather | solution.py:106
  220.0 18.3 %all-gather.4 = f32[8,1,12]{2,1,0:T(1,128)S(1)} all-gather(f32[1,1,12]{2,1,0:T(1,128)S(1)} %get-tuple-element.40), channel_id=1, replica_groups=mesh['lat'=4,'lon'=8] {'lon'}, dimensions={0}, use_global_device_ids=true | all-gather | bytes 432 | tf_op jit(solution)/shard_map/all_gather | solution.py:107
  238.7 8.8 %custom-call.53 = f32[12,8,8]{2,1,0:T(8,128)S(1)} custom-call(f32[12,8,8]{2,1,0:T(8,128)S(1)} %fusion.29), custom_call_target="Cholesky" | custom-call | tf_op jit(solution)/shard_map/jit(cholesky)/cholesky | solution.py:68
  247.4 0.7 select_reduce_fusion.2
  248.3 0.7 select_bitcast_fusion.2
  249.0 7.5 %custom-call.54 = f32[12,1,8,8]{2,3,1,0:T(8,128)S(1)} custom-call(f32[12,1,8,8]{3,2,1,0:T(8,128)S(1)} %select_bitcast_fusion.2), custom_call_target="InvertDiagBlocksLowerTriangular" | custom-call | tf_op jit(solution)/shard_map/jit(_cho_solve)/vmap()/triangular_solve | solution.py:69
  256.5 0.3 fusion.32
  257.1 1.3 fusion.61
  258.4 5.0 %all-gather.8 = f32[4,1,48]{2,1,0:T(1,128)S(1)} all-gather(f32[1,1,48]{2,1,0:T(1,128)S(1)} %get-tuple-element.32), channel_id=1, replica_groups=mesh['lat'=4,'lon'=8] {'lat'}, dimensions={0}, use_global_device_ids=true | all-gather | bytes 960 | tf_op jit(solution)/shard_map/all_gather | solution.py:141
  263.4 5.0 %all-gather.7 = f32[4,1,48]{2,1,0:T(1,128)S(1)} all-gather(f32[1,1,48]{2,1,0:T(1,128)S(1)} %get-tuple-element.33), channel_id=1, replica_groups=mesh['lat'=4,'lon'=8] {'lat'}, dimensions={0}, use_global_device_ids=true | all-gather | bytes 960 | tf_op jit(solution)/shard_map/all_gather | solution.py:140
  268.5 5.2 %all-gather.6 = f32[4,1,48]{2,1,0:T(1,128)S(1)} all-gather(f32[1,1,48]{2,1,0:T(1,128)S(1)} %get-tuple-element.34), channel_id=1, replica_groups=mesh['lat'=4,'lon'=8] {'lat'}, dimensions={0}, use_global_device_ids=true | all-gather | bytes 960 | tf_op jit(solution)/shard_map/all_gather | solution.py:139
  273.9 0.8 fusion.55
  274.7 0.9 fusion.20
  275.6 18.1 %custom-call.57 = f32[48,4,4]{2,1,0:T(4,128)S(1)} custom-call(f32[48,4,4]{2,1,0:T(4,128)S(1)} %fusion.20), custom_call_target="Cholesky" | custom-call | tf_op jit(solution)/shard_map/jit(cholesky)/cholesky | solution.py:68
  294.4 0.6 fusion.34
  295.0 0.4 fusion.77
  295.5 0.7 fusion.48
  296.2 0.7 add_bitcast_fusion
  296.9 0.6 multiply_bitcast_fusion.1
  297.8 0.8 fusion.39
  298.6 30.7 %all-gather.2 = f32[8,12,512]{2,1,0:T(8,128)S(1)} all-gather(f32[1,12,512]{2,1,0:T(8,128)S(1)} %fusion.39), channel_id=2, replica_groups=mesh['lat'=4,'lon'=8] {'lon'}, dimensions={0}, use_global_device_ids=true | all-gather | bytes 221184 | tf_op jit(solution)/shard_map/all_gather | solution.py:109
  329.3 0.4 fusion.14
  329.8 0.3 multiply_add_fusion
  330.1 2.4 fusion
  332.5 0.7 copy.282
  333.3 1.3 collective-permute-start.1
  334.8 0.7 collective-permute-done.1
  335.6 10.3 %all-gather.1 = f32[192,512]{1,0:T(8,128)S(1)} all-gather(f32[48,512]{1,0:T(8,128)S(1)} %fusion.24), channel_id=3, replica_groups=mesh['lat'=4,'lon'=8] {'lat'}, dimensions={0}, use_global_device_ids=true | all-gather | bytes 491520 | tf_op jit(solution)/shard_map/all_gather | solution.py:142
  345.9 1.0 fusion.7
  347.2 1.9 fusion.2
  349.1 1.5 copy.229
  (108 shorter events, 4.6 us)
Async XLA Ops:
  0.0 101.3 %copy-start.6 = (f32[12,48]{1,0:T(8,128)S(1)}, f32[12,48]{1,0:T(8,128)}, u32[]{:S(2)}) copy-start(f32[12,48]{1,0:T(8,128)} %param.9) | copy-start | bytes 6916
  0.0 101.3 %copy-start.1 = (f32[12,48,128]{2,1,0:T(8,128)S(1)}, f32[12,48,128]{2,1,0:T(8,128)}, u32[]{:S(2)}) copy-start(f32[12,48,128]{2,1,0:T(8,128)} %param.8) | copy-start | bytes 884740
  0.0 101.3 %copy-start = (f32[12,48,4,128]{3,2,1,0:T(4,128)S(1)}, f32[12,48,4,128]{3,2,1,0:T(4,128)}, u32[]{:S(2)}) copy-start(f32[12,48,4,128]{3,2,1,0:T(4,128)} %param.7) | copy-start | bytes 3538948
  2.1 182.4 %copy-start.7 = (f32[12]{0:T(128)}, f32[12]{0:T(128)S(1)}, u32[]{:S(2)}) copy-start(f32[12]{0:T(128)S(1)} %get-tuple-element.15) | copy-start | bytes 148
  103.2 11.2 %copy-start.9 = (f32[12,48]{1,0:T(8,128)S(1)}, f32[12,48]{1,0:T(8,128)}, u32[]{:S(2)}) copy-start(f32[12,48]{1,0:T(8,128)} %param.11) | copy-start | bytes 6916
  105.7 192.0 %collective-permute-start = (f32[12,512]{1,0:T(8,128)}, f32[12,512]{1,0:T(8,128)}, u32[]{:S(2)}, u32[]{:S(2)}) collective-permute-start(f32[12,512]{1,0:T(8,128)} %bitcast_multiply_fusion), channel_id=1, source_target_pairs={{0,1},{1,2},{2,3},{3,4},{4,5},{5,6},{6,7},{7,0},{8,9},{9,10},{10,1... | collective-permute-start | bytes 73736 | tf_op jit(solution)/shard_map/ppermute | solution.py:12
  108.8 6.4 %copy-start.12 = (f32[12]{0:T(128)}, f32[12]{0:T(128)S(1)}, u32[]{:S(2)}) copy-start(f32[12]{0:T(128)S(1)} %add_cosine_fusion.1) | copy-start | bytes 148
  114.5 0.9 copy-start.4
  170.7 2.8 copy-start.17
  170.7 2.9 copy-start.14
  172.1 121.8 %copy-start.16 = (pred[4,4]{1,0:T(4,128)(4,1)S(1)}, pred[4,4]{1,0:T(4,128)(4,1)}, u32[]{:S(2)}) copy-start(pred[4,4]{1,0:T(4,128)(4,1)} %iota_compare_fusion.19) | copy-start | bytes 52
  172.1 121.9 %copy-start.15 = (pred[4,4]{1,0:T(4,128)(4,1)S(1)}, pred[4,4]{1,0:T(4,128)(4,1)}, u32[]{:S(2)}) copy-start(pred[4,4]{1,0:T(4,128)(4,1)} %iota_compare_fusion.20) | copy-start | bytes 52
  172.1 122.3 %copy-start.5 = (f32[4,4]{1,0:T(4,128)S(1)}, f32[4,4]{1,0:T(4,128)}, u32[]{:S(2)}) copy-start(f32[4,4]{1,0:T(4,128)} %get-tuple-element.57) | copy-start | bytes 196
  173.5 124.3 %copy-start.3 = (f32[12,1,512]{2,1,0:T(1,128)S(1)}, f32[12,1,512]{2,1,0:T(1,128)}, u32[]{:S(2)}) copy-start(f32[12,1,512]{2,1,0:T(1,128)} %get-tuple-element.18) | copy-start | bytes 73732
  238.6 56.8 %copy-start.8 = (f32[12]{0:T(128)S(1)}, f32[12]{0:T(128)}, u32[]{:S(2)}) copy-start(f32[12]{0:T(128)} %copy-done.7) | copy-start | bytes 148
  332.5 0.7 copy-start.11
  332.5 2.1 copy-start.2
  332.5 3.0 copy-start.10
  333.3 2.2 collective-permute-start.1
  335.6 11.6 %copy-start.13 = (f32[12]{0:T(128)S(1)}, f32[12]{0:T(128)}, u32[]{:S(2)}) copy-start(f32[12]{0:T(128)} %copy-done.12) | copy-start | bytes 148
where the time goes:
time: 351 us
  other arithmetic  215 us (61%)
  blocking collectives  110 us (31%)
  matrix products  12 us (3%)
  local copies, waits for them, and re-layouts  7.52 us (2%)
  starting transfers between devices  4.29 us (1%)
    another operation x8, other arithmetic, block_inverse(): factor = jnp.linalg.cholesky(matrix)  106 us
    another operation x6, other arithmetic, block_inverse(): inverse = jax.scipy.linalg.cho_solve((factor, True), identity)  46.1 us
    all_gather x1, blocking collectives, longitude_split(): lax.all_gather((own_rhs + prior_rhs)[None], 'lon', axis=0, tiled=True)  30.7 us
    another operation x8, other arithmetic, interface_solve(): factor = jnp.linalg.cholesky(system)  29 us
    all_gather x1, blocking collectives, longitude_split(): lax.all_gather(coupling[None], 'lon', axis=0, tiled=True)  19.3 us
    all_gather x1, blocking collectives, longitude_split(): lax.all_gather(next_diag[None], 'lon', axis=0, tiled=True)  18.3 us
    all_gather x1, blocking collectives, longitude_split(): lax.all_gather(own_diag[None], 'lon', axis=0, tiled=True)  16.3 us
    all_gather x1, blocking collectives, latitude_split(): lax.all_gather((own_rhs + prior_rhs)[None], 'lat', axis=0, tiled=True)  10.3 us
  transfers between devices with their start and end apart: 2, of which 1 were waited for; matrix products, arithmetic and copies ran while one was open for 34% of the time, Pallas kernels for 0%

commit v1 on v0

v1 whole, which is shorter than its diff:
```python
import functools
import math

import jax
import jax.numpy as jnp
from jax import lax
from jax.experimental import pallas as pl
from jax.experimental.pallas import tpu as pltpu
from jax.sharding import PartitionSpec as P

F32 = jnp.float32
LANES = 128
CHUNK = 16
PART = 64
VMEM_BYTES = 16 * 2**20


def call(kernel, outs, scratch=(), in_specs=None, out_specs=None, cost=None):
    specs = {k: v for k, v in (("in_specs", in_specs), ("out_specs", out_specs)) if v is not None}
    return pl.pallas_call(
        kernel,
        out_shape=outs,
        **specs,
        scratch_shapes=scratch,
        cost_estimate=cost,
        compiler_params=pltpu.CompilerParams(vmem_limit_bytes=VMEM_BYTES),
    )


def shape(*dims, dtype=F32):
    return jax.ShapeDtypeStruct(dims, dtype)


def lane_of(value, lane, rows):
    return jnp.broadcast_to(value[:, lane : lane + 1], (rows, LANES))


def split_rows(value):
    rest = value.shape[0] - 8
    fill = jnp.ones((8 - rest, value.shape[1]), F32)
    return value[:8], jnp.concatenate([value[8:], fill], axis=0)


def lon_sweep_kernel(ens_hbm, grad_hbm, norm_ref, diff_ref, part_ref, phi_ref, psi_ref, pay_ref, ens, grad, sem):
    rows, cells, _ = ens_hbm.shape
    cols = grad_hbm.shape[1]
    memb = cells // cols
    rest = rows - 8
    copies = []
    for c in range(cols // CHUNK):
        group = []
        for j in range(rows):
            g_rows, e_rows = pl.ds(c * CHUNK, CHUNK), pl.ds(c * CHUNK * memb, CHUNK * memb)
            group.append(pltpu.make_async_copy(grad_hbm.at[j, g_rows], grad.at[g_rows, j, :], sem.at[c, 0, j]))
            group.append(pltpu.make_async_copy(ens_hbm.at[j, e_rows], ens.at[e_rows, j, :], sem.at[c, 1, j]))
        copies.append(group)
    for group in copies:
        for copy in group:
            copy.start()
    step = split_rows(1.0 / diff_ref[...])
    norm = split_rows(norm_ref[...])
    zero, one = jnp.zeros((8, LANES), F32), jnp.ones((8, LANES), F32)
    u = [[zero] * memb for _ in range(2)]
    flux = [[zero] * memb for _ in range(2)]
    phi, phi_f, psi, psi_f = [one] * 2, [zero] * 2, [zero] * 2, [one] * 2
    for i in range(cols):
        if i % CHUNK == 0:
            for copy in copies[i // CHUNK]:
                copy.wait()
        for g in range(2):
            tile = slice(8 * g, 8 * g + 8)
            t = lane_of(step[g], i, 8)
            w = lane_of(norm[g], i, 8) * grad[i, tile, :]
            for m in range(memb):
                part_ref[i * memb + m, tile, :] = u[g][m]
                f = w * ens[i * memb + m, tile, :]
                flux[g][m] = flux[g][m] + (u[g][m] - f)
                u[g][m] = u[g][m] + t * flux[g][m]
            phi_ref[i, tile, :] = phi[g]
            psi_ref[i, tile, :] = psi[g]
            phi_f[g] = phi_f[g] + phi[g]
            psi_f[g] = psi_f[g] + psi[g]
            phi[g] = phi[g] + t * phi_f[g]
            psi[g] = psi[g] + t * psi_f[g]
    lanes = lax.broadcasted_iota(jnp.int32, (8, LANES), 1)
    half = memb * rows
    for g in range(2):
        b = 1.0 / psi[g]
        a, d = phi[g] * b, psi_f[g] * b
        first = 0 if g == 0 else 8 * memb
        size = 8 if g == 0 else rest
        for m in range(memb):
            pay_ref[first + m * size : first + (m + 1) * size, :] = (u[g][m] * b)[:size]
            pay_ref[half + first + m * size : half + first + (m + 1) * size, :] = (flux[g][m] - d * u[g][m])[:size]
        coef = jnp.where(lanes == 0, a, jnp.where(lanes == 1, b, d))
        for k in range(8 // size):
            row = 2 * half + 8 * g + k * size
            pay_ref[row : row + size, :] = coef[:size]


def lon_expand(tiles, memb, rest):
    return jnp.concatenate([tiles[:8]] * memb + [tiles[8:]] * (memb * rest // 8), axis=0)


def lon_parts(pay, half):
    coef = pay[2 * half :]
    a, b, d = (lane_of(coef, k, 16) for k in range(3))
    return pay[:half], pay[half : 2 * half], a, b, d


def lon_join(left, right, memb, rest):
    half = memb * (8 + rest)
    lh1, lh2, la, lb, ld = lon_parts(left, half)
    rh1, rh2, ra, rb, rd = lon_parts(right, half)
    inv = 1.0 / (ld + ra)
    ca, cb = lb * inv, rb * inv
    grow = functools.partial(lon_expand, memb=memb, rest=rest)
    total = lh2 + rh1
    s = total * grow(inv)
    h1 = lh1 + grow(ca) * total
    h2 = rh2 + grow(cb) * total
    return h1, h2, la - lb * ca, lb * cb, rd - rb * cb, s, ca, cb


def on_right(axis, level):
    return ((lax.axis_index(axis) >> level) & 1) == 1


def lon_merge_kernel(mine_ref, other_ref, pay_ref, back_ref, *, level, memb, rest):
    right = on_right("lon", level)
    mine, other = mine_ref[...], other_ref[...]
    h1, h2, a, b, d, s, ca, cb = lon_join(
        jnp.where(right, other, mine), jnp.where(right, mine, other), memb, rest
    )
    half = h1.shape[0]
    lanes = lax.broadcasted_iota(jnp.int32, a.shape, 1)
    pay_ref[:half, :] = h1
    pay_ref[half : 2 * half, :] = h2
    pay_ref[2 * half :, :] = jnp.where(lanes == 0, a, jnp.where(lanes == 1, b, d))
    back_ref[:half, :] = s
    back_ref[half : half + 16, :] = ca
    back_ref[half + 16 :, :] = cb


def times_inverse(rows, weights):
    high = rows.astype(jnp.bfloat16)
    low = (rows - high.astype(F32)).astype(jnp.bfloat16)
    out = jnp.dot(jnp.concatenate([high, low], axis=1), weights, preferred_element_type=F32)
    return out[:, :LANES] + out[:, LANES:]


def vertical_kernel(diag_ref, sub_ref, part_ref, y_ref, weights_ref, line, ratio, inverse, factor, *, stride, rows):
    levels = diag_ref.shape[1]
    line[...] = jnp.zeros_like(line)
    line[0:1, 0 : levels - 1] = sub_ref[...]
    row_ids = lax.broadcasted_iota(jnp.int32, (levels, levels), 0)
    col_ids = lax.broadcasted_iota(jnp.int32, (levels, levels), 1)
    diag = jnp.sum(jnp.where(row_ids == col_ids, diag_ref[...], 0.0), axis=1, keepdims=True)
    below = jnp.sum(jnp.where(row_ids == col_ids + 1, line[0:1, :], 0.0), axis=1, keepdims=True)
    inv = 1.0 / jnp.broadcast_to(diag, (levels, levels))
    inverse[...] = inv
    ratio[...] = -jnp.broadcast_to(below, (levels, levels)) * inv
    lane = lax.broadcasted_iota(jnp.int32, (1, levels), 1)
    row = jnp.zeros((1, levels), F32)
    for i in range(levels):
        row = jnp.where(lane == i, inverse[i : i + 1, :], row * ratio[i : i + 1, :])
        factor[i : i + 1, :] = row
    low_inv = factor[...]
    full = jnp.dot(low_inv.T, low_inv, preferred_element_type=F32, precision=lax.Precision.HIGHEST)
    high = full.astype(jnp.bfloat16)
    low = (full - high.astype(F32)).astype(jnp.bfloat16)
    weights_ref[0:levels, 0:levels] = high
    weights_ref[0:levels, levels:] = low
    weights_ref[levels:, 0:levels] = high
    weights_ref[levels:, levels:] = jnp.zeros_like(low)
    weights = weights_ref[...]
    cells = part_ref.shape[0]
    for c in range(0, cells, 16):
        y = times_inverse(part_ref[c : c + 16].reshape(256, LANES), weights)
        for k in range(16):
            y_ref[pl.ds(c + k, 8, stride=stride), :] = y[16 * k : 16 * k + 8]
            y_ref[pl.ds(8 * stride + c + k, rows - 8, stride=stride), :] = y[16 * k + 8 : 16 * k + rows]


def spread(out_ref, tiles, i, memb, stride, rows):
    for m in range(memb):
        out_ref[pl.ds(i * memb + m, 8, stride=stride), :] = tiles[0]
        out_ref[pl.ds(8 * stride + i * memb + m, rows - 8, stride=stride), :] = tiles[1][: rows - 8]


def expand_kernel(phi_ref, psi_ref, phi_out, psi_out, *, memb, stride, rows):
    for i in range(phi_ref.shape[0]):
        for src, dst in ((phi_ref, phi_out), (psi_ref, psi_out)):
            spread(dst, (src[i, 0:8, :], src[i, 8:16, :]), i, memb, stride, rows)


def lat_coef_kernel(diff_ref, step_out, phi_out, psi_out, coef_out, small_out, cos_out, *, memb, stride, bands):
    rows, cols = diff_ref.shape
    cells = cols * memb
    band = lax.axis_index("lat")
    row_ids = lax.broadcasted_iota(jnp.int32, (rows, cols), 0)
    last = jnp.logical_and(row_ids == rows - 1, band == bands - 1)
    step = split_rows(jnp.where(last, 0.0, 1.0 / diff_ref[...]))
    for i in range(cols):
        spread(step_out, [lane_of(s, i, 8) for s in step], i, memb, stride, rows)
    tile_ids = lax.broadcasted_iota(jnp.int32, (16, LANES), 0) + band * rows
    cosine = jnp.cos(-jnp.pi / 2 + (tile_ids.astype(F32) + 0.5) * jnp.pi / (bands * rows))
    cos_out[...] = cosine
    acc = [jnp.zeros((8, LANES), F32) for _ in range(3)]
    lane = lax.broadcasted_iota(jnp.int32, (PART, LANES), 1)
    for c in range(0, cells, PART):
        phi = jnp.ones((PART, LANES), F32)
        psi = jnp.zeros((PART, LANES), F32)
        phi_f, psi_f = psi, phi
        for j in range(rows):
            cos_j = jnp.broadcast_to(cosine[j : j + 1, :], (PART, LANES))
            t = step_out[j * stride + c : j * stride + c + PART, :]
            now_phi, now_psi = cos_j * phi, cos_j * psi
            phi_out[j * cells + c : j * cells + c + PART, :] = now_phi
            psi_out[j * cells + c : j * cells + c + PART, :] = now_psi
            phi_f = phi_f + now_phi
            psi_f = psi_f + now_psi
            phi = phi + t * phi_f
            psi = psi + t * psi_f
        b = 1.0 / psi
        picked = lax.broadcasted_iota(jnp.int32, (PART, LANES), 0) + c == lane * memb
        for k, value in enumerate((phi * b, b, psi_f * b)):
            coef_out[k * cells + c : k * cells + c + PART, :] = value
            chosen = jnp.where(picked, value, 0.0)
            for r in range(0, PART, 8):
                acc[k] = acc[k] + chosen[r : r + 8]
    small_out[...] = pack_small([jnp.sum(a, axis=0, keepdims=True) for a in acc])


def pack_small(lines):
    tile = lax.broadcasted_iota(jnp.int32, (8, LANES), 0)
    out = jnp.zeros((8, LANES), F32)
    for k, line in enumerate(lines):
        out = jnp.where(tile == k, jnp.broadcast_to(line, (8, LANES)), out)
    return out


def lat_sweep_kernel(*refs, levels, memb, rest, stride):
    own_ref, mine_ref, other_ref = refs[:3]
    backs = refs[3 : 3 + levels - 1]
    (y_ref, phi_ref, psi_ref, weights_ref, step_ref, coef_ref, small_ref, cos_ref, q_ref, pay_ref, ends, tiles) = refs[
        3 + levels - 1 :
    ]
    rows = 8 + rest
    half = memb * rows
    grow = functools.partial(lon_expand, memb=memb, rest=rest)
    right = on_right("lon", levels - 1)
    mine, other = mine_ref[...], other_ref[...]
    h1, h2, a, b, d, s, ca, cb = lon_join(
        jnp.where(right, other, mine), jnp.where(right, mine, other), memb, rest
    )
    outer = -(h1 + h2) * grow(1.0 / (a + d - 2.0 * b))
    middle = grow(ca + cb) * outer - s
    u_in, u_out = jnp.where(right, middle, outer), jnp.where(right, outer, middle)
    for level in reversed(range(levels - 1)):
        back = backs[level]
        middle = grow(back[half : half + 16, :]) * u_in + grow(back[half + 16 :, :]) * u_out - back[:half, :]
        right = on_right("lon", level)
        u_in, u_out = jnp.where(right, middle, u_in), jnp.where(right, u_out, middle)
    oh1, _, oa, ob, _ = lon_parts(own_ref[...], half)
    f_in = grow(ob) * u_out - grow(oa) * u_in - oh1
    weights = weights_ref[...]
    ends[...] = times_inverse(jnp.concatenate([u_in, f_in], axis=0), weights)
    for k in range(2):
        for j in range(rows):
            if j < 8:
                value = ends[pl.ds(k * half + j, memb, stride=8), :]
            else:
                value = ends[pl.ds(k * half + 8 * memb + j - 8, memb, stride=rest), :]
            tiles[8 * (k * rows + j) : 8 * (k * rows + j) + 8, :] = jnp.concatenate([value] * (8 // memb), axis=0)
    cells = coef_ref.shape[0] // 3
    for c in range(0, cells, PART):
        v = jnp.zeros((PART, LANES), F32)
        flux = v
        for j in range(rows):
            at = slice(j * stride + c, j * stride + c + PART)
            u_tile = jnp.concatenate([tiles[8 * j : 8 * j + 8, :]] * (PART // 8), axis=0)
            f_tile = jnp.concatenate([tiles[8 * (rows + j) : 8 * (rows + j) + 8, :]] * (PART // 8), axis=0)
            u = y_ref[at, :] + phi_ref[at, :] * u_tile + psi_ref[at, :] * f_tile
            now = jnp.broadcast_to(cos_ref[j : j + 1, :], (PART, LANES)) * v
            q_ref[j * cells + c : j * cells + c + PART, :] = now
            flux = flux + (now - u)
            v = v + step_ref[at, :] * flux
        b = coef_ref[cells + c : cells + c + PART, :]
        d = coef_ref[2 * cells + c : 2 * cells + c + PART, :]
        pay_ref[c : c + PART, :] = v * b
        pay_ref[cells + c : cells + c + PART, :] = flux - d * v
    pay_ref[2 * cells :, :] = small_ref[...]


def unpack_small(tile, k, c, memb):
    row = lax.broadcasted_iota(jnp.int32, (PART, LANES), 0) + c
    lane = lax.broadcasted_iota(jnp.int32, (PART, LANES), 1) * memb
    mask = jnp.logical_and(row >= lane, row < lane + memb)
    line = jnp.broadcast_to(tile[k : k + 1, :], (PART, LANES))
    return jnp.broadcast_to(jnp.sum(jnp.where(mask, line, 0.0), axis=1, keepdims=True), (PART, LANES))


def lat_merge_kernel(mine_ref, coef_ref, other_ref, *outs, level, levels, memb):
    ready = level == levels - 2
    if ready:
        pay_ref, back_ref, end_ref = outs
    else:
        pay_ref, back_ref, next_ref = outs
    cells = coef_ref.shape[0] // 3
    right = on_right("lat", level)
    upper = on_right("lat", level + 1)
    small = other_ref[2 * cells :, :]
    acc = [jnp.zeros((8, LANES), F32) for _ in range(3)]
    for c in range(0, cells, PART):
        at = slice(c, c + PART)
        lo, mid, hi = (slice(k * cells + c, k * cells + c + PART) for k in range(3))
        mine = [mine_ref[lo, :], mine_ref[mid, :], coef_ref[lo, :], coef_ref[mid, :], coef_ref[hi, :]]
        other = [other_ref[lo, :], other_ref[mid, :]] + [unpack_small(small, k, c, memb) for k in range(3)]
        lh1, lh2, la, lb, ld = (jnp.where(right, o, m) for m, o in zip(mine, other))
        rh1, rh2, ra, rb, rd = (jnp.where(right, m, o) for m, o in zip(mine, other))
        inv = 1.0 / (ld + ra)
        ca, cb = lb * inv, rb * inv
        total = lh2 + rh1
        back_ref[lo, :] = total * inv
        back_ref[mid, :] = ca
        back_ref[hi, :] = cb
        h1, h2 = lh1 + ca * total, rh2 + cb * total
        a, b, d = la - lb * ca, lb * cb, rd - rb * cb
        picked = lax.broadcasted_iota(jnp.int32, (PART, LANES), 0) + c == lax.broadcasted_iota(
            jnp.int32, (PART, LANES), 1
        ) * memb
        if ready:
            free, tied = jnp.where(upper, d, a), jnp.where(upper, a, d)
            h_free, h_tied = jnp.where(upper, h2, h1), jnp.where(upper, h1, h2)
            free_inv = 1.0 / free
            lean = b * free_inv
            pay_ref[at, :] = h_tied + lean * h_free
            stiff = tied - b * lean
            end_ref[lo, :] = lean
            end_ref[mid, :] = h_free * free_inv
            end_ref[hi, :] = stiff
            values = (stiff,)
        else:
            pay_ref[lo, :] = h1
            pay_ref[mid, :] = h2
            values = (a, b, d)
            for k, value in enumerate(values):
                next_ref[k * cells + c : k * cells + c + PART, :] = value
        for k, value in enumerate(values):
            chosen = jnp.where(picked, value, 0.0)
            for r in range(0, PART, 8):
                acc[k] = acc[k] + chosen[r : r + 8]
    lines = [jnp.sum(x, axis=0, keepdims=True) for x in acc[: 1 if ready else 3]]
    pay_ref[cells * (1 if ready else 2) :, :] = pack_small(lines)


def finish_kernel(*refs, levels, memb):
    own_ref, coef_ref, mine_ref, other_ref, end_ref = refs[:5]
    backs = refs[5 : 5 + levels - 1]
    q_ref, phi_ref, psi_ref, out_hbm, values, fluxes, out, sem = refs[5 + levels - 1 :]
    cells = coef_ref.shape[0] // 3
    rows = q_ref.shape[0] // cells
    upper = on_right("lat", levels - 1)
    small = other_ref[cells:, :]
    for c in range(0, cells, PART):
        lo, mid, hi = (slice(k * cells + c, k * cells + c + PART) for k in range(3))
        stiff = end_ref[hi, :] + unpack_small(small, 0, c, memb)
        middle = -(mine_ref[lo, :] + other_ref[lo, :]) / stiff
        outer = end_ref[lo, :] * middle - end_ref[mid, :]
        u_in, u_out = jnp.where(upper, middle, outer), jnp.where(upper, outer, middle)
        for level in reversed(range(levels - 1)):
            back = backs[level]
            middle = back[mid, :] * u_in + back[hi, :] * u_out - back[lo, :]
            right = on_right("lat", level)
            u_in, u_out = jnp.where(right, middle, u_in), jnp.where(right, u_out, middle)
        values[lo, :] = u_in
        fluxes[lo, :] = coef_ref[mid, :] * u_out - coef_ref[lo, :] * u_in - own_ref[lo, :]
    copies = []
    for j in range(rows):
        for c in range(0, cells, PART):
            at = slice(j * cells + c, j * cells + c + PART)
            lo = slice(c, c + PART)
            out[at, :] = q_ref[at, :] + phi_ref[at, :] * values[lo, :] + psi_ref[at, :] * fluxes[lo, :]
        copy = pltpu.make_async_copy(out.at[pl.ds(j * cells, cells), :], out_hbm.at[j], sem.at[j])
        copy.start()
        copies.append(copy)
    for copy in copies:
        copy.wait()


def swapped(value, axis, mask):
    return lax.ppermute(value, axis, [(s, s ^ mask) for s in range(lax.axis_size(axis))])


def shards(ensemble, grad_increment, normalization, lon_diffusion, lat_diffusion, vert_diag, vert_sub):
    rows, cols, memb, lev = ensemble.shape
    bands, blocks = lax.axis_size("lat"), lax.axis_size("lon")
    lat_levels, lon_levels = int(math.log2(bands)), int(math.log2(blocks))
    assert lev == LANES and 8 < rows <= 16 and 8 % memb == 0 and cols <= LANES and cols % CHUNK == 0
    assert 2**lat_levels == bands and 2**lon_levels == blocks and lat_levels >= 2 and lon_levels >= 2
    rest, cells = rows - 8, cols * memb
    assert 8 % rest == 0 and memb * rest % 8 == 0 and cells % PART == 0
    stride = cells + 1
    spaced = -(-rows * stride // 8) * 8
    half = memb * rows
    any_spec = pl.BlockSpec(memory_space=pl.ANY)
    vmem_spec = pl.BlockSpec(memory_space=pltpu.VMEM)

    part, phi_t, psi_t, pay = call(
        lon_sweep_kernel,
        (shape(cells, 16, LANES), shape(cols, 16, LANES), shape(cols, 16, LANES), shape(2 * half + 16, LANES)),
        scratch=[
            pltpu.VMEM((cells, 16, LANES), F32),
            pltpu.VMEM((cols, 16, LANES), F32),
            pltpu.SemaphoreType.DMA((cols // CHUNK, 2, rows)),
        ],
        in_specs=[any_spec, any_spec, vmem_spec, vmem_spec],
        cost=cost(2),
    )(ensemble.reshape(rows, cells, lev), grad_increment, normalization, lon_diffusion)

    y, weights = call(
        functools.partial(vertical_kernel, stride=stride, rows=rows),
        (shape(spaced, LANES), shape(2 * LANES, 2 * LANES, dtype=jnp.bfloat16)),
        scratch=[pltpu.VMEM((8, LANES), F32)] + [pltpu.VMEM((LANES, LANES), F32)] * 3,
        cost=cost(2),
    )(vert_diag.reshape(1, lev), vert_sub.reshape(1, lev - 1), part)
    phi, psi = call(
        functools.partial(expand_kernel, memb=memb, stride=stride, rows=rows),
        (shape(spaced, LANES), shape(spaced, LANES)),
        cost=cost(1),
    )(phi_t, psi_t)
    step, lat_phi, lat_psi, coef, small, cosine = call(
        functools.partial(lat_coef_kernel, memb=memb, stride=stride, bands=bands),
        (
            shape(spaced, LANES),
            shape(rows * cells, LANES),
            shape(rows * cells, LANES),
            shape(3 * cells, LANES),
            shape(8, LANES),
            shape(16, LANES),
        ),
        cost=cost(1),
    )(lat_diffusion)

    own, backs = pay, []
    for level in range(lon_levels - 1):
        other = swapped(pay, "lon", 1 << level)
        pay, back = call(
            functools.partial(lon_merge_kernel, level=level, memb=memb, rest=rest),
            (shape(2 * half + 16, LANES), shape(half + 32, LANES)),
            cost=cost(1),
        )(pay, other)
        backs.append(back)
    other = swapped(pay, "lon", 3 << (lon_levels - 2))
    q, lat_pay = call(
        functools.partial(lat_sweep_kernel, levels=lon_levels, memb=memb, rest=rest, stride=stride),
        (shape(rows * cells, LANES), shape(2 * cells + 8, LANES)),
        scratch=[pltpu.VMEM((2 * half, LANES), F32), pltpu.VMEM((16 * rows, LANES), F32)],
        cost=cost(1),
    )(own, pay, other, *backs, y, phi, psi, weights, step, coef, small, cosine)

    pay, group, lat_backs = lat_pay, coef, []
    for level in range(lat_levels - 1):
        other = swapped(pay, "lat", 1 << level)
        ready = level == lat_levels - 2
        pay, back, group = call(
            functools.partial(lat_merge_kernel, level=level, levels=lat_levels, memb=memb),
            (shape((1 if ready else 2) * cells + 8, LANES), shape(3 * cells, LANES), shape(3 * cells, LANES)),
            cost=cost(1),
        )(pay, group, other)
        lat_backs.append(back)
    other = swapped(pay, "lat", 1 << (lat_levels - 1))
    out = call(
        functools.partial(finish_kernel, levels=lat_levels, memb=memb),
        shape(rows, cells, LANES),
        scratch=[
            pltpu.VMEM((cells, LANES), F32),
            pltpu.VMEM((cells, LANES), F32),
            pltpu.VMEM((rows * cells, LANES), F32),
            pltpu.SemaphoreType.DMA((rows,)),
        ],
        out_specs=any_spec,
        cost=cost(1),
    )(lat_pay, coef, pay, other, group, *lat_backs, q, lat_phi, lat_psi)
    return out.reshape(rows, cols, memb, lev)


def cost(microseconds):
    return pl.CostEstimate(flops=0, bytes_accessed=int(microseconds * 3e6), transcendentals=0)


def solution(mesh):
    in_specs = (
        P("lat", "lon", None, None),
        P("lat", "lon", None),
        P("lat", "lon"),
        P("lat", "lon"),
        P("lat", "lon"),
        P(),
        P(),
    )
    out_specs = P("lat", "lon", None, None)
    return jax.shard_map(shards, mesh=mesh, in_specs=in_specs, out_specs=out_specs, check_vma=False)
```

time: 351 us -> 31.4 us (0.09)
  other arithmetic: 215 us -> 0 us
  blocking collectives: 110 us -> 0 us
  matrix products: 12 us -> 0 us
  waiting for transfers between devices: 0.7 us -> 9.24 us
  Pallas kernels: 0 us -> 7.02 us
  starting transfers between devices: 4.29 us -> 11.1 us
  local copies, waits for them, and re-layouts: 7.52 us -> 3.63 us
    another operation x30 -> x0, other arithmetic: 200 us -> none  [the longest x8 106 us: block_inverse(): factor = jnp.linalg.cholesky(matrix)]
    all_gather x8 -> x0, blocking collectives: 110 us -> none  [the longest x1 30.7 us: longitude_split(): lax.all_gather((own_rhs + prior_rhs)[None], 'lon', axis=0, tiled=True)]
    ppermute x2 -> x5, waiting for transfers between devices: 0.7 us -> 9.24 us  [swapped(): lax.ppermute(value, axis, [(s, s ^ mask) for s in range(lax.axis_size(axi...]
    pallas_call x0 -> x9, Pallas kernels: none -> 7.02 us  [the longest x1 2.41 us: shards(): call(lon_sweep_kernel, (shape(cells, 16, LANES), shape(cols, 16, LANES),...]
    dot_general x5 -> x0, matrix products: 6.84 us -> none  [the longest x1 2.35 us: latitude_split(): interior = jnp.einsum('bij,jbx->ibx', inverse, along_lon, precision=HIGHEST)]
    ppermute x2 -> x5, starting transfers between devices: 4.29 us -> 11.1 us  [swapped(): lax.ppermute(value, axis, [(s, s ^ mask) for s in range(lax.axis_size(axi...]
    another operation x10 -> x0, matrix products: 5.21 us -> none  [the longest x4 2.55 us: block_inverse(): inverse = jax.scipy.linalg.cho_solve((factor, True), identity)]
    unnamed x42 -> x14, local copies, waits for them, and re-layouts: 0.11 us -> 3.63 us
  transfers between devices with their start and end apart: 2 -> 5, of which waited for: 1 -> 5; matrix products, arithmetic and copies ran while one was open for 34% -> 0% of each run, Pallas kernels for 0% -> 6%
where the time goes in v1:
time: 31.4 us; the launch traced here: 31.1 us
  starting transfers between devices  11.1 us (35%)
  waiting for transfers between devices  9.24 us (29%)
  Pallas kernels  7.02 us (22%)
  local copies, waits for them, and re-layouts  3.63 us (12%)
    ppermute x5, starting transfers between devices, swapped(): lax.ppermute(value, axis, [(s, s ^ mask) for s in range(lax.axis_size(axi...  11.1 us
    ppermute x5, waiting for transfers between devices, swapped(): lax.ppermute(value, axis, [(s, s ^ mask) for s in range(lax.axis_size(axi...  9.24 us
    unnamed x14, local copies, waits for them, and re-layouts  3.63 us
    pallas_call x1, Pallas kernels, shards(): call(lon_sweep_kernel, (shape(cells, 16, LANES), shape(cols, 16, LANES),...  2.41 us
    pallas_call x1, Pallas kernels, shards(): call(functools.partial(finish_kernel, levels=lat_levels, memb=memb), shap...  1.59 us
    pallas_call x1, Pallas kernels, shards(): call(functools.partial(vertical_kernel, stride=stride, rows=rows), (shape...  1.23 us
    pallas_call x1, Pallas kernels, shards(): call(functools.partial(lat_sweep_kernel, levels=lon_levels, memb=memb, re...  0.69 us
  transfers between devices with their start and end apart: 5, of which 5 were waited for; matrix products, arithmetic and copies ran while one was open for 0% of the time, Pallas kernels for 6%

profile of v1, /device:TPU:0, one launch (start us, length us, event | category | flops | bytes accessed | tf_op | source)
XLA Modules:
  0.0 31.1 jit_solution(10805070960132704430)
XLA Ops:
  0.0 0.0 copy-start
  0.0 1.3 %copy-done = f32[12,48,4,128]{3,2,1,0:T(4,128)S(1)} copy-done((f32[12,48,4,128]{3,2,1,0:T(4,128)S(1)}, f32[12,48,4,128]{3,2,1,0:T(4,128)}, u32[]{:S(2)}) %copy-start) | copy-done | bytes 1179672
  1.3 0.0 copy-start.1
  1.3 1.0 %copy-done.1 = f32[12,48,128]{2,1,0:T(8,128)S(1)} copy-done((f32[12,48,128]{2,1,0:T(8,128)S(1)}, f32[12,48,128]{2,1,0:T(8,128)}, u32[]{:S(2)}) %copy-start.1) | copy-done | bytes 294936
  2.2 0.0 copy-start.2
  2.2 0.7 %copy-done.2 = f32[12,48]{1,0:T(8,128)S(1)} copy-done((f32[12,48]{1,0:T(8,128)S(1)}, f32[12,48]{1,0:T(8,128)}, u32[]{:S(2)}) %copy-start.2) | copy-done | bytes 2328
  2.9 0.0 copy-start.3
  2.9 0.7 %copy-done.3 = f32[12,48]{1,0:T(8,128)S(1)} copy-done((f32[12,48]{1,0:T(8,128)S(1)}, f32[12,48]{1,0:T(8,128)}, u32[]{:S(2)}) %copy-start.3) | copy-done | bytes 2328
  3.6 0.0 copy-start.4
  3.6 0.0 copy-start.5
  3.6 0.0 copy-start.6
  3.6 2.4 %shard_map.73 = (f32[192,16,128]{2,1,0:T(8,128)S(1)}, f32[48,16,128]{2,1,0:T(8,128)S(1)}, f32[48,16,128]{2,1,0:T(8,128)S(1)}, f32[112,128]{1,0:T(8,128)S(1)}) custom-call(f32[12,192,128]{2,1,0:T(8,128)S(1)} %bitcast.4, f32[12,48,128]{2,1,0:T(8,128)S(1)} %copy-done.1, f32[12,48]{1,0:T(8,128)S(1)} %copy-done.2, f32[12,48]{1,0:T(8,128)S(1)} %copy-done.3), custom_call_target="tpu_custom_call" | custom-call | bytes 6000000 | tf_op jit(solution)/shard_map/pallas_call | solution.py:410
  6.1 3.1 %collective-permute-start = (f32[112,128]{1,0:T(8,128)S(1)}, f32[112,128]{1,0:T(8,128)S(1)}, u32[]{:S(2)}, u32[]{:S(2)}) collective-permute-start(f32[112,128]{1,0:T(8,128)S(1)} %get-tuple-element.28.mine_ref.refs_0_), channel_id=1, source_target_pairs={{0,1},{1,0},{2,3},{3,2},{4,5},{5,4},{6,7},{7,6},{8,9},{9,8},{10,11... | collective-permute-start | bytes 172040 | tf_op jit(solution)/shard_map/ppermute | solution.py:393
  9.1 2.2 %collective-permute-done.other_ref = f32[112,128]{1,0:T(8,128)S(1)} collective-permute-done((f32[112,128]{1,0:T(8,128)S(1)}, f32[112,128]{1,0:T(8,128)S(1)}, u32[]{:S(2)}, u32[]{:S(2)}) %collective-permute-start) | collective-permute-done | bytes 57376 | tf_op jit(solution)/shard_map/ppermute | solution.py:393
  11.3 0.1 shard_map.74
  11.4 2.1 %collective-permute-start.1 = (f32[112,128]{1,0:T(8,128)S(1)}, f32[112,128]{1,0:T(8,128)S(1)}, u32[]{:S(2)}, u32[]{:S(2)}) collective-permute-start(f32[112,128]{1,0:T(8,128)S(1)} %get-tuple-element.29.mine_ref), channel_id=1, source_target_pairs={{0,2},{1,3},{2,0},{3,1},{4,6},{5,7},{6,4},{7,5},{8,10},{9,11},{10,... | collective-permute-start | bytes 172040 | tf_op jit(solution)/shard_map/ppermute | solution.py:393
  13.5 2.2 %collective-permute-done.1.other_ref = f32[112,128]{1,0:T(8,128)S(1)} collective-permute-done((f32[112,128]{1,0:T(8,128)S(1)}, f32[112,128]{1,0:T(8,128)S(1)}, u32[]{:S(2)}, u32[]{:S(2)}) %collective-permute-start.1) | collective-permute-done | bytes 57376 | tf_op jit(solution)/shard_map/ppermute | solution.py:393
  15.7 0.1 shard_map.75
  15.8 4.1 %collective-permute-start.2 = (f32[112,128]{1,0:T(8,128)S(1)}, f32[112,128]{1,0:T(8,128)S(1)}, u32[]{:S(2)}, u32[]{:S(2)}) collective-permute-start(f32[112,128]{1,0:T(8,128)S(1)} %get-tuple-element.30.refs_1_), channel_id=1, source_target_pairs={{0,6},{1,7},{2,4},{3,5},{4,2},{5,3},{6,0},{7,1},{8,14},{9,15},{10,... | collective-permute-start | bytes 172040 | tf_op jit(solution)/shard_map/ppermute | solution.py:393
  19.9 0.0 copy-done.4
  19.9 0.5 %shard_map.78 = (f32[2320,128]{1,0:T(8,128)S(1)}, f32[2304,128]{1,0:T(8,128)S(1)}, f32[2304,128]{1,0:T(8,128)S(1)}, f32[576,128]{1,0:T(8,128)S(1)}, f32[8,128]{1,0:T(8,128)S(1)}, /*index=5*/f32[16,128]{1,0:T(8,128)S(1)}) custom-call(f32[12,48]{1,0:T(8,128)S(1)} %copy-done.4), custom_call_target="tpu_custom_call" | custom-call | bytes 3000000 | tf_op jit(solution)/shard_map/pallas_call | solution.py:433
  20.4 0.2 shard_map.77
  20.6 0.0 copy-done.5
  20.6 0.0 copy-done.6
  20.6 1.2 %shard_map.76 = (f32[2320,128]{1,0:T(8,128)S(1)}, bf16[256,256]{1,0:T(8,128)(2,1)S(1)}) custom-call(f32[1,128]{1,0:T(1,128)S(1)} %bitcast.5, f32[1,127]{1,0:T(1,128)S(1)} %bitcast.6, f32[192,16,128]{2,1,0:T(8,128)S(1)} %get-tuple-element.33.part_ref), custom_call_target="tpu_custom_call" | custom-call | bytes 6000000 | tf_op jit(solution)/shard_map/pallas_call | solution.py:422
  21.8 0.2 collective-permute-done.2.refs_2_
  22.1 0.7 %shard_map.79 = (f32[2304,128]{1,0:T(8,128)S(1)}, f32[392,128]{1,0:T(8,128)S(1)}) custom-call(f32[112,128]{1,0:T(8,128)S(1)} %get-tuple-element.28.mine_ref.refs_0_, f32[112,128]{1,0:T(8,128)S(1)} %get-tuple-element.30.refs_1_, f32[112,128]{1,0:T(8,128)S(1)} %collective-permute-done.2.refs_2_, f32[80,128]{1,0:T(8,128)S(1)} %get-tuple-element.31.refs_3_, ...), custom_call_target="tpu_custom_call" | custom-call | bytes 3000000 | tf_op jit(solution)/shard_map/pallas_call | solution.py:456
  22.8 0.1 collective-permute-start.3
  22.9 1.4 %collective-permute-done.3.other_ref = f32[392,128]{1,0:T(8,128)S(1)} collective-permute-done((f32[392,128]{1,0:T(8,128)S(1)}, f32[392,128]{1,0:T(8,128)S(1)}, u32[]{:S(2)}, u32[]{:S(2)}) %collective-permute-start.3) | collective-permute-done | bytes 200736 | tf_op jit(solution)/shard_map/ppermute | solution.py:393
  24.3 0.2 shard_map.80
  24.5 1.7 %collective-permute-start.4 = (f32[200,128]{1,0:T(8,128)S(1)}, f32[200,128]{1,0:T(8,128)S(1)}, u32[]{:S(2)}, u32[]{:S(2)}) collective-permute-start(f32[200,128]{1,0:T(8,128)S(1)} %get-tuple-element.45.refs_2_), channel_id=1, source_target_pairs={{0,16},{8,24},{16,0},{24,8},{1,17},{9,25},{17,1},{25,9},{2,18},{10... | collective-permute-start | bytes 307208 | tf_op jit(solution)/shard_map/ppermute | solution.py:393
  26.2 3.3 %collective-permute-done.4.refs_3_ = f32[200,128]{1,0:T(8,128)S(1)} collective-permute-done((f32[200,128]{1,0:T(8,128)S(1)}, f32[200,128]{1,0:T(8,128)S(1)}, u32[]{:S(2)}, u32[]{:S(2)}) %collective-permute-start.4) | collective-permute-done | bytes 102432 | tf_op jit(solution)/shard_map/ppermute | solution.py:393
  29.5 1.6 %shard_map.81 = f32[12,192,128]{2,1,0:T(8,128)} custom-call(f32[392,128]{1,0:T(8,128)S(1)} %get-tuple-element.44.mine_ref.refs_0_, f32[576,128]{1,0:T(8,128)S(1)} %get-tuple-element.41.refs_10_.coef_ref.refs_1_, f32[200,128]{1,0:T(8,128)S(1)} %get-tuple-element.45.refs_2_, f32[200,128]{1,0:T(8,128)S(1)} %collective-permute-done.4.refs_3_, ...), custom_call_target="tpu_custom_call" | custom-call | bytes 3000000 | tf_op jit(solution)/shard_map/pallas_call | solution.py:474
Async XLA Ops:
  0.0 1.3 %copy-start = (f32[12,48,4,128]{3,2,1,0:T(4,128)S(1)}, f32[12,48,4,128]{3,2,1,0:T(4,128)}, u32[]{:S(2)}) copy-start(f32[12,48,4,128]{3,2,1,0:T(4,128)} %param.7) | copy-start | bytes 3538948
  1.3 1.0 %copy-start.1 = (f32[12,48,128]{2,1,0:T(8,128)S(1)}, f32[12,48,128]{2,1,0:T(8,128)}, u32[]{:S(2)}) copy-start(f32[12,48,128]{2,1,0:T(8,128)} %grad_hbm.1) | copy-start | bytes 884740
  2.2 0.7 %copy-start.2 = (f32[12,48]{1,0:T(8,128)S(1)}, f32[12,48]{1,0:T(8,128)}, u32[]{:S(2)}) copy-start(f32[12,48]{1,0:T(8,128)} %norm_ref.1) | copy-start | bytes 6916
  2.9 0.7 %copy-start.3 = (f32[12,48]{1,0:T(8,128)S(1)}, f32[12,48]{1,0:T(8,128)}, u32[]{:S(2)}) copy-start(f32[12,48]{1,0:T(8,128)} %diff_ref.2) | copy-start | bytes 6916
  3.6 16.2 %copy-start.4 = (f32[12,48]{1,0:T(8,128)S(1)}, f32[12,48]{1,0:T(8,128)}, u32[]{:S(2)}) copy-start(f32[12,48]{1,0:T(8,128)} %diff_ref.3) | copy-start | bytes 6916
  3.6 17.0 %copy-start.5 = (f32[128]{0:T(128)S(1)}, f32[128]{0:T(128)}, u32[]{:S(2)}) copy-start(f32[128]{0:T(128)} %param.12) | copy-start | bytes 1540
  3.6 17.0 %copy-start.6 = (f32[127]{0:T(128)S(1)}, f32[127]{0:T(128)}, u32[]{:S(2)}) copy-start(f32[127]{0:T(128)} %param.13) | copy-start | bytes 1528
  6.1 5.2 %collective-permute-start = (f32[112,128]{1,0:T(8,128)S(1)}, f32[112,128]{1,0:T(8,128)S(1)}, u32[]{:S(2)}, u32[]{:S(2)}) collective-permute-start(f32[112,128]{1,0:T(8,128)S(1)} %get-tuple-element.28.mine_ref.refs_0_), channel_id=1, source_target_pairs={{0,1},{1,0},{2,3},{3,2},{4,5},{5,4},{6,7},{7,6},{8,9},{9,8},{10,11... | collective-permute-start | bytes 172040 | tf_op jit(solution)/shard_map/ppermute | solution.py:393
  11.4 4.3 %collective-permute-start.1 = (f32[112,128]{1,0:T(8,128)S(1)}, f32[112,128]{1,0:T(8,128)S(1)}, u32[]{:S(2)}, u32[]{:S(2)}) collective-permute-start(f32[112,128]{1,0:T(8,128)S(1)} %get-tuple-element.29.mine_ref), channel_id=1, source_target_pairs={{0,2},{1,3},{2,0},{3,1},{4,6},{5,7},{6,4},{7,5},{8,10},{9,11},{10,... | collective-permute-start | bytes 172040 | tf_op jit(solution)/shard_map/ppermute | solution.py:393
  15.8 6.3 %collective-permute-start.2 = (f32[112,128]{1,0:T(8,128)S(1)}, f32[112,128]{1,0:T(8,128)S(1)}, u32[]{:S(2)}, u32[]{:S(2)}) collective-permute-start(f32[112,128]{1,0:T(8,128)S(1)} %get-tuple-element.30.refs_1_), channel_id=1, source_target_pairs={{0,6},{1,7},{2,4},{3,5},{4,2},{5,3},{6,0},{7,1},{8,14},{9,15},{10,... | collective-permute-start | bytes 172040 | tf_op jit(solution)/shard_map/ppermute | solution.py:393
  22.8 1.5 %collective-permute-start.3 = (f32[392,128]{1,0:T(8,128)S(1)}, f32[392,128]{1,0:T(8,128)S(1)}, u32[]{:S(2)}, u32[]{:S(2)}) collective-permute-start(f32[392,128]{1,0:T(8,128)S(1)} %get-tuple-element.44.mine_ref.refs_0_), channel_id=1, source_target_pairs={{0,8},{8,0},{16,24},{24,16},{1,9},{9,1},{17,25},{25,17},{2,10},{10... | collective-permute-start | bytes 602120 | tf_op jit(solution)/shard_map/ppermute | solution.py:393
  24.5 5.0 %collective-permute-start.4 = (f32[200,128]{1,0:T(8,128)S(1)}, f32[200,128]{1,0:T(8,128)S(1)}, u32[]{:S(2)}, u32[]{:S(2)}) collective-permute-start(f32[200,128]{1,0:T(8,128)S(1)} %get-tuple-element.45.refs_2_), channel_id=1, source_target_pairs={{0,16},{8,24},{16,0},{24,8},{1,17},{9,25},{17,1},{25,9},{2,18},{10... | collective-permute-start | bytes 307208 | tf_op jit(solution)/shard_map/ppermute | solution.py:393

commit v2 on v1

--- a/solution.py
+++ b/solution.py
@@ -41,11 +41,19 @@
     return value[:8], jnp.concatenate([value[8:], fill], axis=0)
 
 
-def lon_sweep_kernel(ens_hbm, grad_hbm, norm_ref, diff_ref, part_ref, phi_ref, psi_ref, pay_ref, ens, grad, sem):
+def lon_sweep_kernel(
+    ens_hbm, grad_hbm, norm_hbm, diff_hbm, part_ref, phi_ref, psi_ref, pay_ref, ens, grad, norm_ref, diff_ref, sem, sem2
+):
     rows, cells, _ = ens_hbm.shape
     cols = grad_hbm.shape[1]
     memb = cells // cols
     rest = rows - 8
+    small = [
+        pltpu.make_async_copy(diff_hbm, diff_ref, sem2.at[0]),
+        pltpu.make_async_copy(norm_hbm, norm_ref, sem2.at[1]),
+    ]
+    for copy in small:
+        copy.start()
     copies = []
     for c in range(cols // CHUNK):
         group = []
@@ -57,6 +65,8 @@
     for group in copies:
         for copy in group:
             copy.start()
+    for copy in small:
+        copy.wait()
     step = split_rows(1.0 / diff_ref[...])
     norm = split_rows(norm_ref[...])
     zero, one = jnp.zeros((8, LANES), F32), jnp.ones((8, LANES), F32)
@@ -265,7 +275,7 @@
     oh1, _, oa, ob, _ = lon_parts(own_ref[...], half)
     f_in = grow(ob) * u_out - grow(oa) * u_in - oh1
     weights = weights_ref[...]
-    ends[...] = times_inverse(jnp.concatenate([u_in, f_in], axis=0), weights)
+    ends[: 2 * half, :] = times_inverse(jnp.concatenate([u_in, f_in], axis=0), weights)
     for k in range(2):
         for j in range(rows):
             if j < 8:
@@ -402,10 +412,9 @@
     rest, cells = rows - 8, cols * memb
     assert 8 % rest == 0 and memb * rest % 8 == 0 and cells % PART == 0
     stride = cells + 1
-    spaced = -(-rows * stride // 8) * 8
+    spaced = -(-(rows + 1) * stride // 8) * 8
     half = memb * rows
-    any_spec = pl.BlockSpec(memory_space=pl.ANY)
-    vmem_spec = pl.BlockSpec(memory_space=pltpu.VMEM)
+    hbm_spec = pl.BlockSpec(memory_space=pltpu.HBM)
 
     part, phi_t, psi_t, pay = call(
         lon_sweep_kernel,
@@ -413,11 +422,14 @@
         scratch=[
             pltpu.VMEM((cells, 16, LANES), F32),
             pltpu.VMEM((cols, 16, LANES), F32),
+            pltpu.VMEM((rows, cols), F32),
+            pltpu.VMEM((rows, cols), F32),
             pltpu.SemaphoreType.DMA((cols // CHUNK, 2, rows)),
+            pltpu.SemaphoreType.DMA((2,)),
         ],
-        in_specs=[any_spec, any_spec, vmem_spec, vmem_spec],
+        in_specs=[hbm_spec] * 4,
         cost=cost(2),
-    )(ensemble.reshape(rows, cells, lev), grad_increment, normalization, lon_diffusion)
+    )(*(in_hbm(x) for x in (ensemble.reshape(rows, cells, lev), grad_increment, normalization, lon_diffusion)))
 
     y, weights = call(
         functools.partial(vertical_kernel, stride=stride, rows=rows),
@@ -452,11 +464,11 @@
             cost=cost(1),
         )(pay, other)
         backs.append(back)
-    other = swapped(pay, "lon", 3 << (lon_levels - 2))
+    other = swapped(pay, "lon", 1 << (lon_levels - 1))
     q, lat_pay = call(
         functools.partial(lat_sweep_kernel, levels=lon_levels, memb=memb, rest=rest, stride=stride),
         (shape(rows * cells, LANES), shape(2 * cells + 8, LANES)),
-        scratch=[pltpu.VMEM((2 * half, LANES), F32), pltpu.VMEM((16 * rows, LANES), F32)],
+        scratch=[pltpu.VMEM((2 * half + 8, LANES), F32), pltpu.VMEM((16 * rows, LANES), F32)],
         cost=cost(1),
     )(own, pay, other, *backs, y, phi, psi, weights, step, coef, small, cosine)
 
@@ -480,10 +492,14 @@
             pltpu.VMEM((rows * cells, LANES), F32),
             pltpu.SemaphoreType.DMA((rows,)),
         ],
-        out_specs=any_spec,
+        out_specs=hbm_spec,
         cost=cost(1),
     )(lat_pay, coef, pay, other, group, *lat_backs, q, lat_phi, lat_psi)
     return out.reshape(rows, cols, memb, lev)
+
+
+def in_hbm(value):
+    return pltpu.with_memory_space_constraint(value, pltpu.HBM)
 
 
 def cost(microseconds):

time: 31.4 us -> 27 us (0.86)
  local copies, waits for them, and re-layouts: 3.63 us -> 0.01 us
  starting transfers between devices: 11.1 us -> 10.3 us
    unnamed x14 -> x6, local copies, waits for them, and re-layouts: 3.63 us -> 0.01 us
    ppermute x5, starting transfers between devices: 11.1 us -> 10.3 us  [swapped(): lax.ppermute(value, axis, [(s, s ^ mask) for s in range(lax.axis_size(axi...]
  transfers between devices with their start and end apart: 5 -> 5, of which waited for: 5 -> 5; matrix products, arithmetic and copies ran while one was open for 0% -> 0% of each run, Pallas kernels for 6% -> 7%
where the time goes in v2:
time: 27 us; the launch traced here: 26.8 us
  starting transfers between devices  10.3 us (38%)
  waiting for transfers between devices  9.12 us (34%)
  Pallas kernels  7.3 us (27%)
    ppermute x5, starting transfers between devices, swapped(): lax.ppermute(value, axis, [(s, s ^ mask) for s in range(lax.axis_size(axi...  10.3 us
    ppermute x5, waiting for transfers between devices, swapped(): lax.ppermute(value, axis, [(s, s ^ mask) for s in range(lax.axis_size(axi...  9.12 us
    pallas_call x1, Pallas kernels, shards(): call(lon_sweep_kernel, (shape(cells, 16, LANES), shape(cols, 16, LANES),...  2.7 us
    pallas_call x1, Pallas kernels, shards(): call(functools.partial(finish_kernel, levels=lat_levels, memb=memb), shap...  1.58 us
    pallas_call x1, Pallas kernels, shards(): call(functools.partial(vertical_kernel, stride=stride, rows=rows), (shape...  1.23 us
    pallas_call x1, Pallas kernels, shards(): call(functools.partial(lat_sweep_kernel, levels=lon_levels, memb=memb, re...  0.69 us
  transfers between devices with their start and end apart: 5, of which 5 were waited for; matrix products, arithmetic and copies ran while one was open for 0% of the time, Pallas kernels for 7%

profile of v2, /device:TPU:0, one launch (start us, length us, event | category | flops | bytes accessed | tf_op | source)
XLA Modules:
  0.0 26.8 jit_solution(7010619206438294473)
XLA Ops:
  0.0 0.0 copy-start
  0.0 0.0 copy-start.2
  0.0 0.0 copy-start.1
  0.0 2.7 %shard_map.73 = (f32[192,16,128]{2,1,0:T(8,128)S(1)}, f32[48,16,128]{2,1,0:T(8,128)S(1)}, f32[48,16,128]{2,1,0:T(8,128)S(1)}, f32[112,128]{1,0:T(8,128)S(1)}) custom-call(f32[12,192,128]{2,1,0:T(8,128)} %bitcast.6, f32[12,48,128]{2,1,0:T(8,128)} %grad_hbm.1, f32[12,48]{1,0:T(8,128)} %norm_hbm.1, f32[12,48]{1,0:T(8,128)} %diff_hbm.1), custom_call_target="tpu_custom_call" | custom-call | bytes 6000000 | tf_op jit(solution)/shard_map/pallas_call | solution.py:419
  2.7 3.1 %collective-permute-start = (f32[112,128]{1,0:T(8,128)S(1)}, f32[112,128]{1,0:T(8,128)S(1)}, u32[]{:S(2)}, u32[]{:S(2)}) collective-permute-start(f32[112,128]{1,0:T(8,128)S(1)} %get-tuple-element.28.mine_ref.refs_0_), channel_id=1, source_target_pairs={{0,1},{1,0},{2,3},{3,2},{4,5},{5,4},{6,7},{7,6},{8,9},{9,8},{10,11... | collective-permute-start | bytes 172040 | tf_op jit(solution)/shard_map/ppermute | solution.py:403
  5.8 2.2 %collective-permute-done.other_ref = f32[112,128]{1,0:T(8,128)S(1)} collective-permute-done((f32[112,128]{1,0:T(8,128)S(1)}, f32[112,128]{1,0:T(8,128)S(1)}, u32[]{:S(2)}, u32[]{:S(2)}) %collective-permute-start) | collective-permute-done | bytes 57376 | tf_op jit(solution)/shard_map/ppermute | solution.py:403
  7.9 0.1 shard_map.74
  8.0 2.1 %collective-permute-start.1 = (f32[112,128]{1,0:T(8,128)S(1)}, f32[112,128]{1,0:T(8,128)S(1)}, u32[]{:S(2)}, u32[]{:S(2)}) collective-permute-start(f32[112,128]{1,0:T(8,128)S(1)} %get-tuple-element.29.mine_ref), channel_id=1, source_target_pairs={{0,2},{1,3},{2,0},{3,1},{4,6},{5,7},{6,4},{7,5},{8,10},{9,11},{10,... | collective-permute-start | bytes 172040 | tf_op jit(solution)/shard_map/ppermute | solution.py:403
  10.2 2.2 %collective-permute-done.1.other_ref = f32[112,128]{1,0:T(8,128)S(1)} collective-permute-done((f32[112,128]{1,0:T(8,128)S(1)}, f32[112,128]{1,0:T(8,128)S(1)}, u32[]{:S(2)}, u32[]{:S(2)}) %collective-permute-start.1) | collective-permute-done | bytes 57376 | tf_op jit(solution)/shard_map/ppermute | solution.py:403
  12.3 0.1 shard_map.75
  12.4 3.1 %collective-permute-start.2 = (f32[112,128]{1,0:T(8,128)S(1)}, f32[112,128]{1,0:T(8,128)S(1)}, u32[]{:S(2)}, u32[]{:S(2)}) collective-permute-start(f32[112,128]{1,0:T(8,128)S(1)} %get-tuple-element.30.refs_1_), channel_id=1, source_target_pairs={{0,4},{1,5},{2,6},{3,7},{4,0},{5,1},{6,2},{7,3},{8,12},{9,13},{10,... | collective-permute-start | bytes 172040 | tf_op jit(solution)/shard_map/ppermute | solution.py:403
  15.5 0.0 copy-done
  15.5 0.5 %shard_map.78 = (f32[2512,128]{1,0:T(8,128)S(1)}, f32[2304,128]{1,0:T(8,128)S(1)}, f32[2304,128]{1,0:T(8,128)S(1)}, f32[576,128]{1,0:T(8,128)S(1)}, f32[8,128]{1,0:T(8,128)S(1)}, /*index=5*/f32[16,128]{1,0:T(8,128)S(1)}) custom-call(f32[12,48]{1,0:T(8,128)S(1)} %copy-done), custom_call_target="tpu_custom_call" | custom-call | bytes 3000000 | tf_op jit(solution)/shard_map/pallas_call | solution.py:445
  16.0 0.2 shard_map.77
  16.2 0.0 copy-done.2
  16.3 0.0 copy-done.1
  16.3 1.2 %shard_map.76 = (f32[2512,128]{1,0:T(8,128)S(1)}, bf16[256,256]{1,0:T(8,128)(2,1)S(1)}) custom-call(f32[1,128]{1,0:T(1,128)S(1)} %bitcast.4, f32[1,127]{1,0:T(1,128)S(1)} %bitcast.5, f32[192,16,128]{2,1,0:T(8,128)S(1)} %get-tuple-element.33.part_ref), custom_call_target="tpu_custom_call" | custom-call | bytes 6000000 | tf_op jit(solution)/shard_map/pallas_call | solution.py:434
  17.5 0.2 collective-permute-done.2.refs_2_
  17.7 0.7 %shard_map.79 = (f32[2304,128]{1,0:T(8,128)S(1)}, f32[392,128]{1,0:T(8,128)S(1)}) custom-call(f32[112,128]{1,0:T(8,128)S(1)} %get-tuple-element.28.mine_ref.refs_0_, f32[112,128]{1,0:T(8,128)S(1)} %get-tuple-element.30.refs_1_, f32[112,128]{1,0:T(8,128)S(1)} %collective-permute-done.2.refs_2_, f32[80,128]{1,0:T(8,128)S(1)} %get-tuple-element.31.refs_3_, ...), custom_call_target="tpu_custom_call" | custom-call | bytes 3000000 | tf_op jit(solution)/shard_map/pallas_call | solution.py:468
  18.4 0.1 collective-permute-start.3
  18.5 1.4 %collective-permute-done.3.other_ref = f32[392,128]{1,0:T(8,128)S(1)} collective-permute-done((f32[392,128]{1,0:T(8,128)S(1)}, f32[392,128]{1,0:T(8,128)S(1)}, u32[]{:S(2)}, u32[]{:S(2)}) %collective-permute-start.3) | collective-permute-done | bytes 200736 | tf_op jit(solution)/shard_map/ppermute | solution.py:403
  19.9 0.2 shard_map.80
  20.1 1.9 %collective-permute-start.4 = (f32[200,128]{1,0:T(8,128)S(1)}, f32[200,128]{1,0:T(8,128)S(1)}, u32[]{:S(2)}, u32[]{:S(2)}) collective-permute-start(f32[200,128]{1,0:T(8,128)S(1)} %get-tuple-element.45.refs_2_), channel_id=1, source_target_pairs={{0,16},{8,24},{16,0},{24,8},{1,17},{9,25},{17,1},{25,9},{2,18},{10... | collective-permute-start | bytes 307208 | tf_op jit(solution)/shard_map/ppermute | solution.py:403
  22.0 3.2 %collective-permute-done.4.refs_3_ = f32[200,128]{1,0:T(8,128)S(1)} collective-permute-done((f32[200,128]{1,0:T(8,128)S(1)}, f32[200,128]{1,0:T(8,128)S(1)}, u32[]{:S(2)}, u32[]{:S(2)}) %collective-permute-start.4) | collective-permute-done | bytes 102432 | tf_op jit(solution)/shard_map/ppermute | solution.py:403
  25.2 1.6 %shard_map.81 = f32[12,192,128]{2,1,0:T(8,128)} custom-call(f32[392,128]{1,0:T(8,128)S(1)} %get-tuple-element.44.mine_ref.refs_0_, f32[576,128]{1,0:T(8,128)S(1)} %get-tuple-element.41.refs_10_.coef_ref.refs_1_, f32[200,128]{1,0:T(8,128)S(1)} %get-tuple-element.45.refs_2_, f32[200,128]{1,0:T(8,128)S(1)} %collective-permute-done.4.refs_3_, ...), custom_call_target="tpu_custom_call" | custom-call | bytes 3000000 | tf_op jit(solution)/shard_map/pallas_call | solution.py:486
Async XLA Ops:
  0.0 15.5 %copy-start = (f32[12,48]{1,0:T(8,128)S(1)}, f32[12,48]{1,0:T(8,128)}, u32[]{:S(2)}) copy-start(f32[12,48]{1,0:T(8,128)} %diff_ref.1) | copy-start | bytes 6916
  0.0 16.2 %copy-start.2 = (f32[127]{0:T(128)S(1)}, f32[127]{0:T(128)}, u32[]{:S(2)}) copy-start(f32[127]{0:T(128)} %param.13) | copy-start | bytes 1528
  0.0 16.2 %copy-start.1 = (f32[128]{0:T(128)S(1)}, f32[128]{0:T(128)}, u32[]{:S(2)}) copy-start(f32[128]{0:T(128)} %param.12) | copy-start | bytes 1540
  2.7 5.2 %collective-permute-start = (f32[112,128]{1,0:T(8,128)S(1)}, f32[112,128]{1,0:T(8,128)S(1)}, u32[]{:S(2)}, u32[]{:S(2)}) collective-permute-start(f32[112,128]{1,0:T(8,128)S(1)} %get-tuple-element.28.mine_ref.refs_0_), channel_id=1, source_target_pairs={{0,1},{1,0},{2,3},{3,2},{4,5},{5,4},{6,7},{7,6},{8,9},{9,8},{10,11... | collective-permute-start | bytes 172040 | tf_op jit(solution)/shard_map/ppermute | solution.py:403
  8.0 4.3 %collective-permute-start.1 = (f32[112,128]{1,0:T(8,128)S(1)}, f32[112,128]{1,0:T(8,128)S(1)}, u32[]{:S(2)}, u32[]{:S(2)}) collective-permute-start(f32[112,128]{1,0:T(8,128)S(1)} %get-tuple-element.29.mine_ref), channel_id=1, source_target_pairs={{0,2},{1,3},{2,0},{3,1},{4,6},{5,7},{6,4},{7,5},{8,10},{9,11},{10,... | collective-permute-start | bytes 172040 | tf_op jit(solution)/shard_map/ppermute | solution.py:403
  12.4 5.3 %collective-permute-start.2 = (f32[112,128]{1,0:T(8,128)S(1)}, f32[112,128]{1,0:T(8,128)S(1)}, u32[]{:S(2)}, u32[]{:S(2)}) collective-permute-start(f32[112,128]{1,0:T(8,128)S(1)} %get-tuple-element.30.refs_1_), channel_id=1, source_target_pairs={{0,4},{1,5},{2,6},{3,7},{4,0},{5,1},{6,2},{7,3},{8,12},{9,13},{10,... | collective-permute-start | bytes 172040 | tf_op jit(solution)/shard_map/ppermute | solution.py:403
  18.4 1.5 %collective-permute-start.3 = (f32[392,128]{1,0:T(8,128)S(1)}, f32[392,128]{1,0:T(8,128)S(1)}, u32[]{:S(2)}, u32[]{:S(2)}) collective-permute-start(f32[392,128]{1,0:T(8,128)S(1)} %get-tuple-element.44.mine_ref.refs_0_), channel_id=1, source_target_pairs={{0,8},{8,0},{16,24},{24,16},{1,9},{9,1},{17,25},{25,17},{2,10},{10... | collective-permute-start | bytes 602120 | tf_op jit(solution)/shard_map/ppermute | solution.py:403
  20.1 5.1 %collective-permute-start.4 = (f32[200,128]{1,0:T(8,128)S(1)}, f32[200,128]{1,0:T(8,128)S(1)}, u32[]{:S(2)}, u32[]{:S(2)}) collective-permute-start(f32[200,128]{1,0:T(8,128)S(1)} %get-tuple-element.45.refs_2_), channel_id=1, source_target_pairs={{0,16},{8,24},{16,0},{24,8},{1,17},{9,25},{17,1},{25,9},{2,18},{10... | collective-permute-start | bytes 307208 | tf_op jit(solution)/shard_map/ppermute | solution.py:403

commit v3 on v2

--- a/solution.py
+++ b/solution.py
@@ -42,70 +42,97 @@
 
 
 def lon_sweep_kernel(
-    ens_hbm, grad_hbm, norm_hbm, diff_hbm, part_ref, phi_ref, psi_ref, pay_ref, ens, grad, norm_ref, diff_ref, sem, sem2
+    ens_hbm,
+    grad_hbm,
+    norm_hbm,
+    diff_hbm,
+    part_ref,
+    phi_ref,
+    psi_ref,
+    pay_ref,
+    ens,
+    grad,
+    norm_ref,
+    diff_ref,
+    step_b,
+    norm_b,
+    sem,
 ):
     rows, cells, _ = ens_hbm.shape
     cols = grad_hbm.shape[1]
     memb = cells // cols
     rest = rows - 8
-    small = [
-        pltpu.make_async_copy(diff_hbm, diff_ref, sem2.at[0]),
-        pltpu.make_async_copy(norm_hbm, norm_ref, sem2.at[1]),
-    ]
-    for copy in small:
-        copy.start()
-    copies = []
-    for c in range(cols // CHUNK):
-        group = []
+    half = memb * rows
+    chunks = cols // CHUNK
+    first = pltpu.make_async_copy(diff_hbm, diff_ref, sem.at[2 * chunks])
+    second = pltpu.make_async_copy(norm_hbm, norm_ref, sem.at[2 * chunks + 1])
+    first.start()
+    second.start()
+    arrivals = []
+    for c in range(chunks):
+        g_rows, e_rows = pl.ds(c * CHUNK, CHUNK), pl.ds(c * CHUNK * memb, CHUNK * memb)
         for j in range(rows):
-            g_rows, e_rows = pl.ds(c * CHUNK, CHUNK), pl.ds(c * CHUNK * memb, CHUNK * memb)
-            group.append(pltpu.make_async_copy(grad_hbm.at[j, g_rows], grad.at[g_rows, j, :], sem.at[c, 0, j]))
-            group.append(pltpu.make_async_copy(ens_hbm.at[j, e_rows], ens.at[e_rows, j, :], sem.at[c, 1, j]))
-        copies.append(group)
-    for group in copies:
-        for copy in group:
-            copy.start()
-    for copy in small:
-        copy.wait()
+            pltpu.make_async_copy(grad_hbm.at[j, g_rows], grad.at[g_rows, j, :], sem.at[2 * c]).start()
+            pltpu.make_async_copy(ens_hbm.at[j, e_rows], ens.at[e_rows, j, :], sem.at[2 * c + 1]).start()
+        arrivals.append(
+            (
+                pltpu.make_async_copy(grad_hbm.at[:, g_rows], grad_hbm.at[:, g_rows], sem.at[2 * c]),
+                pltpu.make_async_copy(ens_hbm.at[:, e_rows], ens_hbm.at[:, e_rows], sem.at[2 * c + 1]),
+            )
+        )
+    zero, one = jnp.zeros((8, LANES), F32), jnp.ones((8, LANES), F32)
+    tiles = [slice(0, 8), slice(8, 16)]
+
+    first.wait()
+    second.wait()
     step = split_rows(1.0 / diff_ref[...])
     norm = split_rows(norm_ref[...])
-    zero, one = jnp.zeros((8, LANES), F32), jnp.ones((8, LANES), F32)
-    u = [[zero] * memb for _ in range(2)]
-    flux = [[zero] * memb for _ in range(2)]
     phi, phi_f, psi, psi_f = [one] * 2, [zero] * 2, [zero] * 2, [one] * 2
     for i in range(cols):
-        if i % CHUNK == 0:
-            for copy in copies[i // CHUNK]:
-                copy.wait()
         for g in range(2):
-            tile = slice(8 * g, 8 * g + 8)
             t = lane_of(step[g], i, 8)
-            w = lane_of(norm[g], i, 8) * grad[i, tile, :]
-            for m in range(memb):
-                part_ref[i * memb + m, tile, :] = u[g][m]
-                f = w * ens[i * memb + m, tile, :]
-                flux[g][m] = flux[g][m] + (u[g][m] - f)
-                u[g][m] = u[g][m] + t * flux[g][m]
-            phi_ref[i, tile, :] = phi[g]
-            psi_ref[i, tile, :] = psi[g]
+            step_b[i, tiles[g], :] = t
+            norm_b[i, tiles[g], :] = lane_of(norm[g], i, 8)
+            phi_ref[i, tiles[g], :] = phi[g]
+            psi_ref[i, tiles[g], :] = psi[g]
             phi_f[g] = phi_f[g] + phi[g]
             psi_f[g] = psi_f[g] + psi[g]
             phi[g] = phi[g] + t * phi_f[g]
             psi[g] = psi[g] + t * psi_f[g]
     lanes = lax.broadcasted_iota(jnp.int32, (8, LANES), 1)
-    half = memb * rows
+    ends = []
     for g in range(2):
         b = 1.0 / psi[g]
         a, d = phi[g] * b, psi_f[g] * b
-        first = 0 if g == 0 else 8 * memb
+        ends.append((b, d))
         size = 8 if g == 0 else rest
-        for m in range(memb):
-            pay_ref[first + m * size : first + (m + 1) * size, :] = (u[g][m] * b)[:size]
-            pay_ref[half + first + m * size : half + first + (m + 1) * size, :] = (flux[g][m] - d * u[g][m])[:size]
         coef = jnp.where(lanes == 0, a, jnp.where(lanes == 1, b, d))
         for k in range(8 // size):
             row = 2 * half + 8 * g + k * size
             pay_ref[row : row + size, :] = coef[:size]
+
+    u = [[zero] * memb for _ in range(2)]
+    flux = [[zero] * memb for _ in range(2)]
+    for i in range(cols):
+        if i % CHUNK == 0:
+            for copy in arrivals[i // CHUNK]:
+                copy.wait()
+        for g in range(2):
+            t = step_b[i, tiles[g], :]
+            w = norm_b[i, tiles[g], :] * grad[i, tiles[g], :]
+            for m in range(memb):
+                part_ref[i * memb + m, tiles[g], :] = u[g][m]
+                f = w * ens[i * memb + m, tiles[g], :]
+                flux[g][m] = flux[g][m] + (u[g][m] - f)
+                u[g][m] = u[g][m] + t * flux[g][m]
+    for g in range(2):
+        b, d = ends[g]
+        start = 0 if g == 0 else 8 * memb
+        size = 8 if g == 0 else rest
+        for m in range(memb):
+            at = start + m * size
+            pay_ref[at : at + size, :] = (u[g][m] * b)[:size]
+            pay_ref[half + at : half + at + size, :] = (flux[g][m] - d * u[g][m])[:size]
 
 
 def lon_expand(tiles, memb, rest):
@@ -368,13 +395,20 @@
 def finish_kernel(*refs, levels, memb):
     own_ref, coef_ref, mine_ref, other_ref, end_ref = refs[:5]
     backs = refs[5 : 5 + levels - 1]
-    q_ref, phi_ref, psi_ref, out_hbm, values, fluxes, out, sem = refs[5 + levels - 1 :]
+    q_ref, phi_ref, psi_ref, out_hbm, out, sem = refs[5 + levels - 1 :]
     cells = coef_ref.shape[0] // 3
     rows = q_ref.shape[0] // cells
     upper = on_right("lat", levels - 1)
     small = other_ref[cells:, :]
-    for c in range(0, cells, PART):
-        lo, mid, hi = (slice(k * cells + c, k * cells + c + PART) for k in range(3))
+
+    def chunk_copy(k):
+        at = pl.ds(pl.multiple_of(k * PART, PART), PART)
+        return pltpu.make_async_copy(out.at[:, at, :], out_hbm.at[:, at, :], sem.at[k])
+
+    @pl.loop(0, cells // PART)
+    def _(k):
+        c = pl.multiple_of(k * PART, PART)
+        lo, mid, hi = (pl.ds(pl.multiple_of(p * cells + c, PART), PART) for p in range(3))
         stiff = end_ref[hi, :] + unpack_small(small, 0, c, memb)
         middle = -(mine_ref[lo, :] + other_ref[lo, :]) / stiff
         outer = end_ref[lo, :] * middle - end_ref[mid, :]
@@ -384,19 +418,14 @@
             middle = back[mid, :] * u_in + back[hi, :] * u_out - back[lo, :]
             right = on_right("lat", level)
             u_in, u_out = jnp.where(right, middle, u_in), jnp.where(right, u_out, middle)
-        values[lo, :] = u_in
-        fluxes[lo, :] = coef_ref[mid, :] * u_out - coef_ref[lo, :] * u_in - own_ref[lo, :]
-    copies = []
-    for j in range(rows):
-        for c in range(0, cells, PART):
-            at = slice(j * cells + c, j * cells + c + PART)
-            lo = slice(c, c + PART)
-            out[at, :] = q_ref[at, :] + phi_ref[at, :] * values[lo, :] + psi_ref[at, :] * fluxes[lo, :]
-        copy = pltpu.make_async_copy(out.at[pl.ds(j * cells, cells), :], out_hbm.at[j], sem.at[j])
-        copy.start()
-        copies.append(copy)
-    for copy in copies:
-        copy.wait()
+        flux = coef_ref[mid, :] * u_out - coef_ref[lo, :] * u_in - own_ref[lo, :]
+        for j in range(rows):
+            at = pl.ds(pl.multiple_of(j * cells + c, PART), PART)
+            out[j, lo, :] = q_ref[at, :] + phi_ref[at, :] * u_in + psi_ref[at, :] * flux
+        chunk_copy(k).start()
+
+    for k in range(cells // PART):
+        chunk_copy(k).wait()
 
 
 def swapped(value, axis, mask):
@@ -424,40 +453,47 @@
             pltpu.VMEM((cols, 16, LANES), F32),
             pltpu.VMEM((rows, cols), F32),
             pltpu.VMEM((rows, cols), F32),
-            pltpu.SemaphoreType.DMA((cols // CHUNK, 2, rows)),
-            pltpu.SemaphoreType.DMA((2,)),
+            pltpu.VMEM((cols, 16, LANES), F32),
+            pltpu.VMEM((cols, 16, LANES), F32),
+            pltpu.SemaphoreType.DMA((2 * (cols // CHUNK) + 2,)),
         ],
         in_specs=[hbm_spec] * 4,
         cost=cost(2),
     )(*(in_hbm(x) for x in (ensemble.reshape(rows, cells, lev), grad_increment, normalization, lon_diffusion)))
 
-    y, weights = call(
-        functools.partial(vertical_kernel, stride=stride, rows=rows),
-        (shape(spaced, LANES), shape(2 * LANES, 2 * LANES, dtype=jnp.bfloat16)),
-        scratch=[pltpu.VMEM((8, LANES), F32)] + [pltpu.VMEM((LANES, LANES), F32)] * 3,
-        cost=cost(2),
-    )(vert_diag.reshape(1, lev), vert_sub.reshape(1, lev - 1), part)
-    phi, psi = call(
-        functools.partial(expand_kernel, memb=memb, stride=stride, rows=rows),
-        (shape(spaced, LANES), shape(spaced, LANES)),
-        cost=cost(1),
-    )(phi_t, psi_t)
-    step, lat_phi, lat_psi, coef, small, cosine = call(
-        functools.partial(lat_coef_kernel, memb=memb, stride=stride, bands=bands),
-        (
-            shape(spaced, LANES),
-            shape(rows * cells, LANES),
-            shape(rows * cells, LANES),
-            shape(3 * cells, LANES),
-            shape(8, LANES),
-            shape(16, LANES),
-        ),
-        cost=cost(1),
-    )(lat_diffusion)
-
     own, backs = pay, []
     for level in range(lon_levels - 1):
         other = swapped(pay, "lon", 1 << level)
+        if level == 0:
+            phi, psi = call(
+                functools.partial(expand_kernel, memb=memb, stride=stride, rows=rows),
+                (shape(spaced, LANES), shape(spaced, LANES)),
+                cost=cost(1),
+            )(phi_t, psi_t)
+            step, lat_phi, lat_psi, coef, small, cosine = call(
+                functools.partial(lat_coef_kernel, memb=memb, stride=stride, bands=bands),
+                (
+                    shape(spaced, LANES),
+                    shape(rows * cells, LANES),
+                    shape(rows * cells, LANES),
+                    shape(3 * cells, LANES),
+                    shape(8, LANES),
+                    shape(16, LANES),
+                ),
+                cost=cost(1),
+            )(lat_diffusion)
+            other, phi, psi, step, lat_phi, lat_psi, coef = lax.optimization_barrier(
+                (other, phi, psi, step, lat_phi, lat_psi, coef)
+            )
+        elif level == 1:
+            pay, part = lax.optimization_barrier((pay, part))
+            y, weights = call(
+                functools.partial(vertical_kernel, stride=stride, rows=rows),
+                (shape(spaced, LANES), shape(2 * LANES, 2 * LANES, dtype=jnp.bfloat16)),
+                scratch=[pltpu.VMEM((8, LANES), F32)] + [pltpu.VMEM((LANES, LANES), F32)] * 3,
+                cost=cost(2),
+            )(vert_diag.reshape(1, lev), vert_sub.reshape(1, lev - 1), part)
+            other, y, weights = lax.optimization_barrier((other, y, weights))
         pay, back = call(
             functools.partial(lon_merge_kernel, level=level, memb=memb, rest=rest),
             (shape(2 * half + 16, LANES), shape(half + 32, LANES)),
@@ -487,10 +523,8 @@
         functools.partial(finish_kernel, levels=lat_levels, memb=memb),
         shape(rows, cells, LANES),
         scratch=[
-            pltpu.VMEM((cells, LANES), F32),
-            pltpu.VMEM((cells, LANES), F32),
-            pltpu.VMEM((rows * cells, LANES), F32),
-            pltpu.SemaphoreType.DMA((rows,)),
+            pltpu.VMEM((rows, cells, LANES), F32),
+            pltpu.SemaphoreType.DMA((cells // PART,)),
         ],
         out_specs=hbm_spec,
         cost=cost(1),

time: 27 us -> 25.6 us (0.948)
  Pallas kernels: 7.3 us -> 5.9 us
    pallas_call x1, Pallas kernels: 2.7 us -> 1.57 us  [shards(): call(lon_sweep_kernel, (shape(cells, 16, LANES), shape(cols, 16, LANES),...]
    pallas_call x1, Pallas kernels: 1.58 us -> 1.31 us  [shards(): call(functools.partial(finish_kernel, levels=lat_levels, memb=memb), shap...]
  transfers between devices with their start and end apart: 5 -> 5, of which waited for: 5 -> 5; matrix products, arithmetic and copies ran while one was open for 0% -> 0% of each run, Pallas kernels for 7% -> 8%
where the time goes in v3:
time: 25.6 us; the launch traced here: 25.4 us
  starting transfers between devices  10.3 us (40%)
  waiting for transfers between devices  9.14 us (36%)
  Pallas kernels  5.9 us (23%)
    ppermute x5, starting transfers between devices, swapped(): lax.ppermute(value, axis, [(s, s ^ mask) for s in range(lax.axis_size(axi...  10.3 us
    ppermute x5, waiting for transfers between devices, swapped(): lax.ppermute(value, axis, [(s, s ^ mask) for s in range(lax.axis_size(axi...  9.14 us
    pallas_call x1, Pallas kernels, shards(): call(lon_sweep_kernel, (shape(cells, 16, LANES), shape(cols, 16, LANES),...  1.57 us
    pallas_call x1, Pallas kernels, shards(): call(functools.partial(finish_kernel, levels=lat_levels, memb=memb), shap...  1.31 us
    pallas_call x1, Pallas kernels, shards(): call(functools.partial(vertical_kernel, stride=stride, rows=rows), (shape...  1.23 us
    pallas_call x1, Pallas kernels, shards(): call(functools.partial(lat_sweep_kernel, levels=lon_levels, memb=memb, re...  0.69 us
  transfers between devices with their start and end apart: 5, of which 5 were waited for; matrix products, arithmetic and copies ran while one was open for 0% of the time, Pallas kernels for 8%

profile of v3, /device:TPU:0, one launch (start us, length us, event | category | flops | bytes accessed | tf_op | source)
XLA Modules:
  0.0 25.4 jit_solution(14140119817507254290)
XLA Ops:
  0.0 0.0 copy-start
  0.0 0.0 copy-start.1
  0.0 0.0 copy-start.2
  0.0 1.6 %shard_map.73 = (f32[192,16,128]{2,1,0:T(8,128)S(1)}, f32[48,16,128]{2,1,0:T(8,128)S(1)}, f32[48,16,128]{2,1,0:T(8,128)S(1)}, f32[112,128]{1,0:T(8,128)S(1)}) custom-call(f32[12,192,128]{2,1,0:T(8,128)} %bitcast.6, f32[12,48,128]{2,1,0:T(8,128)} %grad_hbm.1, f32[12,48]{1,0:T(8,128)} %norm_hbm.1, f32[12,48]{1,0:T(8,128)} %diff_hbm.1), custom_call_target="tpu_custom_call" | custom-call | bytes 6000000 | tf_op jit(solution)/shard_map/pallas_call | solution.py:448
  1.6 3.1 %collective-permute-start = (f32[112,128]{1,0:T(8,128)S(1)}, f32[112,128]{1,0:T(8,128)S(1)}, u32[]{:S(2)}, u32[]{:S(2)}) collective-permute-start(f32[112,128]{1,0:T(8,128)S(1)} %get-tuple-element.40.mine_ref.refs_0_), channel_id=1, source_target_pairs={{0,1},{1,0},{2,3},{3,2},{4,5},{5,4},{6,7},{7,6},{8,9},{9,8},{10,11... | collective-permute-start | bytes 172040 | tf_op jit(solution)/shard_map/ppermute | solution.py:432
  4.6 0.0 copy-done
  4.6 0.5 %shard_map.75 = (f32[2512,128]{1,0:T(8,128)S(1)}, f32[2304,128]{1,0:T(8,128)S(1)}, f32[2304,128]{1,0:T(8,128)S(1)}, f32[576,128]{1,0:T(8,128)S(1)}, f32[8,128]{1,0:T(8,128)S(1)}, /*index=5*/f32[16,128]{1,0:T(8,128)S(1)}) custom-call(f32[12,48]{1,0:T(8,128)S(1)} %copy-done), custom_call_target="tpu_custom_call" | custom-call | bytes 3000000 | tf_op jit(solution)/shard_map/pallas_call | solution.py:473
  5.1 0.2 shard_map.74
  5.4 1.4 %collective-permute-done.other_ref = f32[112,128]{1,0:T(8,128)S(1)} collective-permute-done((f32[112,128]{1,0:T(8,128)S(1)}, f32[112,128]{1,0:T(8,128)S(1)}, u32[]{:S(2)}, u32[]{:S(2)}) %collective-permute-start) | collective-permute-done | bytes 57376 | tf_op jit(solution)/shard_map/ppermute | solution.py:432
  6.8 0.1 shard_map.76
  6.9 2.1 %collective-permute-start.1 = (f32[112,128]{1,0:T(8,128)S(1)}, f32[112,128]{1,0:T(8,128)S(1)}, u32[]{:S(2)}, u32[]{:S(2)}) collective-permute-start(f32[112,128]{1,0:T(8,128)S(1)} %get-tuple-element.52.mine_ref), channel_id=1, source_target_pairs={{0,2},{1,3},{2,0},{3,1},{4,6},{5,7},{6,4},{7,5},{8,10},{9,11},{10,... | collective-permute-start | bytes 172040 | tf_op jit(solution)/shard_map/ppermute | solution.py:432
  9.0 0.0 copy-done.1
  9.0 0.0 copy-done.2
  9.0 1.2 %shard_map.77 = (f32[2512,128]{1,0:T(8,128)S(1)}, bf16[256,256]{1,0:T(8,128)(2,1)S(1)}) custom-call(f32[1,128]{1,0:T(1,128)S(1)} %bitcast.4, f32[1,127]{1,0:T(1,128)S(1)} %bitcast.5, f32[192,16,128]{2,1,0:T(8,128)S(1)} %get-tuple-element.53.part_ref), custom_call_target="tpu_custom_call" | custom-call | bytes 6000000 | tf_op jit(solution)/shard_map/pallas_call | solution.py:490
  10.3 0.9 %collective-permute-done.1.other_ref = f32[112,128]{1,0:T(8,128)S(1)} collective-permute-done((f32[112,128]{1,0:T(8,128)S(1)}, f32[112,128]{1,0:T(8,128)S(1)}, u32[]{:S(2)}, u32[]{:S(2)}) %collective-permute-start.1) | collective-permute-done | bytes 57376 | tf_op jit(solution)/shard_map/ppermute | solution.py:432
  11.2 0.1 shard_map.78
  11.3 3.1 %collective-permute-start.2 = (f32[112,128]{1,0:T(8,128)S(1)}, f32[112,128]{1,0:T(8,128)S(1)}, u32[]{:S(2)}, u32[]{:S(2)}) collective-permute-start(f32[112,128]{1,0:T(8,128)S(1)} %get-tuple-element.57.refs_1_), channel_id=1, source_target_pairs={{0,4},{1,5},{2,6},{3,7},{4,0},{5,1},{6,2},{7,3},{8,12},{9,13},{10,... | collective-permute-start | bytes 172040 | tf_op jit(solution)/shard_map/ppermute | solution.py:432
  14.4 2.2 %collective-permute-done.2.refs_2_ = f32[112,128]{1,0:T(8,128)S(1)} collective-permute-done((f32[112,128]{1,0:T(8,128)S(1)}, f32[112,128]{1,0:T(8,128)S(1)}, u32[]{:S(2)}, u32[]{:S(2)}) %collective-permute-start.2) | collective-permute-done | bytes 57376 | tf_op jit(solution)/shard_map/ppermute | solution.py:432
  16.5 0.7 %shard_map.79 = (f32[2304,128]{1,0:T(8,128)S(1)}, f32[392,128]{1,0:T(8,128)S(1)}) custom-call(f32[112,128]{1,0:T(8,128)S(1)} %get-tuple-element.40.mine_ref.refs_0_, f32[112,128]{1,0:T(8,128)S(1)} %get-tuple-element.57.refs_1_, f32[112,128]{1,0:T(8,128)S(1)} %collective-permute-done.2.refs_2_, f32[80,128]{1,0:T(8,128)S(1)} %get-tuple-element.58.refs_3_, ...), custom_call_target="tpu_custom_call" | custom-call | bytes 3000000 | tf_op jit(solution)/shard_map/pallas_call | solution.py:504
  17.2 0.1 collective-permute-start.3
  17.3 1.4 %collective-permute-done.3.other_ref = f32[392,128]{1,0:T(8,128)S(1)} collective-permute-done((f32[392,128]{1,0:T(8,128)S(1)}, f32[392,128]{1,0:T(8,128)S(1)}, u32[]{:S(2)}, u32[]{:S(2)}) %collective-permute-start.3) | collective-permute-done | bytes 200736 | tf_op jit(solution)/shard_map/ppermute | solution.py:432
  18.8 0.2 shard_map.80
  19.0 1.9 %collective-permute-start.4 = (f32[200,128]{1,0:T(8,128)S(1)}, f32[200,128]{1,0:T(8,128)S(1)}, u32[]{:S(2)}, u32[]{:S(2)}) collective-permute-start(f32[200,128]{1,0:T(8,128)S(1)} %get-tuple-element.69.refs_2_), channel_id=1, source_target_pairs={{0,16},{8,24},{16,0},{24,8},{1,17},{9,25},{17,1},{25,9},{2,18},{10... | collective-permute-start | bytes 307208 | tf_op jit(solution)/shard_map/ppermute | solution.py:432
  20.9 3.2 %collective-permute-done.4.refs_3_ = f32[200,128]{1,0:T(8,128)S(1)} collective-permute-done((f32[200,128]{1,0:T(8,128)S(1)}, f32[200,128]{1,0:T(8,128)S(1)}, u32[]{:S(2)}, u32[]{:S(2)}) %collective-permute-start.4) | collective-permute-done | bytes 102432 | tf_op jit(solution)/shard_map/ppermute | solution.py:432
  24.1 1.3 %shard_map.81 = f32[12,192,128]{2,1,0:T(8,128)} custom-call(f32[392,128]{1,0:T(8,128)S(1)} %get-tuple-element.68.mine_ref.refs_0_, f32[576,128]{1,0:T(8,128)S(1)} %get-tuple-element.65.refs_10_.coef_ref.refs_1_, f32[200,128]{1,0:T(8,128)S(1)} %get-tuple-element.69.refs_2_, f32[200,128]{1,0:T(8,128)S(1)} %collective-permute-done.4.refs_3_, ...), custom_call_target="tpu_custom_call" | custom-call | bytes 3000000 | tf_op jit(solution)/shard_map/pallas_call | solution.py:522
Async XLA Ops:
  0.0 4.6 %copy-start = (f32[12,48]{1,0:T(8,128)S(1)}, f32[12,48]{1,0:T(8,128)}, u32[]{:S(2)}) copy-start(f32[12,48]{1,0:T(8,128)} %diff_ref.1) | copy-start | bytes 6916
  0.0 9.0 %copy-start.1 = (f32[128]{0:T(128)S(1)}, f32[128]{0:T(128)}, u32[]{:S(2)}) copy-start(f32[128]{0:T(128)} %param.12) | copy-start | bytes 1540
  0.0 9.0 %copy-start.2 = (f32[127]{0:T(128)S(1)}, f32[127]{0:T(128)}, u32[]{:S(2)}) copy-start(f32[127]{0:T(128)} %param.13) | copy-start | bytes 1528
  1.6 5.2 %collective-permute-start = (f32[112,128]{1,0:T(8,128)S(1)}, f32[112,128]{1,0:T(8,128)S(1)}, u32[]{:S(2)}, u32[]{:S(2)}) collective-permute-start(f32[112,128]{1,0:T(8,128)S(1)} %get-tuple-element.40.mine_ref.refs_0_), channel_id=1, source_target_pairs={{0,1},{1,0},{2,3},{3,2},{4,5},{5,4},{6,7},{7,6},{8,9},{9,8},{10,11... | collective-permute-start | bytes 172040 | tf_op jit(solution)/shard_map/ppermute | solution.py:432
  6.9 4.3 %collective-permute-start.1 = (f32[112,128]{1,0:T(8,128)S(1)}, f32[112,128]{1,0:T(8,128)S(1)}, u32[]{:S(2)}, u32[]{:S(2)}) collective-permute-start(f32[112,128]{1,0:T(8,128)S(1)} %get-tuple-element.52.mine_ref), channel_id=1, source_target_pairs={{0,2},{1,3},{2,0},{3,1},{4,6},{5,7},{6,4},{7,5},{8,10},{9,11},{10,... | collective-permute-start | bytes 172040 | tf_op jit(solution)/shard_map/ppermute | solution.py:432
  11.3 5.3 %collective-permute-start.2 = (f32[112,128]{1,0:T(8,128)S(1)}, f32[112,128]{1,0:T(8,128)S(1)}, u32[]{:S(2)}, u32[]{:S(2)}) collective-permute-start(f32[112,128]{1,0:T(8,128)S(1)} %get-tuple-element.57.refs_1_), channel_id=1, source_target_pairs={{0,4},{1,5},{2,6},{3,7},{4,0},{5,1},{6,2},{7,3},{8,12},{9,13},{10,... | collective-permute-start | bytes 172040 | tf_op jit(solution)/shard_map/ppermute | solution.py:432
  17.2 1.5 %collective-permute-start.3 = (f32[392,128]{1,0:T(8,128)S(1)}, f32[392,128]{1,0:T(8,128)S(1)}, u32[]{:S(2)}, u32[]{:S(2)}) collective-permute-start(f32[392,128]{1,0:T(8,128)S(1)} %get-tuple-element.68.mine_ref.refs_0_), channel_id=1, source_target_pairs={{0,8},{8,0},{16,24},{24,16},{1,9},{9,1},{17,25},{25,17},{2,10},{10... | collective-permute-start | bytes 602120 | tf_op jit(solution)/shard_map/ppermute | solution.py:432
  19.0 5.1 %collective-permute-start.4 = (f32[200,128]{1,0:T(8,128)S(1)}, f32[200,128]{1,0:T(8,128)S(1)}, u32[]{:S(2)}, u32[]{:S(2)}) collective-permute-start(f32[200,128]{1,0:T(8,128)S(1)} %get-tuple-element.69.refs_2_), channel_id=1, source_target_pairs={{0,16},{8,24},{16,0},{24,8},{1,17},{9,25},{17,1},{25,9},{2,18},{10... | collective-permute-start | bytes 307208 | tf_op jit(solution)/shard_map/ppermute | solution.py:432

commit v4 on v3

--- a/solution.py
+++ b/solution.py
@@ -13,6 +13,7 @@
 CHUNK = 16
 PART = 64
 VMEM_BYTES = 16 * 2**20
+LOCAL_ROUND = 1
 
 
 def call(kernel, outs, scratch=(), in_specs=None, out_specs=None, cost=None):
@@ -141,42 +142,48 @@
 
 def lon_parts(pay, half):
     coef = pay[2 * half :]
-    a, b, d = (lane_of(coef, k, 16) for k in range(3))
-    return pay[:half], pay[half : 2 * half], a, b, d
-
-
-def lon_join(left, right, memb, rest):
-    half = memb * (8 + rest)
-    lh1, lh2, la, lb, ld = lon_parts(left, half)
-    rh1, rh2, ra, rb, rd = lon_parts(right, half)
+    return (pay[:half], pay[half : 2 * half]) + tuple(lane_of(coef, k, 16) for k in range(3))
+
+
+def lon_join(mine, other, right, memb, rest):
+    lh1, lh2, la, lb, ld = (jnp.where(right, o, m) for m, o in zip(mine, other))
+    rh1, rh2, ra, rb, rd = (jnp.where(right, m, o) for m, o in zip(mine, other))
     inv = 1.0 / (ld + ra)
     ca, cb = lb * inv, rb * inv
     grow = functools.partial(lon_expand, memb=memb, rest=rest)
     total = lh2 + rh1
-    s = total * grow(inv)
-    h1 = lh1 + grow(ca) * total
-    h2 = rh2 + grow(cb) * total
-    return h1, h2, la - lb * ca, lb * cb, rd - rb * cb, s, ca, cb
+    joined = (lh1 + grow(ca) * total, rh2 + grow(cb) * total, la - lb * ca, lb * cb, rd - rb * cb)
+    return joined, (total * grow(inv), ca, cb)
+
+
+def lon_join_round(pays, levels, memb, rest):
+    half = memb * (8 + rest)
+    groups = [lon_parts(p[...], half) for p in pays]
+    backs = []
+    for level in levels:
+        right = on_right("lon", level)
+        pairs = [lon_join(groups[k], groups[k + 1], right, memb, rest) for k in range(0, len(groups), 2)]
+        groups = [joined for joined, _ in pairs]
+        backs.append(pairs[0][1])
+    return groups[0], backs
 
 
 def on_right(axis, level):
     return ((lax.axis_index(axis) >> level) & 1) == 1
 
 
-def lon_merge_kernel(mine_ref, other_ref, pay_ref, back_ref, *, level, memb, rest):
-    right = on_right("lon", level)
-    mine, other = mine_ref[...], other_ref[...]
-    h1, h2, a, b, d, s, ca, cb = lon_join(
-        jnp.where(right, other, mine), jnp.where(right, mine, other), memb, rest
-    )
+def lon_merge_kernel(*refs, levels, memb, rest):
+    pays, (pay_ref, *back_refs) = refs[: 1 << len(levels)], refs[1 << len(levels) :]
+    (h1, h2, a, b, d), backs = lon_join_round(pays, levels, memb, rest)
     half = h1.shape[0]
     lanes = lax.broadcasted_iota(jnp.int32, a.shape, 1)
     pay_ref[:half, :] = h1
     pay_ref[half : 2 * half, :] = h2
     pay_ref[2 * half :, :] = jnp.where(lanes == 0, a, jnp.where(lanes == 1, b, d))
-    back_ref[:half, :] = s
-    back_ref[half : half + 16, :] = ca
-    back_ref[half + 16 :, :] = cb
+    for back_ref, (s, ca, cb) in zip(back_refs, backs):
+        back_ref[:half, :] = s
+        back_ref[half : half + 16, :] = ca
+        back_ref[half + 16 :, :] = cb
 
 
 def times_inverse(rows, weights):
@@ -278,25 +285,20 @@
 
 
 def lat_sweep_kernel(*refs, levels, memb, rest, stride):
-    own_ref, mine_ref, other_ref = refs[:3]
-    backs = refs[3 : 3 + levels - 1]
+    count = 1 << len(levels)
+    own_ref, pays, backs = refs[0], refs[1 : 1 + count], refs[1 + count : 1 + count + levels[0]]
     (y_ref, phi_ref, psi_ref, weights_ref, step_ref, coef_ref, small_ref, cos_ref, q_ref, pay_ref, ends, tiles) = refs[
-        3 + levels - 1 :
+        1 + count + levels[0] :
     ]
     rows = 8 + rest
     half = memb * rows
     grow = functools.partial(lon_expand, memb=memb, rest=rest)
-    right = on_right("lon", levels - 1)
-    mine, other = mine_ref[...], other_ref[...]
-    h1, h2, a, b, d, s, ca, cb = lon_join(
-        jnp.where(right, other, mine), jnp.where(right, mine, other), memb, rest
-    )
-    outer = -(h1 + h2) * grow(1.0 / (a + d - 2.0 * b))
-    middle = grow(ca + cb) * outer - s
-    u_in, u_out = jnp.where(right, middle, outer), jnp.where(right, outer, middle)
-    for level in reversed(range(levels - 1)):
-        back = backs[level]
-        middle = grow(back[half : half + 16, :]) * u_in + grow(back[half + 16 :, :]) * u_out - back[:half, :]
+    (h1, h2, a, b, d), last = lon_join_round(pays, levels, memb, rest)
+    u_in = -(h1 + h2) * grow(1.0 / (a + d - 2.0 * b))
+    u_out = u_in
+    stored = [(back[:half, :], back[half : half + 16, :], back[half + 16 :, :]) for back in backs]
+    for level, (s, ca, cb) in reversed(list(enumerate(stored + last))):
+        middle = grow(ca) * u_in + grow(cb) * u_out - s
         right = on_right("lon", level)
         u_in, u_out = jnp.where(right, middle, u_in), jnp.where(right, u_out, middle)
     oh1, _, oa, ob, _ = lon_parts(own_ref[...], half)
@@ -462,9 +464,13 @@
     )(*(in_hbm(x) for x in (ensemble.reshape(rows, cells, lev), grad_increment, normalization, lon_diffusion)))
 
     own, backs = pay, []
-    for level in range(lon_levels - 1):
-        other = swapped(pay, "lon", 1 << level)
-        if level == 0:
+    spans = lon_rounds(lon_levels)
+    for index, span in enumerate(spans):
+        others = [swapped(pay, "lon", k << span[0]) for k in reversed(range(1, 1 << len(span)))][::-1]
+        if index == LOCAL_ROUND:
+            pay, part, phi_t, psi_t, lat_diffusion = lax.optimization_barrier(
+                (pay, part, phi_t, psi_t, lat_diffusion)
+            )
             phi, psi = call(
                 functools.partial(expand_kernel, memb=memb, stride=stride, rows=rows),
                 (shape(spaced, LANES), shape(spaced, LANES)),
@@ -482,31 +488,28 @@
                 ),
                 cost=cost(1),
             )(lat_diffusion)
-            other, phi, psi, step, lat_phi, lat_psi, coef = lax.optimization_barrier(
-                (other, phi, psi, step, lat_phi, lat_psi, coef)
-            )
-        elif level == 1:
-            pay, part = lax.optimization_barrier((pay, part))
             y, weights = call(
                 functools.partial(vertical_kernel, stride=stride, rows=rows),
                 (shape(spaced, LANES), shape(2 * LANES, 2 * LANES, dtype=jnp.bfloat16)),
                 scratch=[pltpu.VMEM((8, LANES), F32)] + [pltpu.VMEM((LANES, LANES), F32)] * 3,
                 cost=cost(2),
             )(vert_diag.reshape(1, lev), vert_sub.reshape(1, lev - 1), part)
-            other, y, weights = lax.optimization_barrier((other, y, weights))
-        pay, back = call(
-            functools.partial(lon_merge_kernel, level=level, memb=memb, rest=rest),
-            (shape(2 * half + 16, LANES), shape(half + 32, LANES)),
-            cost=cost(1),
-        )(pay, other)
-        backs.append(back)
-    other = swapped(pay, "lon", 1 << (lon_levels - 1))
+            others, phi, psi, step, lat_phi, lat_psi, coef, small, cosine, y, weights = lax.optimization_barrier(
+                (others, phi, psi, step, lat_phi, lat_psi, coef, small, cosine, y, weights)
+            )
+        if index < len(spans) - 1:
+            pay, *more = call(
+                functools.partial(lon_merge_kernel, levels=span, memb=memb, rest=rest),
+                (shape(2 * half + 16, LANES),) + (shape(half + 32, LANES),) * len(span),
+                cost=cost(1),
+            )(pay, *others)
+            backs += more
     q, lat_pay = call(
-        functools.partial(lat_sweep_kernel, levels=lon_levels, memb=memb, rest=rest, stride=stride),
+        functools.partial(lat_sweep_kernel, levels=spans[-1], memb=memb, rest=rest, stride=stride),
         (shape(rows * cells, LANES), shape(2 * cells + 8, LANES)),
         scratch=[pltpu.VMEM((2 * half + 8, LANES), F32), pltpu.VMEM((16 * rows, LANES), F32)],
         cost=cost(1),
-    )(own, pay, other, *backs, y, phi, psi, weights, step, coef, small, cosine)
+    )(own, pay, *others, *backs, y, phi, psi, weights, step, coef, small, cosine)
 
     pay, group, lat_backs = lat_pay, coef, []
     for level in range(lat_levels - 1):
@@ -532,6 +535,10 @@
     return out.reshape(rows, cols, memb, lev)
 
 
+def lon_rounds(levels):
+    return [tuple(range(k, min(k + 2, levels))) for k in range(0, levels, 2)]
+
+
 def in_hbm(value):
     return pltpu.with_memory_space_constraint(value, pltpu.HBM)
 

time: 25.6 us -> 24.5 us (0.957)
  starting transfers between devices: 10.3 us -> 8.99 us
    ppermute x5 -> x6, starting transfers between devices: 10.3 us -> 8.99 us  [swapped(): lax.ppermute(value, axis, [(s, s ^ mask) for s in range(lax.axis_size(axi...]
    ppermute x5 -> x6, waiting for transfers between devices: 9.14 us -> 9.37 us  [swapped(): lax.ppermute(value, axis, [(s, s ^ mask) for s in range(lax.axis_size(axi...]
    pallas_call x3 -> x2, Pallas kernels: 0.87 us -> 0.8 us  [the longest x1 0.68 us: shards(): call(functools.partial(lat_sweep_kernel, levels=spans[-1], memb=memb, res...]
  transfers between devices with their start and end apart: 5 -> 6, of which waited for: 5 -> 6; matrix products, arithmetic and copies ran while one was open for 0% -> 0% of each run, Pallas kernels for 8% -> 8%
where the time goes in v4:
time: 24.5 us; the launch traced here: 24.3 us
  waiting for transfers between devices  9.37 us (38%)
  starting transfers between devices  8.99 us (37%)
  Pallas kernels  5.84 us (24%)
    ppermute x6, waiting for transfers between devices, swapped(): lax.ppermute(value, axis, [(s, s ^ mask) for s in range(lax.axis_size(axi...  9.37 us
    ppermute x6, starting transfers between devices, swapped(): lax.ppermute(value, axis, [(s, s ^ mask) for s in range(lax.axis_size(axi...  8.99 us
    pallas_call x1, Pallas kernels, shards(): call(lon_sweep_kernel, (shape(cells, 16, LANES), shape(cols, 16, LANES),...  1.57 us
    pallas_call x1, Pallas kernels, shards(): call(functools.partial(finish_kernel, levels=lat_levels, memb=memb), shap...  1.32 us
    pallas_call x1, Pallas kernels, shards(): call(functools.partial(vertical_kernel, stride=stride, rows=rows), (shape...  1.23 us
    pallas_call x1, Pallas kernels, shards(): call(functools.partial(lat_sweep_kernel, levels=spans[-1], memb=memb, res...  0.68 us
    pallas_call x1, Pallas kernels, shards(): call(functools.partial(lat_coef_kernel, memb=memb, stride=stride, bands=b...  0.49 us
  transfers between devices with their start and end apart: 6, of which 6 were waited for; matrix products, arithmetic and copies ran while one was open for 0% of the time, Pallas kernels for 8%

profile of v4, /device:TPU:0, one launch (start us, length us, event | category | flops | bytes accessed | tf_op | source)
XLA Modules:
  0.0 24.3 jit_solution(14191874728782012226)
XLA Ops:
  0.0 0.0 copy-start
  0.0 0.0 copy-start.2
  0.0 0.0 copy-start.1
  0.0 1.6 %shard_map.73 = (f32[192,16,128]{2,1,0:T(8,128)S(1)}, f32[48,16,128]{2,1,0:T(8,128)S(1)}, f32[48,16,128]{2,1,0:T(8,128)S(1)}, f32[112,128]{1,0:T(8,128)S(1)}) custom-call(f32[12,192,128]{2,1,0:T(8,128)} %bitcast.6, f32[12,48,128]{2,1,0:T(8,128)} %grad_hbm.1, f32[12,48]{1,0:T(8,128)} %norm_hbm.1, f32[12,48]{1,0:T(8,128)} %diff_hbm.1), custom_call_target="tpu_custom_call" | custom-call | bytes 6000000 | tf_op jit(solution)/shard_map/pallas_call | solution.py:450
  1.6 4.1 %collective-permute-start.2 = (f32[112,128]{1,0:T(8,128)S(1)}, f32[112,128]{1,0:T(8,128)S(1)}, u32[]{:S(2)}, u32[]{:S(2)}) collective-permute-start(f32[112,128]{1,0:T(8,128)S(1)} %get-tuple-element.43.refs_0_), channel_id=1, source_target_pairs={{0,3},{1,2},{2,1},{3,0},{4,7},{5,6},{6,5},{7,4},{8,11},{9,10},{10,... | collective-permute-start | bytes 172040 | tf_op jit(solution)/shard_map/ppermute | solution.py:434
  5.7 0.4 %collective-permute-start.1 = (f32[112,128]{1,0:T(8,128)S(1)}, f32[112,128]{1,0:T(8,128)S(1)}, u32[]{:S(2)}, u32[]{:S(2)}) collective-permute-start(f32[112,128]{1,0:T(8,128)S(1)} %get-tuple-element.43.refs_0_), channel_id=1, source_target_pairs={{0,2},{1,3},{2,0},{3,1},{4,6},{5,7},{6,4},{7,5},{8,10},{9,11},{10,... | collective-permute-start | bytes 172040 | tf_op jit(solution)/shard_map/ppermute | solution.py:434
  6.1 0.2 collective-permute-start
  6.3 1.6 %collective-permute-done.2.refs_3_ = f32[112,128]{1,0:T(8,128)S(1)} collective-permute-done((f32[112,128]{1,0:T(8,128)S(1)}, f32[112,128]{1,0:T(8,128)S(1)}, u32[]{:S(2)}, u32[]{:S(2)}) %collective-permute-start.2) | collective-permute-done | bytes 57376 | tf_op jit(solution)/shard_map/ppermute | solution.py:434
  7.9 2.0 %collective-permute-done.1.refs_2_ = f32[112,128]{1,0:T(8,128)S(1)} collective-permute-done((f32[112,128]{1,0:T(8,128)S(1)}, f32[112,128]{1,0:T(8,128)S(1)}, u32[]{:S(2)}, u32[]{:S(2)}) %collective-permute-start.1) | collective-permute-done | bytes 57376 | tf_op jit(solution)/shard_map/ppermute | solution.py:434
  9.8 0.4 %collective-permute-done.refs_1_ = f32[112,128]{1,0:T(8,128)S(1)} collective-permute-done((f32[112,128]{1,0:T(8,128)S(1)}, f32[112,128]{1,0:T(8,128)S(1)}, u32[]{:S(2)}, u32[]{:S(2)}) %collective-permute-start) | collective-permute-done | bytes 57376 | tf_op jit(solution)/shard_map/ppermute | solution.py:434
  10.3 0.1 shard_map.74
  10.4 2.7 %collective-permute-start.3 = (f32[112,128]{1,0:T(8,128)S(1)}, f32[112,128]{1,0:T(8,128)S(1)}, u32[]{:S(2)}, u32[]{:S(2)}) collective-permute-start(f32[112,128]{1,0:T(8,128)S(1)} %get-tuple-element.48.refs_1_), channel_id=1, source_target_pairs={{0,4},{1,5},{2,6},{3,7},{4,0},{5,1},{6,2},{7,3},{8,12},{9,13},{10,... | collective-permute-start | bytes 172040 | tf_op jit(solution)/shard_map/ppermute | solution.py:434
  13.1 0.0 copy-done
  13.1 0.5 %shard_map.76 = (f32[2512,128]{1,0:T(8,128)S(1)}, f32[2304,128]{1,0:T(8,128)S(1)}, f32[2304,128]{1,0:T(8,128)S(1)}, f32[576,128]{1,0:T(8,128)S(1)}, f32[8,128]{1,0:T(8,128)S(1)}, /*index=5*/f32[16,128]{1,0:T(8,128)S(1)}) custom-call(f32[12,48]{1,0:T(8,128)S(1)} %copy-done), custom_call_target="tpu_custom_call" | custom-call | bytes 3000000 | tf_op jit(solution)/shard_map/pallas_call | solution.py:479
  13.6 0.2 shard_map.75
  13.8 0.0 copy-done.2
  13.8 0.0 copy-done.1
  13.8 1.2 %shard_map.77 = (f32[2512,128]{1,0:T(8,128)S(1)}, bf16[256,256]{1,0:T(8,128)(2,1)S(1)}) custom-call(f32[1,128]{1,0:T(1,128)S(1)} %bitcast.4, f32[1,127]{1,0:T(1,128)S(1)} %bitcast.5, f32[192,16,128]{2,1,0:T(8,128)S(1)} %get-tuple-element.60.part_ref), custom_call_target="tpu_custom_call" | custom-call | bytes 6000000 | tf_op jit(solution)/shard_map/pallas_call | solution.py:491
  15.0 0.5 %collective-permute-done.3.refs_2_ = f32[112,128]{1,0:T(8,128)S(1)} collective-permute-done((f32[112,128]{1,0:T(8,128)S(1)}, f32[112,128]{1,0:T(8,128)S(1)}, u32[]{:S(2)}, u32[]{:S(2)}) %collective-permute-start.3) | collective-permute-done | bytes 57376 | tf_op jit(solution)/shard_map/ppermute | solution.py:434
  15.6 0.7 %shard_map.78 = (f32[2304,128]{1,0:T(8,128)S(1)}, f32[392,128]{1,0:T(8,128)S(1)}) custom-call(f32[112,128]{1,0:T(8,128)S(1)} %get-tuple-element.43.refs_0_, f32[112,128]{1,0:T(8,128)S(1)} %get-tuple-element.48.refs_1_, f32[112,128]{1,0:T(8,128)S(1)} %collective-permute-done.3.refs_2_, f32[80,128]{1,0:T(8,128)S(1)} %get-tuple-element.64.refs_3_, ...), custom_call_target="tpu_custom_call" | custom-call | bytes 3000000 | tf_op jit(solution)/shard_map/pallas_call | solution.py:507
  16.2 0.1 collective-permute-start.4
  16.3 1.4 %collective-permute-done.4.other_ref = f32[392,128]{1,0:T(8,128)S(1)} collective-permute-done((f32[392,128]{1,0:T(8,128)S(1)}, f32[392,128]{1,0:T(8,128)S(1)}, u32[]{:S(2)}, u32[]{:S(2)}) %collective-permute-start.4) | collective-permute-done | bytes 200736 | tf_op jit(solution)/shard_map/ppermute | solution.py:434
  17.8 0.2 shard_map.79
  18.0 1.6 %collective-permute-start.5 = (f32[200,128]{1,0:T(8,128)S(1)}, f32[200,128]{1,0:T(8,128)S(1)}, u32[]{:S(2)}, u32[]{:S(2)}) collective-permute-start(f32[200,128]{1,0:T(8,128)S(1)} %get-tuple-element.75.refs_2_), channel_id=1, source_target_pairs={{0,16},{8,24},{16,0},{24,8},{1,17},{9,25},{17,1},{25,9},{2,18},{10... | collective-permute-start | bytes 307208 | tf_op jit(solution)/shard_map/ppermute | solution.py:434
  19.5 3.4 %collective-permute-done.5.refs_3_ = f32[200,128]{1,0:T(8,128)S(1)} collective-permute-done((f32[200,128]{1,0:T(8,128)S(1)}, f32[200,128]{1,0:T(8,128)S(1)}, u32[]{:S(2)}, u32[]{:S(2)}) %collective-permute-start.5) | collective-permute-done | bytes 102432 | tf_op jit(solution)/shard_map/ppermute | solution.py:434
  23.0 1.3 %shard_map.80 = f32[12,192,128]{2,1,0:T(8,128)} custom-call(f32[392,128]{1,0:T(8,128)S(1)} %get-tuple-element.74.mine_ref.refs_0_, f32[576,128]{1,0:T(8,128)S(1)} %get-tuple-element.71.refs_10_.coef_ref.refs_1_, f32[200,128]{1,0:T(8,128)S(1)} %get-tuple-element.75.refs_2_, f32[200,128]{1,0:T(8,128)S(1)} %collective-permute-done.5.refs_3_, ...), custom_call_target="tpu_custom_call" | custom-call | bytes 3000000 | tf_op jit(solution)/shard_map/pallas_call | solution.py:525
Async XLA Ops:
  0.0 13.1 %copy-start = (f32[12,48]{1,0:T(8,128)S(1)}, f32[12,48]{1,0:T(8,128)}, u32[]{:S(2)}) copy-start(f32[12,48]{1,0:T(8,128)} %diff_ref) | copy-start | bytes 6916
  0.0 13.8 %copy-start.2 = (f32[127]{0:T(128)S(1)}, f32[127]{0:T(128)}, u32[]{:S(2)}) copy-start(f32[127]{0:T(128)} %param.13) | copy-start | bytes 1528
  0.0 13.8 %copy-start.1 = (f32[128]{0:T(128)S(1)}, f32[128]{0:T(128)}, u32[]{:S(2)}) copy-start(f32[128]{0:T(128)} %param.12) | copy-start | bytes 1540
  1.6 6.3 %collective-permute-start.2 = (f32[112,128]{1,0:T(8,128)S(1)}, f32[112,128]{1,0:T(8,128)S(1)}, u32[]{:S(2)}, u32[]{:S(2)}) collective-permute-start(f32[112,128]{1,0:T(8,128)S(1)} %get-tuple-element.43.refs_0_), channel_id=1, source_target_pairs={{0,3},{1,2},{2,1},{3,0},{4,7},{5,6},{6,5},{7,4},{8,11},{9,10},{10,... | collective-permute-start | bytes 172040 | tf_op jit(solution)/shard_map/ppermute | solution.py:434
  5.7 4.2 %collective-permute-start.1 = (f32[112,128]{1,0:T(8,128)S(1)}, f32[112,128]{1,0:T(8,128)S(1)}, u32[]{:S(2)}, u32[]{:S(2)}) collective-permute-start(f32[112,128]{1,0:T(8,128)S(1)} %get-tuple-element.43.refs_0_), channel_id=1, source_target_pairs={{0,2},{1,3},{2,0},{3,1},{4,6},{5,7},{6,4},{7,5},{8,10},{9,11},{10,... | collective-permute-start | bytes 172040 | tf_op jit(solution)/shard_map/ppermute | solution.py:434
  6.1 4.2 %collective-permute-start = (f32[112,128]{1,0:T(8,128)S(1)}, f32[112,128]{1,0:T(8,128)S(1)}, u32[]{:S(2)}, u32[]{:S(2)}) collective-permute-start(f32[112,128]{1,0:T(8,128)S(1)} %get-tuple-element.43.refs_0_), channel_id=1, source_target_pairs={{0,1},{1,0},{2,3},{3,2},{4,5},{5,4},{6,7},{7,6},{8,9},{9,8},{10,11... | collective-permute-start | bytes 172040 | tf_op jit(solution)/shard_map/ppermute | solution.py:434
  10.4 5.1 %collective-permute-start.3 = (f32[112,128]{1,0:T(8,128)S(1)}, f32[112,128]{1,0:T(8,128)S(1)}, u32[]{:S(2)}, u32[]{:S(2)}) collective-permute-start(f32[112,128]{1,0:T(8,128)S(1)} %get-tuple-element.48.refs_1_), channel_id=1, source_target_pairs={{0,4},{1,5},{2,6},{3,7},{4,0},{5,1},{6,2},{7,3},{8,12},{9,13},{10,... | collective-permute-start | bytes 172040 | tf_op jit(solution)/shard_map/ppermute | solution.py:434
  16.2 1.5 %collective-permute-start.4 = (f32[392,128]{1,0:T(8,128)S(1)}, f32[392,128]{1,0:T(8,128)S(1)}, u32[]{:S(2)}, u32[]{:S(2)}) collective-permute-start(f32[392,128]{1,0:T(8,128)S(1)} %get-tuple-element.74.mine_ref.refs_0_), channel_id=1, source_target_pairs={{0,8},{8,0},{16,24},{24,16},{1,9},{9,1},{17,25},{25,17},{2,10},{10... | collective-permute-start | bytes 602120 | tf_op jit(solution)/shard_map/ppermute | solution.py:434
  18.0 5.0 %collective-permute-start.5 = (f32[200,128]{1,0:T(8,128)S(1)}, f32[200,128]{1,0:T(8,128)S(1)}, u32[]{:S(2)}, u32[]{:S(2)}) collective-permute-start(f32[200,128]{1,0:T(8,128)S(1)} %get-tuple-element.75.refs_2_), channel_id=1, source_target_pairs={{0,16},{8,24},{16,0},{24,8},{1,17},{9,25},{17,1},{25,9},{2,18},{10... | collective-permute-start | bytes 307208 | tf_op jit(solution)/shard_map/ppermute | solution.py:434

commit v5 on v4

--- a/solution.py
+++ b/solution.py
@@ -7,6 +7,7 @@
 from jax.experimental import pallas as pl
 from jax.experimental.pallas import tpu as pltpu
 from jax.sharding import PartitionSpec as P
+
 
 F32 = jnp.float32
 LANES = 128
@@ -284,12 +285,13 @@
     return out
 
 
-def lat_sweep_kernel(*refs, levels, memb, rest, stride):
+def lat_sweep_kernel(*refs, levels, memb, rest, stride, paired):
     count = 1 << len(levels)
     own_ref, pays, backs = refs[0], refs[1 : 1 + count], refs[1 + count : 1 + count + levels[0]]
-    (y_ref, phi_ref, psi_ref, weights_ref, step_ref, coef_ref, small_ref, cos_ref, q_ref, pay_ref, ends, tiles) = refs[
-        1 + count + levels[0] :
-    ]
+    refs = refs[1 + count + levels[0] :]
+    y_ref, phi_ref, psi_ref, weights_ref, step_ref, coef_ref, small_ref, cos_ref = refs[:8]
+    weight_ref, sum_ref = (refs[8], refs[11]) if paired else (None, None)
+    (q_ref, pay_ref), (ends, tiles) = refs[8 + paired : 10 + paired], refs[-2:]
     rows = 8 + rest
     half = memb * rows
     grow = functools.partial(lon_expand, memb=memb, rest=rest)
@@ -327,8 +329,13 @@
             v = v + step_ref[at, :] * flux
         b = coef_ref[cells + c : cells + c + PART, :]
         d = coef_ref[2 * cells + c : 2 * cells + c + PART, :]
-        pay_ref[c : c + PART, :] = v * b
-        pay_ref[cells + c : cells + c + PART, :] = flux - d * v
+        h1, h2 = v * b, flux - d * v
+        pay_ref[c : c + PART, :] = h1
+        pay_ref[cells + c : cells + c + PART, :] = h2
+        if paired:
+            sum_ref[c : c + PART, :] = (
+                weight_ref[c : c + PART, :] * h1 + weight_ref[cells + c : cells + c + PART, :] * h2
+            )
     pay_ref[2 * cells :, :] = small_ref[...]
 
 
@@ -378,7 +385,6 @@
             stiff = tied - b * lean
             end_ref[lo, :] = lean
             end_ref[mid, :] = h_free * free_inv
-            end_ref[hi, :] = stiff
             values = (stiff,)
         else:
             pay_ref[lo, :] = h1
@@ -394,14 +400,57 @@
     pay_ref[cells * (1 if ready else 2) :, :] = pack_small(lines)
 
 
+def lat_pair_kernel(coef_ref, other_ref, weight_ref, small_ref, *, memb):
+    cells = coef_ref.shape[0] // 3
+    right, upper = on_right("lat", 0), on_right("lat", 1)
+    small = other_ref[...]
+    acc = jnp.zeros((8, LANES), F32)
+    one = jnp.ones((PART, LANES), F32)
+    for c in range(0, cells, PART):
+        lo, mid, hi = (slice(k * cells + c, k * cells + c + PART) for k in range(3))
+        mine = [coef_ref[lo, :], coef_ref[mid, :], coef_ref[hi, :]]
+        other = [unpack_small(small, k, c, memb) for k in range(3)]
+        la, lb, ld = (jnp.where(right, o, m) for m, o in zip(mine, other))
+        ra, rb, rd = (jnp.where(right, m, o) for m, o in zip(mine, other))
+        inv = 1.0 / (ld + ra)
+        ca, cb = lb * inv, rb * inv
+        a, b, d = la - lb * ca, lb * cb, rd - rb * cb
+        free, tied = jnp.where(upper, d, a), jnp.where(upper, a, d)
+        lean = b / free
+        shared = jnp.where(upper, ca + lean * cb, cb + lean * ca)
+        own = jnp.where(right == upper, lean, one)
+        weight_ref[lo, :] = jnp.where(right, shared, own)
+        weight_ref[mid, :] = jnp.where(right, own, shared)
+        acc = pick_small(acc, tied - b * lean, c, memb)
+    small_ref[...] = pack_small([jnp.sum(acc, axis=0, keepdims=True)])
+
+
+def pick_small(acc, value, c, memb):
+    row = lax.broadcasted_iota(jnp.int32, (PART, LANES), 0) + c
+    chosen = jnp.where(row == lax.broadcasted_iota(jnp.int32, (PART, LANES), 1) * memb, value, 0.0)
+    for r in range(0, PART, 8):
+        acc = acc + chosen[r : r + 8]
+    return acc
+
+
+def lat_add_kernel(mine_ref, other_ref, small_ref, pay_ref):
+    cells = mine_ref.shape[0]
+    pay_ref[:cells, :] = mine_ref[...] + other_ref[...]
+    pay_ref[cells:, :] = small_ref[...]
+
+
 def finish_kernel(*refs, levels, memb):
     own_ref, coef_ref, mine_ref, other_ref, end_ref = refs[:5]
     backs = refs[5 : 5 + levels - 1]
-    q_ref, phi_ref, psi_ref, out_hbm, out, sem = refs[5 + levels - 1 :]
+    q_ref, phi_ref, psi_ref, out_hbm, out, middles, sem = refs[5 + levels - 1 :]
     cells = coef_ref.shape[0] // 3
     rows = q_ref.shape[0] // cells
     upper = on_right("lat", levels - 1)
-    small = other_ref[cells:, :]
+    soft = 1.0 / (mine_ref[cells:, :] + other_ref[cells:, :])
+    for c in range(0, cells, PART):
+        middles[c : c + PART, :] = -(mine_ref[c : c + PART, :] + other_ref[c : c + PART, :]) * unpack_small(
+            soft, 0, c, memb
+        )
 
     def chunk_copy(k):
         at = pl.ds(pl.multiple_of(k * PART, PART), PART)
@@ -411,8 +460,7 @@
     def _(k):
         c = pl.multiple_of(k * PART, PART)
         lo, mid, hi = (pl.ds(pl.multiple_of(p * cells + c, PART), PART) for p in range(3))
-        stiff = end_ref[hi, :] + unpack_small(small, 0, c, memb)
-        middle = -(mine_ref[lo, :] + other_ref[lo, :]) / stiff
+        middle = middles[lo, :]
         outer = end_ref[lo, :] * middle - end_ref[mid, :]
         u_in, u_out = jnp.where(upper, middle, outer), jnp.where(upper, outer, middle)
         for level in reversed(range(levels - 1)):
@@ -437,7 +485,7 @@
 def shards(ensemble, grad_increment, normalization, lon_diffusion, lat_diffusion, vert_diag, vert_sub):
     rows, cols, memb, lev = ensemble.shape
     bands, blocks = lax.axis_size("lat"), lax.axis_size("lon")
-    lat_levels, lon_levels = int(math.log2(bands)), int(math.log2(blocks))
+    lat_levels, lon_levels = levels_of(bands), levels_of(blocks)
     assert lev == LANES and 8 < rows <= 16 and 8 % memb == 0 and cols <= LANES and cols % CHUNK == 0
     assert 2**lat_levels == bands and 2**lon_levels == blocks and lat_levels >= 2 and lon_levels >= 2
     rest, cells = rows - 8, cols * memb
@@ -464,6 +512,7 @@
     )(*(in_hbm(x) for x in (ensemble.reshape(rows, cells, lev), grad_increment, normalization, lon_diffusion)))
 
     own, backs = pay, []
+    paired = lat_levels == 2
     spans = lon_rounds(lon_levels)
     for index, span in enumerate(spans):
         others = [swapped(pay, "lon", k << span[0]) for k in reversed(range(1, 1 << len(span)))][::-1]
@@ -488,14 +537,24 @@
                 ),
                 cost=cost(1),
             )(lat_diffusion)
+            if paired:
+                pair_weight, pair_small = call(
+                    functools.partial(lat_pair_kernel, memb=memb),
+                    (shape(2 * cells, LANES), shape(8, LANES)),
+                    cost=cost(1),
+                )(coef, swapped(small, "lat", 1))
+            else:
+                pair_weight = pair_small = small
             y, weights = call(
                 functools.partial(vertical_kernel, stride=stride, rows=rows),
                 (shape(spaced, LANES), shape(2 * LANES, 2 * LANES, dtype=jnp.bfloat16)),
                 scratch=[pltpu.VMEM((8, LANES), F32)] + [pltpu.VMEM((LANES, LANES), F32)] * 3,
                 cost=cost(2),
             )(vert_diag.reshape(1, lev), vert_sub.reshape(1, lev - 1), part)
-            others, phi, psi, step, lat_phi, lat_psi, coef, small, cosine, y, weights = lax.optimization_barrier(
-                (others, phi, psi, step, lat_phi, lat_psi, coef, small, cosine, y, weights)
+            others, phi, psi, step, lat_phi, lat_psi, coef, cosine, y, weights, pair_weight, pair_small = (
+                lax.optimization_barrier(
+                    (others, phi, psi, step, lat_phi, lat_psi, coef, cosine, y, weights, pair_weight, pair_small)
+                )
             )
         if index < len(spans) - 1:
             pay, *more = call(
@@ -504,35 +563,61 @@
                 cost=cost(1),
             )(pay, *others)
             backs += more
-    q, lat_pay = call(
-        functools.partial(lat_sweep_kernel, levels=spans[-1], memb=memb, rest=rest, stride=stride),
-        (shape(rows * cells, LANES), shape(2 * cells + 8, LANES)),
+    q, lat_pay, *sums = call(
+        functools.partial(
+            lat_sweep_kernel, levels=spans[-1], memb=memb, rest=rest, stride=stride, paired=paired
+        ),
+        (shape(rows * cells, LANES), shape(2 * cells + 8, LANES)) + (shape(cells, LANES),) * paired,
         scratch=[pltpu.VMEM((2 * half + 8, LANES), F32), pltpu.VMEM((16 * rows, LANES), F32)],
         cost=cost(1),
-    )(own, pay, *others, *backs, y, phi, psi, weights, step, coef, small, cosine)
-
-    pay, group, lat_backs = lat_pay, coef, []
-    for level in range(lat_levels - 1):
-        other = swapped(pay, "lat", 1 << level)
-        ready = level == lat_levels - 2
-        pay, back, group = call(
-            functools.partial(lat_merge_kernel, level=level, levels=lat_levels, memb=memb),
-            (shape((1 if ready else 2) * cells + 8, LANES), shape(3 * cells, LANES), shape(3 * cells, LANES)),
+    )(own, pay, *others, *backs, y, phi, psi, weights, step, coef, small, cosine, *(pair_weight,) * paired)
+
+    if paired:
+        pay = call(lat_add_kernel, shape(cells + 8, LANES), cost=cost(1))(
+            sums[0], swapped(sums[0], "lat", 1), pair_small
+        )
+        final = swapped(pay, "lat", 3)
+        behind, _ = lax.optimization_barrier((lat_pay, pay))
+        inner = swapped(behind, "lat", 1)
+        _, back, group = call(
+            functools.partial(lat_merge_kernel, level=0, levels=2, memb=memb),
+            (shape(cells + 8, LANES), shape(3 * cells, LANES), shape(2 * cells, LANES)),
             cost=cost(1),
-        )(pay, group, other)
-        lat_backs.append(back)
-    other = swapped(pay, "lat", 1 << (lat_levels - 1))
+        )(lat_pay, coef, inner)
+        lat_backs = [back]
+        final, group, back = lax.optimization_barrier((final, group, back))
+    else:
+        pay, group, lat_backs = lat_pay, coef, []
+        for level in range(lat_levels - 1):
+            other = swapped(pay, "lat", 1 << level)
+            ready = level == lat_levels - 2
+            pay, back, group = call(
+                functools.partial(lat_merge_kernel, level=level, levels=lat_levels, memb=memb),
+                (
+                    shape((1 if ready else 2) * cells + 8, LANES),
+                    shape(3 * cells, LANES),
+                    shape((2 if ready else 3) * cells, LANES),
+                ),
+                cost=cost(1),
+            )(pay, group, other)
+            lat_backs.append(back)
+        final = swapped(pay, "lat", 1 << (lat_levels - 1) | 1)
     out = call(
         functools.partial(finish_kernel, levels=lat_levels, memb=memb),
         shape(rows, cells, LANES),
         scratch=[
             pltpu.VMEM((rows, cells, LANES), F32),
+            pltpu.VMEM((cells, LANES), F32),
             pltpu.SemaphoreType.DMA((cells // PART,)),
         ],
         out_specs=hbm_spec,
         cost=cost(1),
-    )(lat_pay, coef, pay, other, group, *lat_backs, q, lat_phi, lat_psi)
+    )(lat_pay, coef, pay, final, group, *lat_backs, q, lat_phi, lat_psi)
     return out.reshape(rows, cols, memb, lev)
+
+
+def levels_of(count):
+    return int(math.log2(count))
 
 
 def lon_rounds(levels):

time: 24.5 us -> 24.2 us (0.988)
  waiting for transfers between devices: 9.37 us -> 7.8 us
  Pallas kernels: 5.84 us -> 6.64 us
  starting transfers between devices: 8.99 us -> 9.46 us
    ppermute x6 -> x8, waiting for transfers between devices: 9.37 us -> 7.8 us  [swapped(): lax.ppermute(value, axis, [(s, s ^ mask) for s in range(lax.axis_size(axi...]
    pallas_call x1 -> x3, Pallas kernels: 0.23 us -> 1.1 us  [the longest x1 0.88 us: shards(): call(functools.partial(lat_merge_kernel, level=0, levels=2, memb=memb), (...]
    ppermute x6 -> x8, starting transfers between devices: 8.99 us -> 9.46 us  [swapped(): lax.ppermute(value, axis, [(s, s ^ mask) for s in range(lax.axis_size(axi...]
  transfers between devices with their start and end apart: 6 -> 8, of which waited for: 6 -> 6; matrix products, arithmetic and copies ran while one was open for 0% -> 0% of each run, Pallas kernels for 8% -> 13%
where the time goes in v5:
time: 24.2 us; the launch traced here: 24 us
  starting transfers between devices  9.46 us (39%)
  waiting for transfers between devices  7.8 us (32%)
  Pallas kernels  6.64 us (27%)
    ppermute x8, starting transfers between devices, swapped(): lax.ppermute(value, axis, [(s, s ^ mask) for s in range(lax.axis_size(axi...  9.46 us
    ppermute x8, waiting for transfers between devices, swapped(): lax.ppermute(value, axis, [(s, s ^ mask) for s in range(lax.axis_size(axi...  7.8 us
    pallas_call x1, Pallas kernels, shards(): call(lon_sweep_kernel, (shape(cells, 16, LANES), shape(cols, 16, LANES),...  1.57 us
    pallas_call x1, Pallas kernels, shards(): call(functools.partial(vertical_kernel, stride=stride, rows=rows), (shape...  1.23 us
    pallas_call x1, Pallas kernels, shards(): call(functools.partial(finish_kernel, levels=lat_levels, memb=memb), shap...  1.22 us
    pallas_call x1, Pallas kernels, shards(): call(functools.partial(lat_merge_kernel, level=0, levels=2, memb=memb), (...  0.88 us
    pallas_call x1, Pallas kernels, shards(): call(functools.partial(lat_sweep_kernel, levels=spans[-1], memb=memb, res...  0.7 us
    pallas_call x1, Pallas kernels, shards(): call(functools.partial(lat_coef_kernel, memb=memb, stride=stride, bands=b...  0.49 us
  transfers between devices with their start and end apart: 8, of which 6 were waited for; matrix products, arithmetic and copies ran while one was open for 0% of the time, Pallas kernels for 13%

profile of v5, /device:TPU:0, one launch (start us, length us, event | category | flops | bytes accessed | tf_op | source)
XLA Modules:
  0.0 24.0 jit_solution(6386575717477085627)
XLA Ops:
  0.0 0.0 copy-start
  0.0 0.0 copy-start.2
  0.0 0.0 copy-start.1
  0.0 1.6 %shard_map.73 = (f32[192,16,128]{2,1,0:T(8,128)S(1)}, f32[48,16,128]{2,1,0:T(8,128)S(1)}, f32[48,16,128]{2,1,0:T(8,128)S(1)}, f32[112,128]{1,0:T(8,128)S(1)}) custom-call(f32[12,192,128]{2,1,0:T(8,128)} %bitcast.6, f32[12,48,128]{2,1,0:T(8,128)} %grad_hbm.1, f32[12,48]{1,0:T(8,128)} %norm_hbm.1, f32[12,48]{1,0:T(8,128)} %diff_hbm.1), custom_call_target="tpu_custom_call" | custom-call | bytes 6000000 | tf_op jit(solution)/shard_map/pallas_call | solution.py:498
  1.6 4.1 %collective-permute-start.2 = (f32[112,128]{1,0:T(8,128)S(1)}, f32[112,128]{1,0:T(8,128)S(1)}, u32[]{:S(2)}, u32[]{:S(2)}) collective-permute-start(f32[112,128]{1,0:T(8,128)S(1)} %get-tuple-element.49.refs_0_), channel_id=1, source_target_pairs={{0,3},{1,2},{2,1},{3,0},{4,7},{5,6},{6,5},{7,4},{8,11},{9,10},{10,... | collective-permute-start | bytes 172040 | tf_op jit(solution)/shard_map/ppermute | solution.py:482
  5.7 0.4 %collective-permute-start.1 = (f32[112,128]{1,0:T(8,128)S(1)}, f32[112,128]{1,0:T(8,128)S(1)}, u32[]{:S(2)}, u32[]{:S(2)}) collective-permute-start(f32[112,128]{1,0:T(8,128)S(1)} %get-tuple-element.49.refs_0_), channel_id=1, source_target_pairs={{0,2},{1,3},{2,0},{3,1},{4,6},{5,7},{6,4},{7,5},{8,10},{9,11},{10,... | collective-permute-start | bytes 172040 | tf_op jit(solution)/shard_map/ppermute | solution.py:482
  6.1 0.2 collective-permute-start
  6.3 1.6 %collective-permute-done.2.refs_3_ = f32[112,128]{1,0:T(8,128)S(1)} collective-permute-done((f32[112,128]{1,0:T(8,128)S(1)}, f32[112,128]{1,0:T(8,128)S(1)}, u32[]{:S(2)}, u32[]{:S(2)}) %collective-permute-start.2) | collective-permute-done | bytes 57376 | tf_op jit(solution)/shard_map/ppermute | solution.py:482
  7.9 2.0 %collective-permute-done.1.refs_2_ = f32[112,128]{1,0:T(8,128)S(1)} collective-permute-done((f32[112,128]{1,0:T(8,128)S(1)}, f32[112,128]{1,0:T(8,128)S(1)}, u32[]{:S(2)}, u32[]{:S(2)}) %collective-permute-start.1) | collective-permute-done | bytes 57376 | tf_op jit(solution)/shard_map/ppermute | solution.py:482
  9.8 0.4 %collective-permute-done.refs_1_ = f32[112,128]{1,0:T(8,128)S(1)} collective-permute-done((f32[112,128]{1,0:T(8,128)S(1)}, f32[112,128]{1,0:T(8,128)S(1)}, u32[]{:S(2)}, u32[]{:S(2)}) %collective-permute-start) | collective-permute-done | bytes 57376 | tf_op jit(solution)/shard_map/ppermute | solution.py:482
  10.3 0.1 shard_map.74
  10.4 2.7 %collective-permute-start.3 = (f32[112,128]{1,0:T(8,128)S(1)}, f32[112,128]{1,0:T(8,128)S(1)}, u32[]{:S(2)}, u32[]{:S(2)}) collective-permute-start(f32[112,128]{1,0:T(8,128)S(1)} %get-tuple-element.54.refs_1_), channel_id=1, source_target_pairs={{0,4},{1,5},{2,6},{3,7},{4,0},{5,1},{6,2},{7,3},{8,12},{9,13},{10,... | collective-permute-start | bytes 172040 | tf_op jit(solution)/shard_map/ppermute | solution.py:482
  13.1 0.0 copy-done
  13.1 0.5 %shard_map.76 = (f32[2512,128]{1,0:T(8,128)S(1)}, f32[2304,128]{1,0:T(8,128)S(1)}, f32[2304,128]{1,0:T(8,128)S(1)}, f32[576,128]{1,0:T(8,128)S(1)}, f32[8,128]{1,0:T(8,128)S(1)}, /*index=5*/f32[16,128]{1,0:T(8,128)S(1)}) custom-call(f32[12,48]{1,0:T(8,128)S(1)} %copy-done), custom_call_target="tpu_custom_call" | custom-call | bytes 3000000 | tf_op jit(solution)/shard_map/pallas_call | solution.py:528
  13.6 0.1 collective-permute-start.4
  13.6 0.2 shard_map.75
  13.9 0.0 copy-done.2
  13.9 0.0 copy-done.1
  13.9 1.2 %shard_map.77 = (f32[2512,128]{1,0:T(8,128)S(1)}, bf16[256,256]{1,0:T(8,128)(2,1)S(1)}) custom-call(f32[1,128]{1,0:T(1,128)S(1)} %bitcast.4, f32[1,127]{1,0:T(1,128)S(1)} %bitcast.5, f32[192,16,128]{2,1,0:T(8,128)S(1)} %get-tuple-element.65.part_ref), custom_call_target="tpu_custom_call" | custom-call | bytes 6000000 | tf_op jit(solution)/shard_map/pallas_call | solution.py:548
  15.1 0.0 collective-permute-done.4.other_ref
  15.1 0.2 shard_map.78
  15.3 0.2 collective-permute-done.3.refs_2_
  15.6 0.7 %shard_map.79 = (f32[2304,128]{1,0:T(8,128)S(1)}, f32[392,128]{1,0:T(8,128)S(1)}, f32[192,128]{1,0:T(8,128)S(1)}) custom-call(f32[112,128]{1,0:T(8,128)S(1)} %get-tuple-element.49.refs_0_, f32[112,128]{1,0:T(8,128)S(1)} %get-tuple-element.54.refs_1_, f32[112,128]{1,0:T(8,128)S(1)} %collective-permute-done.3.refs_2_, ...), custom_call_target="tpu_custom_call" | custom-call | bytes 3000000 | tf_op jit(solution)/shard_map/pallas_call | solution.py:566
  16.3 0.4 %collective-permute-start.5 = (f32[192,128]{1,0:T(8,128)S(1)}, f32[192,128]{1,0:T(8,128)S(1)}, u32[]{:S(2)}, u32[]{:S(2)}) collective-permute-start(f32[192,128]{1,0:T(8,128)S(1)} %get-tuple-element.83.mine_ref), channel_id=1, source_target_pairs={{0,8},{8,0},{16,24},{24,16},{1,9},{9,1},{17,25},{25,17},{2,10},{10... | collective-permute-start | bytes 294920 | tf_op jit(solution)/shard_map/ppermute | solution.py:482
  16.6 1.0 %collective-permute-done.5.other_ref = f32[192,128]{1,0:T(8,128)S(1)} collective-permute-done((f32[192,128]{1,0:T(8,128)S(1)}, f32[192,128]{1,0:T(8,128)S(1)}, u32[]{:S(2)}, u32[]{:S(2)}) %collective-permute-start.5) | collective-permute-done | bytes 98336 | tf_op jit(solution)/shard_map/ppermute | solution.py:482
  17.6 0.4 %collective-permute-start.7 = (f32[392,128]{1,0:T(8,128)S(1)}, f32[392,128]{1,0:T(8,128)S(1)}, u32[]{:S(2)}, u32[]{:S(2)}) collective-permute-start(f32[392,128]{1,0:T(8,128)S(1)} %get-tuple-element.85.mine_ref.refs_0_), channel_id=1, source_target_pairs={{0,8},{8,0},{16,24},{24,16},{1,9},{9,1},{17,25},{25,17},{2,10},{10... | collective-permute-start | bytes 602120 | tf_op jit(solution)/shard_map/ppermute | solution.py:482
  18.0 1.3 %collective-permute-start.6 = (f32[200,128]{1,0:T(8,128)S(1)}, f32[200,128]{1,0:T(8,128)S(1)}, u32[]{:S(2)}, u32[]{:S(2)}) collective-permute-start(f32[200,128]{1,0:T(8,128)S(1)} %shard_map.80.refs_2_), channel_id=1, source_target_pairs={{0,24},{8,16},{16,8},{24,0},{1,25},{9,17},{17,9},{25,1},{2,26},{10... | collective-permute-start | bytes 307208 | tf_op jit(solution)/shard_map/ppermute | solution.py:482
  19.3 0.0 collective-permute-done.7.other_ref
  19.3 0.9 %shard_map.81 = (f32[200,128]{1,0:T(8,128)}, f32[576,128]{1,0:T(8,128)S(1)}, f32[384,128]{1,0:T(8,128)S(1)}) custom-call(f32[392,128]{1,0:T(8,128)S(1)} %get-tuple-element.85.mine_ref.refs_0_, f32[576,128]{1,0:T(8,128)S(1)} %get-tuple-element.79.coef_ref.refs_10_.refs_1_, f32[392,128]{1,0:T(8,128)S(1)} %collective-permute-done.7.other_ref), custom_call_target="tpu_custom_call" | custom-call | bytes 3000000 | tf_op jit(solution)/shard_map/pallas_call | solution.py:582
  20.2 2.6 %collective-permute-done.6.refs_3_ = f32[200,128]{1,0:T(8,128)S(1)} collective-permute-done((f32[200,128]{1,0:T(8,128)S(1)}, f32[200,128]{1,0:T(8,128)S(1)}, u32[]{:S(2)}, u32[]{:S(2)}) %collective-permute-start.6) | collective-permute-done | bytes 102432 | tf_op jit(solution)/shard_map/ppermute | solution.py:482
  22.8 1.2 %shard_map.82 = f32[12,192,128]{2,1,0:T(8,128)} custom-call(f32[392,128]{1,0:T(8,128)S(1)} %get-tuple-element.85.mine_ref.refs_0_, f32[576,128]{1,0:T(8,128)S(1)} %get-tuple-element.79.coef_ref.refs_10_.refs_1_, f32[200,128]{1,0:T(8,128)S(1)} %shard_map.80.refs_2_, f32[200,128]{1,0:T(8,128)S(1)} %collective-permute-done.6.refs_3_, ...), custom_call_target="tpu_custom_call" | custom-call | bytes 3000000 | tf_op jit(solution)/shard_map/pallas_call | solution.py:605
  (1 shorter events, 0.0 us)
Async XLA Ops:
  0.0 13.1 %copy-start = (f32[12,48]{1,0:T(8,128)S(1)}, f32[12,48]{1,0:T(8,128)}, u32[]{:S(2)}) copy-start(f32[12,48]{1,0:T(8,128)} %diff_ref) | copy-start | bytes 6916
  0.0 13.9 %copy-start.2 = (f32[127]{0:T(128)S(1)}, f32[127]{0:T(128)}, u32[]{:S(2)}) copy-start(f32[127]{0:T(128)} %param.13) | copy-start | bytes 1528
  0.0 13.9 %copy-start.1 = (f32[128]{0:T(128)S(1)}, f32[128]{0:T(128)}, u32[]{:S(2)}) copy-start(f32[128]{0:T(128)} %param.12) | copy-start | bytes 1540
  1.6 6.3 %collective-permute-start.2 = (f32[112,128]{1,0:T(8,128)S(1)}, f32[112,128]{1,0:T(8,128)S(1)}, u32[]{:S(2)}, u32[]{:S(2)}) collective-permute-start(f32[112,128]{1,0:T(8,128)S(1)} %get-tuple-element.49.refs_0_), channel_id=1, source_target_pairs={{0,3},{1,2},{2,1},{3,0},{4,7},{5,6},{6,5},{7,4},{8,11},{9,10},{10,... | collective-permute-start | bytes 172040 | tf_op jit(solution)/shard_map/ppermute | solution.py:482
  5.7 4.2 %collective-permute-start.1 = (f32[112,128]{1,0:T(8,128)S(1)}, f32[112,128]{1,0:T(8,128)S(1)}, u32[]{:S(2)}, u32[]{:S(2)}) collective-permute-start(f32[112,128]{1,0:T(8,128)S(1)} %get-tuple-element.49.refs_0_), channel_id=1, source_target_pairs={{0,2},{1,3},{2,0},{3,1},{4,6},{5,7},{6,4},{7,5},{8,10},{9,11},{10,... | collective-permute-start | bytes 172040 | tf_op jit(solution)/shard_map/ppermute | solution.py:482
  6.1 4.2 %collective-permute-start = (f32[112,128]{1,0:T(8,128)S(1)}, f32[112,128]{1,0:T(8,128)S(1)}, u32[]{:S(2)}, u32[]{:S(2)}) collective-permute-start(f32[112,128]{1,0:T(8,128)S(1)} %get-tuple-element.49.refs_0_), channel_id=1, source_target_pairs={{0,1},{1,0},{2,3},{3,2},{4,5},{5,4},{6,7},{7,6},{8,9},{9,8},{10,11... | collective-permute-start | bytes 172040 | tf_op jit(solution)/shard_map/ppermute | solution.py:482
  10.4 5.1 %collective-permute-start.3 = (f32[112,128]{1,0:T(8,128)S(1)}, f32[112,128]{1,0:T(8,128)S(1)}, u32[]{:S(2)}, u32[]{:S(2)}) collective-permute-start(f32[112,128]{1,0:T(8,128)S(1)} %get-tuple-element.54.refs_1_), channel_id=1, source_target_pairs={{0,4},{1,5},{2,6},{3,7},{4,0},{5,1},{6,2},{7,3},{8,12},{9,13},{10,... | collective-permute-start | bytes 172040 | tf_op jit(solution)/shard_map/ppermute | solution.py:482
  13.6 1.5 %collective-permute-start.4 = (f32[8,128]{1,0:T(8,128)S(1)}, f32[8,128]{1,0:T(8,128)S(1)}, u32[]{:S(2)}, u32[]{:S(2)}) collective-permute-start(f32[8,128]{1,0:T(8,128)S(1)} %get-tuple-element.68.refs_11_), channel_id=1, source_target_pairs={{0,8},{8,0},{16,24},{24,16},{1,9},{9,1},{17,25},{25,17},{2,10},{10... | collective-permute-start | bytes 12296 | tf_op jit(solution)/shard_map/ppermute | solution.py:482
  16.3 1.4 %collective-permute-start.5 = (f32[192,128]{1,0:T(8,128)S(1)}, f32[192,128]{1,0:T(8,128)S(1)}, u32[]{:S(2)}, u32[]{:S(2)}) collective-permute-start(f32[192,128]{1,0:T(8,128)S(1)} %get-tuple-element.83.mine_ref), channel_id=1, source_target_pairs={{0,8},{8,0},{16,24},{24,16},{1,9},{9,1},{17,25},{25,17},{2,10},{10... | collective-permute-start | bytes 294920 | tf_op jit(solution)/shard_map/ppermute | solution.py:482
  17.6 1.7 %collective-permute-start.7 = (f32[392,128]{1,0:T(8,128)S(1)}, f32[392,128]{1,0:T(8,128)S(1)}, u32[]{:S(2)}, u32[]{:S(2)}) collective-permute-start(f32[392,128]{1,0:T(8,128)S(1)} %get-tuple-element.85.mine_ref.refs_0_), channel_id=1, source_target_pairs={{0,8},{8,0},{16,24},{24,16},{1,9},{9,1},{17,25},{25,17},{2,10},{10... | collective-permute-start | bytes 602120 | tf_op jit(solution)/shard_map/ppermute | solution.py:482
  18.0 4.8 %collective-permute-start.6 = (f32[200,128]{1,0:T(8,128)S(1)}, f32[200,128]{1,0:T(8,128)S(1)}, u32[]{:S(2)}, u32[]{:S(2)}) collective-permute-start(f32[200,128]{1,0:T(8,128)S(1)} %shard_map.80.refs_2_), channel_id=1, source_target_pairs={{0,24},{8,16},{16,8},{24,0},{1,25},{9,17},{17,9},{25,1},{2,26},{10... | collective-permute-start | bytes 307208 | tf_op jit(solution)/shard_map/ppermute | solution.py:482

commit v6 on v5

--- a/solution.py
+++ b/solution.py
@@ -13,8 +13,8 @@
 LANES = 128
 CHUNK = 16
 PART = 64
+BLOCK = 64
 VMEM_BYTES = 16 * 2**20
-LOCAL_ROUND = 1
 
 
 def call(kernel, outs, scratch=(), in_specs=None, out_specs=None, cost=None):
@@ -101,17 +101,13 @@
             psi_f[g] = psi_f[g] + psi[g]
             phi[g] = phi[g] + t * phi_f[g]
             psi[g] = psi[g] + t * psi_f[g]
-    lanes = lax.broadcasted_iota(jnp.int32, (8, LANES), 1)
-    ends = []
+    ends, coefs = [], []
     for g in range(2):
         b = 1.0 / psi[g]
         a, d = phi[g] * b, psi_f[g] * b
         ends.append((b, d))
-        size = 8 if g == 0 else rest
-        coef = jnp.where(lanes == 0, a, jnp.where(lanes == 1, b, d))
-        for k in range(8 // size):
-            row = 2 * half + 8 * g + k * size
-            pay_ref[row : row + size, :] = coef[:size]
+        coefs.append((a, b, d))
+    pay_ref[2 * half :, :] = lon_coef_tile(coefs, rest)
 
     u = [[zero] * memb for _ in range(2)]
     flux = [[zero] * memb for _ in range(2)]
@@ -141,9 +137,21 @@
     return jnp.concatenate([tiles[:8]] * memb + [tiles[8:]] * (memb * rest // 8), axis=0)
 
 
+def lon_coef_tile(groups, rest):
+    lane = lax.broadcasted_iota(jnp.int32, (8, LANES), 1)
+    tile = jnp.zeros((8, LANES), F32)
+    for g, group in enumerate(groups):
+        for k, value in enumerate(group):
+            if g == 1:
+                value = jnp.concatenate([value[:rest]] * (8 // rest), axis=0)
+            tile = jnp.where(lane == 3 * g + k, value, tile)
+    return tile
+
+
 def lon_parts(pay, half):
     coef = pay[2 * half :]
-    return (pay[:half], pay[half : 2 * half]) + tuple(lane_of(coef, k, 16) for k in range(3))
+    coefs = tuple(jnp.concatenate([lane_of(coef, k, 8), lane_of(coef, 3 + k, 8)], axis=0) for k in range(3))
+    return (pay[:half], pay[half : 2 * half]) + coefs
 
 
 def lon_join(mine, other, right, memb, rest):
@@ -177,10 +185,9 @@
     pays, (pay_ref, *back_refs) = refs[: 1 << len(levels)], refs[1 << len(levels) :]
     (h1, h2, a, b, d), backs = lon_join_round(pays, levels, memb, rest)
     half = h1.shape[0]
-    lanes = lax.broadcasted_iota(jnp.int32, a.shape, 1)
     pay_ref[:half, :] = h1
     pay_ref[half : 2 * half, :] = h2
-    pay_ref[2 * half :, :] = jnp.where(lanes == 0, a, jnp.where(lanes == 1, b, d))
+    pay_ref[2 * half :, :] = lon_coef_tile([(a[:8], b[:8], d[:8]), (a[8:], b[8:], d[8:])], rest)
     for back_ref, (s, ca, cb) in zip(back_refs, backs):
         back_ref[:half, :] = s
         back_ref[half : half + 16, :] = ca
@@ -285,13 +292,10 @@
     return out
 
 
-def lat_sweep_kernel(*refs, levels, memb, rest, stride, paired):
+def lon_close_kernel(*refs, levels, memb, rest):
     count = 1 << len(levels)
     own_ref, pays, backs = refs[0], refs[1 : 1 + count], refs[1 + count : 1 + count + levels[0]]
-    refs = refs[1 + count + levels[0] :]
-    y_ref, phi_ref, psi_ref, weights_ref, step_ref, coef_ref, small_ref, cos_ref = refs[:8]
-    weight_ref, sum_ref = (refs[8], refs[11]) if paired else (None, None)
-    (q_ref, pay_ref), (ends, tiles) = refs[8 + paired : 10 + paired], refs[-2:]
+    weights_ref, *refs = refs[1 + count + levels[0] :]
     rows = 8 + rest
     half = memb * rows
     grow = functools.partial(lon_expand, memb=memb, rest=rest)
@@ -305,8 +309,27 @@
         u_in, u_out = jnp.where(right, middle, u_in), jnp.where(right, u_out, middle)
     oh1, _, oa, ob, _ = lon_parts(own_ref[...], half)
     f_in = grow(ob) * u_out - grow(oa) * u_in - oh1
-    weights = weights_ref[...]
-    ends[: 2 * half, :] = times_inverse(jnp.concatenate([u_in, f_in], axis=0), weights)
+    ends = times_inverse(jnp.concatenate([u_in, f_in], axis=0), weights_ref[...])
+    full = jnp.concatenate([ends, jnp.zeros((LANES - 2 * half, LANES), F32)], axis=0)
+    if len(refs) == 1:
+        refs[0][...] = full
+        return
+    response_ref, part_ref, ends_ref, sum_ref = refs
+    ends_ref[...] = full
+    high = full.astype(jnp.bfloat16)
+    low = (full - high.astype(F32)).astype(jnp.bfloat16)
+    table = jnp.concatenate(
+        [jnp.concatenate([high, low], axis=1), jnp.concatenate([high, jnp.zeros_like(low)], axis=1)], axis=0
+    )
+    out = jnp.dot(response_ref[...], table, preferred_element_type=F32)
+    sum_ref[...] = part_ref[...] + (out[:, :LANES] + out[:, LANES:])
+
+
+def lat_sweep_kernel(
+    ends, y_ref, phi_ref, psi_ref, step_ref, coef_ref, small_ref, cos_ref, q_ref, pay_ref, tiles, *, memb, stride
+):
+    rows = step_ref.shape[0] // stride - 1
+    rest, half = rows - 8, memb * rows
     for k in range(2):
         for j in range(rows):
             if j < 8:
@@ -329,13 +352,8 @@
             v = v + step_ref[at, :] * flux
         b = coef_ref[cells + c : cells + c + PART, :]
         d = coef_ref[2 * cells + c : 2 * cells + c + PART, :]
-        h1, h2 = v * b, flux - d * v
-        pay_ref[c : c + PART, :] = h1
-        pay_ref[cells + c : cells + c + PART, :] = h2
-        if paired:
-            sum_ref[c : c + PART, :] = (
-                weight_ref[c : c + PART, :] * h1 + weight_ref[cells + c : cells + c + PART, :] * h2
-            )
+        pay_ref[c : c + PART, :] = v * b
+        pay_ref[cells + c : cells + c + PART, :] = flux - d * v
     pay_ref[2 * cells :, :] = small_ref[...]
 
 
@@ -347,9 +365,11 @@
     return jnp.broadcast_to(jnp.sum(jnp.where(mask, line, 0.0), axis=1, keepdims=True), (PART, LANES))
 
 
-def lat_merge_kernel(mine_ref, coef_ref, other_ref, *outs, level, levels, memb):
+def lat_merge_kernel(mine_ref, coef_ref, other_ref, *outs, level, levels, memb, send=True):
     ready = level == levels - 2
-    if ready:
+    if not send:
+        back_ref, end_ref = outs
+    elif ready:
         pay_ref, back_ref, end_ref = outs
     else:
         pay_ref, back_ref, next_ref = outs
@@ -381,11 +401,12 @@
             h_free, h_tied = jnp.where(upper, h2, h1), jnp.where(upper, h1, h2)
             free_inv = 1.0 / free
             lean = b * free_inv
-            pay_ref[at, :] = h_tied + lean * h_free
-            stiff = tied - b * lean
             end_ref[lo, :] = lean
             end_ref[mid, :] = h_free * free_inv
-            values = (stiff,)
+            if not send:
+                continue
+            pay_ref[at, :] = h_tied + lean * h_free
+            values = (tied - b * lean,)
         else:
             pay_ref[lo, :] = h1
             pay_ref[mid, :] = h2
@@ -396,6 +417,8 @@
             chosen = jnp.where(picked, value, 0.0)
             for r in range(0, PART, 8):
                 acc[k] = acc[k] + chosen[r : r + 8]
+    if not send:
+        return
     lines = [jnp.sum(x, axis=0, keepdims=True) for x in acc[: 1 if ready else 3]]
     pay_ref[cells * (1 if ready else 2) :, :] = pack_small(lines)
 
@@ -425,6 +448,51 @@
     small_ref[...] = pack_small([jnp.sum(acc, axis=0, keepdims=True)])
 
 
+def sum_weights(weight_ref, coef_ref, c):
+    cells = coef_ref.shape[0] // 3
+    e1, e2 = (weight_ref[k * cells + c : k * cells + c + PART, :] for k in range(2))
+    b, d = (coef_ref[k * cells + c : k * cells + c + PART, :] for k in (1, 2))
+    return e1 * b - e2 * d, e2
+
+
+def lat_response_kernel(step_ref, phi_ref, psi_ref, coef_ref, cos_ref, weight_ref, out_ref, *, memb, stride):
+    cells = coef_ref.shape[0] // 3
+    rows = step_ref.shape[0] // stride - 1
+    rest, half = rows - 8, memb * rows
+    lane = lax.broadcasted_iota(jnp.int32, (8, LANES), 1)
+    member = lax.broadcasted_iota(jnp.int32, (8, LANES), 0) % memb
+    for c in range(0, cells, PART):
+        value, flux = sum_weights(weight_ref, coef_ref, c)
+        tiles = [jnp.zeros((8, LANES), F32)] * (PART // 8)
+        for j in reversed(range(rows)):
+            at = slice(j * stride + c, j * stride + c + PART)
+            flux = flux + step_ref[at, :] * value
+            value = value + jnp.broadcast_to(cos_ref[j : j + 1, :], (PART, LANES)) * flux
+            for end, source in enumerate((phi_ref, psi_ref)):
+                first = end * half + (j if j < 8 else 8 * memb + j - 8)
+                mask = lane == first + member * (8 if j < 8 else rest)
+                entry = flux * source[at, :]
+                tiles = [jnp.where(mask, entry[8 * r : 8 * r + 8], tile) for r, tile in enumerate(tiles)]
+        full = -jnp.concatenate(tiles, axis=0)
+        high = full.astype(jnp.bfloat16)
+        out_ref[c : c + PART, :LANES] = high
+        out_ref[c : c + PART, LANES:] = (full - high.astype(F32)).astype(jnp.bfloat16)
+
+
+def lat_own_kernel(y_ref, step_ref, coef_ref, cos_ref, weight_ref, out_ref, *, stride):
+    cells = coef_ref.shape[0] // 3
+    rows = step_ref.shape[0] // stride - 1
+    for c in range(0, cells, PART):
+        v = jnp.zeros((PART, LANES), F32)
+        flux = v
+        for j in range(rows):
+            at = slice(j * stride + c, j * stride + c + PART)
+            flux = flux + (jnp.broadcast_to(cos_ref[j : j + 1, :], (PART, LANES)) * v - y_ref[at, :])
+            v = v + step_ref[at, :] * flux
+        of_value, of_flux = sum_weights(weight_ref, coef_ref, c)
+        out_ref[c : c + PART, :] = of_value * v + of_flux * flux
+
+
 def pick_small(acc, value, c, memb):
     row = lax.broadcasted_iota(jnp.int32, (PART, LANES), 0) + c
     chosen = jnp.where(row == lax.broadcasted_iota(jnp.int32, (PART, LANES), 1) * memb, value, 0.0)
@@ -453,13 +521,13 @@
         )
 
     def chunk_copy(k):
-        at = pl.ds(pl.multiple_of(k * PART, PART), PART)
+        at = pl.ds(pl.multiple_of(k * BLOCK, BLOCK), BLOCK)
         return pltpu.make_async_copy(out.at[:, at, :], out_hbm.at[:, at, :], sem.at[k])
 
-    @pl.loop(0, cells // PART)
+    @pl.loop(0, cells // BLOCK)
     def _(k):
-        c = pl.multiple_of(k * PART, PART)
-        lo, mid, hi = (pl.ds(pl.multiple_of(p * cells + c, PART), PART) for p in range(3))
+        c = pl.multiple_of(k * BLOCK, BLOCK)
+        lo, mid, hi = (pl.ds(pl.multiple_of(p * cells + c, BLOCK), BLOCK) for p in range(3))
         middle = middles[lo, :]
         outer = end_ref[lo, :] * middle - end_ref[mid, :]
         u_in, u_out = jnp.where(upper, middle, outer), jnp.where(upper, outer, middle)
@@ -470,11 +538,11 @@
             u_in, u_out = jnp.where(right, middle, u_in), jnp.where(right, u_out, middle)
         flux = coef_ref[mid, :] * u_out - coef_ref[lo, :] * u_in - own_ref[lo, :]
         for j in range(rows):
-            at = pl.ds(pl.multiple_of(j * cells + c, PART), PART)
+            at = pl.ds(pl.multiple_of(j * cells + c, BLOCK), BLOCK)
             out[j, lo, :] = q_ref[at, :] + phi_ref[at, :] * u_in + psi_ref[at, :] * flux
         chunk_copy(k).start()
 
-    for k in range(cells // PART):
+    for k in range(cells // BLOCK):
         chunk_copy(k).wait()
 
 
@@ -497,7 +565,7 @@
 
     part, phi_t, psi_t, pay = call(
         lon_sweep_kernel,
-        (shape(cells, 16, LANES), shape(cols, 16, LANES), shape(cols, 16, LANES), shape(2 * half + 16, LANES)),
+        (shape(cells, 16, LANES), shape(cols, 16, LANES), shape(cols, 16, LANES), shape(2 * half + 8, LANES)),
         scratch=[
             pltpu.VMEM((cells, 16, LANES), F32),
             pltpu.VMEM((cols, 16, LANES), F32),
@@ -515,16 +583,10 @@
     paired = lat_levels == 2
     spans = lon_rounds(lon_levels)
     for index, span in enumerate(spans):
-        others = [swapped(pay, "lon", k << span[0]) for k in reversed(range(1, 1 << len(span)))][::-1]
-        if index == LOCAL_ROUND:
-            pay, part, phi_t, psi_t, lat_diffusion = lax.optimization_barrier(
-                (pay, part, phi_t, psi_t, lat_diffusion)
-            )
-            phi, psi = call(
-                functools.partial(expand_kernel, memb=memb, stride=stride, rows=rows),
-                (shape(spaced, LANES), shape(spaced, LANES)),
-                cost=cost(1),
-            )(phi_t, psi_t)
+        others = []
+        for k in range(1, 1 << len(span)):
+            others.append(swapped(pay, "lon", k << span[0]))
+        if index == 0:
             step, lat_phi, lat_psi, coef, small, cosine = call(
                 functools.partial(lat_coef_kernel, memb=memb, stride=stride, bands=bands),
                 (
@@ -537,56 +599,79 @@
                 ),
                 cost=cost(1),
             )(lat_diffusion)
+            phi, psi = call(
+                functools.partial(expand_kernel, memb=memb, stride=stride, rows=rows),
+                (shape(spaced, LANES), shape(spaced, LANES)),
+                cost=cost(1),
+            )(phi_t, psi_t)
             if paired:
                 pair_weight, pair_small = call(
                     functools.partial(lat_pair_kernel, memb=memb),
                     (shape(2 * cells, LANES), shape(8, LANES)),
                     cost=cost(1),
                 )(coef, swapped(small, "lat", 1))
+                response = call(
+                    functools.partial(lat_response_kernel, memb=memb, stride=stride),
+                    shape(cells, 2 * LANES, dtype=jnp.bfloat16),
+                    cost=cost(1),
+                )(step, phi, psi, coef, cosine, pair_weight)
             else:
-                pair_weight = pair_small = small
+                response = small
+            others, phi, psi, lat_phi, lat_psi, response = lax.optimization_barrier(
+                (others, phi, psi, lat_phi, lat_psi, response)
+            )
+        elif index == 1:
+            pay, part = lax.optimization_barrier((pay, part))
             y, weights = call(
                 functools.partial(vertical_kernel, stride=stride, rows=rows),
                 (shape(spaced, LANES), shape(2 * LANES, 2 * LANES, dtype=jnp.bfloat16)),
                 scratch=[pltpu.VMEM((8, LANES), F32)] + [pltpu.VMEM((LANES, LANES), F32)] * 3,
                 cost=cost(2),
             )(vert_diag.reshape(1, lev), vert_sub.reshape(1, lev - 1), part)
-            others, phi, psi, step, lat_phi, lat_psi, coef, cosine, y, weights, pair_weight, pair_small = (
-                lax.optimization_barrier(
-                    (others, phi, psi, step, lat_phi, lat_psi, coef, cosine, y, weights, pair_weight, pair_small)
-                )
-            )
+            own_sum = ()
+            if paired:
+                own_sum = call(
+                    functools.partial(lat_own_kernel, stride=stride), shape(cells, LANES), cost=cost(1)
+                )(y, step, coef, cosine, pair_weight)
+            others, y, weights, own_sum = lax.optimization_barrier((others, y, weights, own_sum))
         if index < len(spans) - 1:
             pay, *more = call(
                 functools.partial(lon_merge_kernel, levels=span, memb=memb, rest=rest),
-                (shape(2 * half + 16, LANES),) + (shape(half + 32, LANES),) * len(span),
+                (shape(2 * half + 8, LANES),) + (shape(half + 32, LANES),) * len(span),
                 cost=cost(1),
             )(pay, *others)
             backs += more
-    q, lat_pay, *sums = call(
-        functools.partial(
-            lat_sweep_kernel, levels=spans[-1], memb=memb, rest=rest, stride=stride, paired=paired
-        ),
-        (shape(rows * cells, LANES), shape(2 * cells + 8, LANES)) + (shape(cells, LANES),) * paired,
-        scratch=[pltpu.VMEM((2 * half + 8, LANES), F32), pltpu.VMEM((16 * rows, LANES), F32)],
+    ends, *sums = call(
+        functools.partial(lon_close_kernel, levels=spans[-1], memb=memb, rest=rest),
+        (shape(LANES, LANES),) + (shape(cells, LANES),) * paired,
         cost=cost(1),
-    )(own, pay, *others, *backs, y, phi, psi, weights, step, coef, small, cosine, *(pair_weight,) * paired)
+    )(own, pay, *others, *backs, weights, *(response, own_sum) * paired)
+
+    def sweep(ends):
+        return call(
+            functools.partial(lat_sweep_kernel, memb=memb, stride=stride),
+            (shape(rows * cells, LANES), shape(2 * cells + 8, LANES)),
+            scratch=[pltpu.VMEM((16 * rows, LANES), F32)],
+            cost=cost(1),
+        )(ends, y, phi, psi, step, coef, small, cosine)
 
     if paired:
         pay = call(lat_add_kernel, shape(cells + 8, LANES), cost=cost(1))(
             sums[0], swapped(sums[0], "lat", 1), pair_small
         )
         final = swapped(pay, "lat", 3)
-        behind, _ = lax.optimization_barrier((lat_pay, pay))
-        inner = swapped(behind, "lat", 1)
-        _, back, group = call(
-            functools.partial(lat_merge_kernel, level=0, levels=2, memb=memb),
-            (shape(cells + 8, LANES), shape(3 * cells, LANES), shape(2 * cells, LANES)),
+        behind, _ = lax.optimization_barrier((ends, pay))
+        q, lat_pay = sweep(behind)
+        inner = swapped(lat_pay, "lat", 1)
+        back, group = call(
+            functools.partial(lat_merge_kernel, level=0, levels=2, memb=memb, send=False),
+            (shape(3 * cells, LANES), shape(2 * cells, LANES)),
             cost=cost(1),
         )(lat_pay, coef, inner)
         lat_backs = [back]
-        final, group, back = lax.optimization_barrier((final, group, back))
+        final, group, back, q = lax.optimization_barrier((final, group, back, q))
     else:
+        q, lat_pay = sweep(ends)
         pay, group, lat_backs = lat_pay, coef, []
         for level in range(lat_levels - 1):
             other = swapped(pay, "lat", 1 << level)
@@ -608,7 +693,7 @@
         scratch=[
             pltpu.VMEM((rows, cells, LANES), F32),
             pltpu.VMEM((cells, LANES), F32),
-            pltpu.SemaphoreType.DMA((cells // PART,)),
+            pltpu.SemaphoreType.DMA((cells // BLOCK,)),
         ],
         out_specs=hbm_spec,
         cost=cost(1),

time: 24.2 us -> 25.5 us (1.054)
  waiting for transfers between devices: 7.8 us -> 9.12 us
  starting transfers between devices: 9.46 us -> 9.11 us
  Pallas kernels: 6.64 us -> 6.98 us
    ppermute x8, waiting for transfers between devices: 7.8 us -> 9.12 us  [swapped(): lax.ppermute(value, axis, [(s, s ^ mask) for s in range(lax.axis_size(axi...]
    ppermute x8, starting transfers between devices: 9.46 us -> 9.11 us  [swapped(): lax.ppermute(value, axis, [(s, s ^ mask) for s in range(lax.axis_size(axi...]
    pallas_call x2 -> x5, Pallas kernels: 1.57 us -> 1.85 us  [the longest x1 0.48 us: shards(): call(functools.partial(lat_response_kernel, memb=memb, stride=stride), sh...]
  transfers between devices with their start and end apart: 8 -> 8, of which waited for: 6 -> 6; matrix products, arithmetic and copies ran while one was open for 0% -> 0% of each run, Pallas kernels for 13% -> 12%
where the time goes in v6:
time: 25.5 us; the launch traced here: 25.3 us
  waiting for transfers between devices  9.12 us (36%)
  starting transfers between devices  9.11 us (36%)
  Pallas kernels  6.98 us (27%)
    ppermute x8, waiting for transfers between devices, swapped(): lax.ppermute(value, axis, [(s, s ^ mask) for s in range(lax.axis_size(axi...  9.12 us
    ppermute x8, starting transfers between devices, swapped(): lax.ppermute(value, axis, [(s, s ^ mask) for s in range(lax.axis_size(axi...  9.11 us
    pallas_call x1, Pallas kernels, shards(): call(lon_sweep_kernel, (shape(cells, 16, LANES), shape(cols, 16, LANES),...  1.57 us
    pallas_call x1, Pallas kernels, shards(): call(functools.partial(finish_kernel, levels=lat_levels, memb=memb), shap...  1.25 us
    pallas_call x1, Pallas kernels, shards(): call(functools.partial(vertical_kernel, stride=stride, rows=rows), (shape...  1.23 us
  transfers between devices with their start and end apart: 8, of which 6 were waited for; matrix products, arithmetic and copies ran while one was open for 0% of the time, Pallas kernels for 12%

profile of v6, /device:TPU:0, one launch (start us, length us, event | category | flops | bytes accessed | tf_op | source)
XLA Modules:
  0.0 25.3 jit_solution(17870873413435600014)
XLA Ops:
  0.0 0.0 copy-start
  0.0 1.6 %shard_map.73 = (f32[192,16,128]{2,1,0:T(8,128)S(1)}, f32[48,16,128]{2,1,0:T(8,128)S(1)}, f32[48,16,128]{2,1,0:T(8,128)S(1)}, f32[104,128]{1,0:T(8,128)S(1)}) custom-call(f32[12,192,128]{2,1,0:T(8,128)} %bitcast.6, f32[12,48,128]{2,1,0:T(8,128)} %grad_hbm.1, f32[12,48]{1,0:T(8,128)} %norm_hbm.1, f32[12,48]{1,0:T(8,128)} %diff_hbm.1), custom_call_target="tpu_custom_call" | custom-call | bytes 6000000 | tf_op jit(solution)/shard_map/pallas_call | solution.py:566
  1.6 3.1 %collective-permute-start = (f32[104,128]{1,0:T(8,128)S(1)}, f32[104,128]{1,0:T(8,128)S(1)}, u32[]{:S(2)}, u32[]{:S(2)}) collective-permute-start(f32[104,128]{1,0:T(8,128)S(1)} %get-tuple-element.48.refs_0_), channel_id=1, source_target_pairs={{0,1},{1,0},{2,3},{3,2},{4,5},{5,4},{6,7},{7,6},{8,9},{9,8},{10,11... | collective-permute-start | bytes 159752 | tf_op jit(solution)/shard_map/ppermute | solution.py:550
  4.6 1.6 %collective-permute-start.1 = (f32[104,128]{1,0:T(8,128)S(1)}, f32[104,128]{1,0:T(8,128)S(1)}, u32[]{:S(2)}, u32[]{:S(2)}) collective-permute-start(f32[104,128]{1,0:T(8,128)S(1)} %get-tuple-element.48.refs_0_), channel_id=1, source_target_pairs={{0,2},{1,3},{2,0},{3,1},{4,6},{5,7},{6,4},{7,5},{8,10},{9,11},{10,... | collective-permute-start | bytes 159752 | tf_op jit(solution)/shard_map/ppermute | solution.py:550
  6.2 0.0 collective-permute-start.2
  6.2 0.0 copy-done
  6.2 0.5 %shard_map.75 = (f32[2512,128]{1,0:T(8,128)S(1)}, f32[2304,128]{1,0:T(8,128)S(1)}, f32[2304,128]{1,0:T(8,128)S(1)}, f32[576,128]{1,0:T(8,128)S(1)}, f32[8,128]{1,0:T(8,128)S(1)}, /*index=5*/f32[16,128]{1,0:T(8,128)S(1)}) custom-call(f32[12,48]{1,0:T(8,128)S(1)} %copy-done), custom_call_target="tpu_custom_call" | custom-call | bytes 3000000 | tf_op jit(solution)/shard_map/pallas_call | solution.py:590
  6.7 0.1 collective-permute-start.3
  6.8 0.2 shard_map.74
  7.0 0.9 %collective-permute-done.3.other_ref = f32[8,128]{1,0:T(8,128)S(1)} collective-permute-done((f32[8,128]{1,0:T(8,128)S(1)}, f32[8,128]{1,0:T(8,128)S(1)}, u32[]{:S(2)}, u32[]{:S(2)}) %collective-permute-start.3) | collective-permute-done | bytes 4128 | tf_op jit(solution)/shard_map/ppermute | solution.py:550
  8.0 0.2 shard_map.76
  8.2 0.0 copy-start.1
  8.2 0.0 copy-start.2
  8.2 0.5 %shard_map.77.refs_6_ = bf16[192,256]{1,0:T(8,128)(2,1)S(1)} custom-call(f32[2512,128]{1,0:T(8,128)S(1)} %get-tuple-element.55.step_ref, f32[2512,128]{1,0:T(8,128)S(1)} %get-tuple-element.80.phi_ref, f32[2512,128]{1,0:T(8,128)S(1)} %get-tuple-element.81.psi_ref, f32[576,128]{1,0:T(8,128)S(1)} %get-tuple-element.56.coef_ref.refs_1_, ...), custom_call_target="tpu_custom_call" | custom-call | bytes 3000000 | tf_op jit(solution)/shard_map/pallas_call | solution.py:613
  8.7 0.0 collective-permute-done.refs_1_
  8.7 0.5 %collective-permute-done.1.refs_2_ = f32[104,128]{1,0:T(8,128)S(1)} collective-permute-done((f32[104,128]{1,0:T(8,128)S(1)}, f32[104,128]{1,0:T(8,128)S(1)}, u32[]{:S(2)}, u32[]{:S(2)}) %collective-permute-start.1) | collective-permute-done | bytes 53280 | tf_op jit(solution)/shard_map/ppermute | solution.py:550
  9.2 2.1 %collective-permute-done.2.refs_3_ = f32[104,128]{1,0:T(8,128)S(1)} collective-permute-done((f32[104,128]{1,0:T(8,128)S(1)}, f32[104,128]{1,0:T(8,128)S(1)}, u32[]{:S(2)}, u32[]{:S(2)}) %collective-permute-start.2) | collective-permute-done | bytes 53280 | tf_op jit(solution)/shard_map/ppermute | solution.py:550
  11.3 0.1 shard_map.78
  11.4 2.7 %collective-permute-start.4 = (f32[104,128]{1,0:T(8,128)S(1)}, f32[104,128]{1,0:T(8,128)S(1)}, u32[]{:S(2)}, u32[]{:S(2)}) collective-permute-start(f32[104,128]{1,0:T(8,128)S(1)} %get-tuple-element.65.refs_1_), channel_id=1, source_target_pairs={{0,4},{1,5},{2,6},{3,7},{4,0},{5,1},{6,2},{7,3},{8,12},{9,13},{10,... | collective-permute-start | bytes 159752 | tf_op jit(solution)/shard_map/ppermute | solution.py:550
  14.0 0.0 copy-done.1
  14.0 0.0 copy-done.2
  14.0 1.2 %shard_map.79 = (f32[2512,128]{1,0:T(8,128)S(1)}, bf16[256,256]{1,0:T(8,128)(2,1)S(1)}) custom-call(f32[1,128]{1,0:T(1,128)S(1)} %bitcast.4, f32[1,127]{1,0:T(1,128)S(1)} %bitcast.5, f32[192,16,128]{2,1,0:T(8,128)S(1)} %get-tuple-element.66.part_ref), custom_call_target="tpu_custom_call" | custom-call | bytes 6000000 | tf_op jit(solution)/shard_map/pallas_call | solution.py:625
  15.3 0.3 %shard_map.80.refs_7_ = f32[192,128]{1,0:T(8,128)S(1)} custom-call(f32[2512,128]{1,0:T(8,128)S(1)} %get-tuple-element.79.y_ref, f32[2512,128]{1,0:T(8,128)S(1)} %get-tuple-element.55.step_ref, f32[576,128]{1,0:T(8,128)S(1)} %get-tuple-element.56.coef_ref.refs_1_, f32[16,128]{1,0:T(8,128)S(1)} %get-tuple-element.57.cos_ref, ...), custom_call_target="tpu_custom_call" | custom-call | bytes 3000000 | tf_op jit(solution)/shard_map/pallas_call | solution.py:633
  15.6 1.4 %collective-permute-done.4.refs_2_ = f32[104,128]{1,0:T(8,128)S(1)} collective-permute-done((f32[104,128]{1,0:T(8,128)S(1)}, f32[104,128]{1,0:T(8,128)S(1)}, u32[]{:S(2)}, u32[]{:S(2)}) %collective-permute-start.4) | collective-permute-done | bytes 53280 | tf_op jit(solution)/shard_map/ppermute | solution.py:550
  16.9 0.4 %shard_map.81 = (f32[128,128]{1,0:T(8,128)S(1)}, f32[192,128]{1,0:T(8,128)S(1)}) custom-call(f32[104,128]{1,0:T(8,128)S(1)} %get-tuple-element.48.refs_0_, f32[104,128]{1,0:T(8,128)S(1)} %get-tuple-element.65.refs_1_, f32[104,128]{1,0:T(8,128)S(1)} %collective-permute-done.4.refs_2_, f32[80,128]{1,0:T(8,128)S(1)} %get-tuple-element.70.refs_3_, ...), custom_call_target="tpu_custom_call" | custom-call | bytes 3000000 | tf_op jit(solution)/shard_map/pallas_call | solution.py:644
  17.4 0.1 collective-permute-start.5
  17.5 1.3 %collective-permute-done.5.other_ref = f32[192,128]{1,0:T(8,128)S(1)} collective-permute-done((f32[192,128]{1,0:T(8,128)S(1)}, f32[192,128]{1,0:T(8,128)S(1)}, u32[]{:S(2)}, u32[]{:S(2)}) %collective-permute-start.5) | collective-permute-done | bytes 98336 | tf_op jit(solution)/shard_map/ppermute | solution.py:550
  18.8 0.4 %shard_map.83 = (f32[2304,128]{1,0:T(8,128)S(1)}, f32[392,128]{1,0:T(8,128)S(1)}) custom-call(f32[128,128]{1,0:T(8,128)S(1)} %get-tuple-element.78.ends, f32[2512,128]{1,0:T(8,128)S(1)} %get-tuple-element.79.y_ref, f32[2512,128]{1,0:T(8,128)S(1)} %get-tuple-element.80.phi_ref, f32[2512,128]{1,0:T(8,128)S(1)} %get-tuple-element.81.psi_ref, ...), custom_call_target="tpu_custom_call" | custom-call | bytes 3000000 | tf_op jit(solution)/shard_map/pallas_call | solution.py:651
  19.2 0.2 collective-permute-start.7
  19.4 1.5 %collective-permute-start.6 = (f32[200,128]{1,0:T(8,128)S(1)}, f32[200,128]{1,0:T(8,128)S(1)}, u32[]{:S(2)}, u32[]{:S(2)}) collective-permute-start(f32[200,128]{1,0:T(8,128)S(1)} %shard_map.82.refs_2_), channel_id=1, source_target_pairs={{0,24},{8,16},{16,8},{24,0},{1,25},{9,17},{17,9},{25,1},{2,26},{10... | collective-permute-start | bytes 307208 | tf_op jit(solution)/shard_map/ppermute | solution.py:550
  20.9 0.0 collective-permute-done.7.other_ref
  20.9 0.2 shard_map.84
  21.1 3.0 %collective-permute-done.6.refs_3_ = f32[200,128]{1,0:T(8,128)S(1)} collective-permute-done((f32[200,128]{1,0:T(8,128)S(1)}, f32[200,128]{1,0:T(8,128)S(1)}, u32[]{:S(2)}, u32[]{:S(2)}) %collective-permute-start.6) | collective-permute-done | bytes 102432 | tf_op jit(solution)/shard_map/ppermute | solution.py:550
  24.1 1.2 %shard_map.85 = f32[12,192,128]{2,1,0:T(8,128)} custom-call(f32[392,128]{1,0:T(8,128)S(1)} %get-tuple-element.82.mine_ref.refs_0_, f32[576,128]{1,0:T(8,128)S(1)} %get-tuple-element.56.coef_ref.refs_1_, f32[200,128]{1,0:T(8,128)S(1)} %shard_map.82.refs_2_, f32[200,128]{1,0:T(8,128)S(1)} %collective-permute-done.6.refs_3_, ...), custom_call_target="tpu_custom_call" | custom-call | bytes 3000000 | tf_op jit(solution)/shard_map/pallas_call | solution.py:690
  (1 shorter events, 0.0 us)
Async XLA Ops:
  0.0 6.2 %copy-start = (f32[12,48]{1,0:T(8,128)S(1)}, f32[12,48]{1,0:T(8,128)}, u32[]{:S(2)}) copy-start(f32[12,48]{1,0:T(8,128)} %diff_ref.1) | copy-start | bytes 6916
  1.6 7.1 %collective-permute-start = (f32[104,128]{1,0:T(8,128)S(1)}, f32[104,128]{1,0:T(8,128)S(1)}, u32[]{:S(2)}, u32[]{:S(2)}) collective-permute-start(f32[104,128]{1,0:T(8,128)S(1)} %get-tuple-element.48.refs_0_), channel_id=1, source_target_pairs={{0,1},{1,0},{2,3},{3,2},{4,5},{5,4},{6,7},{7,6},{8,9},{9,8},{10,11... | collective-permute-start | bytes 159752 | tf_op jit(solution)/shard_map/ppermute | solution.py:550
  4.6 4.5 %collective-permute-start.1 = (f32[104,128]{1,0:T(8,128)S(1)}, f32[104,128]{1,0:T(8,128)S(1)}, u32[]{:S(2)}, u32[]{:S(2)}) collective-permute-start(f32[104,128]{1,0:T(8,128)S(1)} %get-tuple-element.48.refs_0_), channel_id=1, source_target_pairs={{0,2},{1,3},{2,0},{3,1},{4,6},{5,7},{6,4},{7,5},{8,10},{9,11},{10,... | collective-permute-start | bytes 159752 | tf_op jit(solution)/shard_map/ppermute | solution.py:550
  6.2 5.0 %collective-permute-start.2 = (f32[104,128]{1,0:T(8,128)S(1)}, f32[104,128]{1,0:T(8,128)S(1)}, u32[]{:S(2)}, u32[]{:S(2)}) collective-permute-start(f32[104,128]{1,0:T(8,128)S(1)} %get-tuple-element.48.refs_0_), channel_id=1, source_target_pairs={{0,3},{1,2},{2,1},{3,0},{4,7},{5,6},{6,5},{7,4},{8,11},{9,10},{10,... | collective-permute-start | bytes 159752 | tf_op jit(solution)/shard_map/ppermute | solution.py:550
  6.7 1.2 %collective-permute-start.3 = (f32[8,128]{1,0:T(8,128)S(1)}, f32[8,128]{1,0:T(8,128)S(1)}, u32[]{:S(2)}, u32[]{:S(2)}) collective-permute-start(f32[8,128]{1,0:T(8,128)S(1)} %get-tuple-element.58.small_ref), channel_id=1, source_target_pairs={{0,8},{8,0},{16,24},{24,16},{1,9},{9,1},{17,25},{25,17},{2,10},{10... | collective-permute-start | bytes 12296 | tf_op jit(solution)/shard_map/ppermute | solution.py:550
  8.2 5.9 %copy-start.1 = (f32[128]{0:T(128)S(1)}, f32[128]{0:T(128)}, u32[]{:S(2)}) copy-start(f32[128]{0:T(128)} %param.12) | copy-start | bytes 1540
  8.2 5.9 %copy-start.2 = (f32[127]{0:T(128)S(1)}, f32[127]{0:T(128)}, u32[]{:S(2)}) copy-start(f32[127]{0:T(128)} %param.13) | copy-start | bytes 1528
  11.4 5.6 %collective-permute-start.4 = (f32[104,128]{1,0:T(8,128)S(1)}, f32[104,128]{1,0:T(8,128)S(1)}, u32[]{:S(2)}, u32[]{:S(2)}) collective-permute-start(f32[104,128]{1,0:T(8,128)S(1)} %get-tuple-element.65.refs_1_), channel_id=1, source_target_pairs={{0,4},{1,5},{2,6},{3,7},{4,0},{5,1},{6,2},{7,3},{8,12},{9,13},{10,... | collective-permute-start | bytes 159752 | tf_op jit(solution)/shard_map/ppermute | solution.py:550
  17.4 1.4 %collective-permute-start.5 = (f32[192,128]{1,0:T(8,128)S(1)}, f32[192,128]{1,0:T(8,128)S(1)}, u32[]{:S(2)}, u32[]{:S(2)}) collective-permute-start(f32[192,128]{1,0:T(8,128)S(1)} %get-tuple-element.76.mine_ref), channel_id=1, source_target_pairs={{0,8},{8,0},{16,24},{24,16},{1,9},{9,1},{17,25},{25,17},{2,10},{10... | collective-permute-start | bytes 294920 | tf_op jit(solution)/shard_map/ppermute | solution.py:550
  19.2 1.7 %collective-permute-start.7 = (f32[392,128]{1,0:T(8,128)S(1)}, f32[392,128]{1,0:T(8,128)S(1)}, u32[]{:S(2)}, u32[]{:S(2)}) collective-permute-start(f32[392,128]{1,0:T(8,128)S(1)} %get-tuple-element.82.mine_ref.refs_0_), channel_id=1, source_target_pairs={{0,8},{8,0},{16,24},{24,16},{1,9},{9,1},{17,25},{25,17},{2,10},{10... | collective-permute-start | bytes 602120 | tf_op jit(solution)/shard_map/ppermute | solution.py:550
  19.4 4.6 %collective-permute-start.6 = (f32[200,128]{1,0:T(8,128)S(1)}, f32[200,128]{1,0:T(8,128)S(1)}, u32[]{:S(2)}, u32[]{:S(2)}) collective-permute-start(f32[200,128]{1,0:T(8,128)S(1)} %shard_map.82.refs_2_), channel_id=1, source_target_pairs={{0,24},{8,16},{16,8},{24,0},{1,25},{9,17},{17,9},{25,1},{2,26},{10... | collective-permute-start | bytes 307208 | tf_op jit(solution)/shard_map/ppermute | solution.py:550

commit v7 on v6

--- a/solution.py
+++ b/solution.py
@@ -604,21 +604,9 @@
                 (shape(spaced, LANES), shape(spaced, LANES)),
                 cost=cost(1),
             )(phi_t, psi_t)
-            if paired:
-                pair_weight, pair_small = call(
-                    functools.partial(lat_pair_kernel, memb=memb),
-                    (shape(2 * cells, LANES), shape(8, LANES)),
-                    cost=cost(1),
-                )(coef, swapped(small, "lat", 1))
-                response = call(
-                    functools.partial(lat_response_kernel, memb=memb, stride=stride),
-                    shape(cells, 2 * LANES, dtype=jnp.bfloat16),
-                    cost=cost(1),
-                )(step, phi, psi, coef, cosine, pair_weight)
-            else:
-                response = small
-            others, phi, psi, lat_phi, lat_psi, response = lax.optimization_barrier(
-                (others, phi, psi, lat_phi, lat_psi, response)
+            other_small = swapped(small, "lat", 1)
+            others, phi, psi, lat_phi, lat_psi, other_small = lax.optimization_barrier(
+                (others, phi, psi, lat_phi, lat_psi, other_small)
             )
         elif index == 1:
             pay, part = lax.optimization_barrier((pay, part))
@@ -628,12 +616,25 @@
                 scratch=[pltpu.VMEM((8, LANES), F32)] + [pltpu.VMEM((LANES, LANES), F32)] * 3,
                 cost=cost(2),
             )(vert_diag.reshape(1, lev), vert_sub.reshape(1, lev - 1), part)
+            if paired:
+                pair_weight, pair_small = call(
+                    functools.partial(lat_pair_kernel, memb=memb),
+                    (shape(2 * cells, LANES), shape(8, LANES)),
+                    cost=cost(1),
+                )(coef, other_small)
+                response = call(
+                    functools.partial(lat_response_kernel, memb=memb, stride=stride),
+                    shape(cells, 2 * LANES, dtype=jnp.bfloat16),
+                    cost=cost(1),
+                )(step, phi, psi, coef, cosine, pair_weight)
+            else:
+                response = small
             own_sum = ()
             if paired:
                 own_sum = call(
                     functools.partial(lat_own_kernel, stride=stride), shape(cells, LANES), cost=cost(1)
                 )(y, step, coef, cosine, pair_weight)
-            others, y, weights, own_sum = lax.optimization_barrier((others, y, weights, own_sum))
+            others, y, weights, own_sum, response = lax.optimization_barrier((others, y, weights, own_sum, response))
         if index < len(spans) - 1:
             pay, *more = call(
                 functools.partial(lon_merge_kernel, levels=span, memb=memb, rest=rest),

time: 25.5 us -> 25.5 us (level)
  no operation moved by 1% of the time
where the time goes in v7:
time: 25.5 us; the launch traced here: 25.3 us
  waiting for transfers between devices  9.16 us (36%)
  starting transfers between devices  9.1 us (36%)
  Pallas kernels  6.91 us (27%)
    ppermute x8, waiting for transfers between devices, swapped(): lax.ppermute(value, axis, [(s, s ^ mask) for s in range(lax.axis_size(axi...  9.16 us
    ppermute x8, starting transfers between devices, swapped(): lax.ppermute(value, axis, [(s, s ^ mask) for s in range(lax.axis_size(axi...  9.1 us
    pallas_call x1, Pallas kernels, shards(): call(lon_sweep_kernel, (shape(cells, 16, LANES), shape(cols, 16, LANES),...  1.57 us
    pallas_call x1, Pallas kernels, shards(): call(functools.partial(vertical_kernel, stride=stride, rows=rows), (shape...  1.22 us
    pallas_call x1, Pallas kernels, shards(): call(functools.partial(finish_kernel, levels=lat_levels, memb=memb), shap...  1.22 us
  transfers between devices with their start and end apart: 8, of which 6 were waited for; matrix products, arithmetic and copies ran while one was open for 0% of the time, Pallas kernels for 12%

profile of v7, /device:TPU:0, one launch (start us, length us, event | category | flops | bytes accessed | tf_op | source)
XLA Modules:
  0.0 25.3 jit_solution(3572541923048396909)
XLA Ops:
  0.0 0.0 copy-start
  0.0 0.0 copy-start.1
  0.0 0.0 copy-start.2
  0.0 1.6 %shard_map.73 = (f32[192,16,128]{2,1,0:T(8,128)S(1)}, f32[48,16,128]{2,1,0:T(8,128)S(1)}, f32[48,16,128]{2,1,0:T(8,128)S(1)}, f32[104,128]{1,0:T(8,128)S(1)}) custom-call(f32[12,192,128]{2,1,0:T(8,128)} %bitcast.6, f32[12,48,128]{2,1,0:T(8,128)} %grad_hbm.1, f32[12,48]{1,0:T(8,128)} %norm_hbm.1, f32[12,48]{1,0:T(8,128)} %diff_hbm.1), custom_call_target="tpu_custom_call" | custom-call | bytes 6000000 | tf_op jit(solution)/shard_map/pallas_call | solution.py:566
  1.6 3.1 %collective-permute-start = (f32[104,128]{1,0:T(8,128)S(1)}, f32[104,128]{1,0:T(8,128)S(1)}, u32[]{:S(2)}, u32[]{:S(2)}) collective-permute-start(f32[104,128]{1,0:T(8,128)S(1)} %get-tuple-element.49.refs_0_), channel_id=1, source_target_pairs={{0,1},{1,0},{2,3},{3,2},{4,5},{5,4},{6,7},{7,6},{8,9},{9,8},{10,11... | collective-permute-start | bytes 159752 | tf_op jit(solution)/shard_map/ppermute | solution.py:550
  4.6 1.6 %collective-permute-start.1 = (f32[104,128]{1,0:T(8,128)S(1)}, f32[104,128]{1,0:T(8,128)S(1)}, u32[]{:S(2)}, u32[]{:S(2)}) collective-permute-start(f32[104,128]{1,0:T(8,128)S(1)} %get-tuple-element.49.refs_0_), channel_id=1, source_target_pairs={{0,2},{1,3},{2,0},{3,1},{4,6},{5,7},{6,4},{7,5},{8,10},{9,11},{10,... | collective-permute-start | bytes 159752 | tf_op jit(solution)/shard_map/ppermute | solution.py:550
  6.2 0.0 collective-permute-start.2
  6.2 0.0 copy-done
  6.2 0.5 %shard_map.75 = (f32[2512,128]{1,0:T(8,128)S(1)}, f32[2304,128]{1,0:T(8,128)S(1)}, f32[2304,128]{1,0:T(8,128)S(1)}, f32[576,128]{1,0:T(8,128)S(1)}, f32[8,128]{1,0:T(8,128)S(1)}, /*index=5*/f32[16,128]{1,0:T(8,128)S(1)}) custom-call(f32[12,48]{1,0:T(8,128)S(1)} %copy-done), custom_call_target="tpu_custom_call" | custom-call | bytes 3000000 | tf_op jit(solution)/shard_map/pallas_call | solution.py:590
  6.7 0.1 collective-permute-start.3
  6.8 0.2 shard_map.74
  7.0 0.9 %collective-permute-done.3.other_ref = f32[8,128]{1,0:T(8,128)S(1)} collective-permute-done((f32[8,128]{1,0:T(8,128)S(1)}, f32[8,128]{1,0:T(8,128)S(1)}, u32[]{:S(2)}, u32[]{:S(2)}) %collective-permute-start.3) | collective-permute-done | bytes 4128 | tf_op jit(solution)/shard_map/ppermute | solution.py:550
  8.0 0.0 collective-permute-done.refs_1_
  8.0 1.2 %collective-permute-done.1.refs_2_ = f32[104,128]{1,0:T(8,128)S(1)} collective-permute-done((f32[104,128]{1,0:T(8,128)S(1)}, f32[104,128]{1,0:T(8,128)S(1)}, u32[]{:S(2)}, u32[]{:S(2)}) %collective-permute-start.1) | collective-permute-done | bytes 53280 | tf_op jit(solution)/shard_map/ppermute | solution.py:550
  9.2 2.1 %collective-permute-done.2.refs_3_ = f32[104,128]{1,0:T(8,128)S(1)} collective-permute-done((f32[104,128]{1,0:T(8,128)S(1)}, f32[104,128]{1,0:T(8,128)S(1)}, u32[]{:S(2)}, u32[]{:S(2)}) %collective-permute-start.2) | collective-permute-done | bytes 53280 | tf_op jit(solution)/shard_map/ppermute | solution.py:550
  11.3 0.1 shard_map.76
  11.4 2.7 %collective-permute-start.4 = (f32[104,128]{1,0:T(8,128)S(1)}, f32[104,128]{1,0:T(8,128)S(1)}, u32[]{:S(2)}, u32[]{:S(2)}) collective-permute-start(f32[104,128]{1,0:T(8,128)S(1)} %get-tuple-element.62.refs_1_), channel_id=1, source_target_pairs={{0,4},{1,5},{2,6},{3,7},{4,0},{5,1},{6,2},{7,3},{8,12},{9,13},{10,... | collective-permute-start | bytes 159752 | tf_op jit(solution)/shard_map/ppermute | solution.py:550
  14.0 0.2 shard_map.78
  14.3 0.0 copy-done.1
  14.3 0.0 copy-done.2
  14.3 1.2 %shard_map.77 = (f32[2512,128]{1,0:T(8,128)S(1)}, bf16[256,256]{1,0:T(8,128)(2,1)S(1)}) custom-call(f32[1,128]{1,0:T(1,128)S(1)} %bitcast.4, f32[1,127]{1,0:T(1,128)S(1)} %bitcast.5, f32[192,16,128]{2,1,0:T(8,128)S(1)} %get-tuple-element.63.part_ref), custom_call_target="tpu_custom_call" | custom-call | bytes 6000000 | tf_op jit(solution)/shard_map/pallas_call | solution.py:613
  15.5 0.3 %shard_map.79.refs_7_ = f32[192,128]{1,0:T(8,128)S(1)} custom-call(f32[2512,128]{1,0:T(8,128)S(1)} %get-tuple-element.83.y_ref, f32[2512,128]{1,0:T(8,128)S(1)} %get-tuple-element.66.step_ref, f32[576,128]{1,0:T(8,128)S(1)} %get-tuple-element.67.coef_ref.refs_1_, f32[16,128]{1,0:T(8,128)S(1)} %get-tuple-element.68.cos_ref, ...), custom_call_target="tpu_custom_call" | custom-call | bytes 3000000 | tf_op jit(solution)/shard_map/pallas_call | solution.py:634
  15.8 0.5 %shard_map.80.refs_6_ = bf16[192,256]{1,0:T(8,128)(2,1)S(1)} custom-call(f32[2512,128]{1,0:T(8,128)S(1)} %get-tuple-element.66.step_ref, f32[2512,128]{1,0:T(8,128)S(1)} %get-tuple-element.71.phi_ref, f32[2512,128]{1,0:T(8,128)S(1)} %get-tuple-element.72.psi_ref, f32[576,128]{1,0:T(8,128)S(1)} %get-tuple-element.67.coef_ref.refs_1_, ...), custom_call_target="tpu_custom_call" | custom-call | bytes 3000000 | tf_op jit(solution)/shard_map/pallas_call | solution.py:625
  16.3 0.7 %collective-permute-done.4.refs_2_ = f32[104,128]{1,0:T(8,128)S(1)} collective-permute-done((f32[104,128]{1,0:T(8,128)S(1)}, f32[104,128]{1,0:T(8,128)S(1)}, u32[]{:S(2)}, u32[]{:S(2)}) %collective-permute-start.4) | collective-permute-done | bytes 53280 | tf_op jit(solution)/shard_map/ppermute | solution.py:550
  16.9 0.4 %shard_map.81 = (f32[128,128]{1,0:T(8,128)S(1)}, f32[192,128]{1,0:T(8,128)S(1)}) custom-call(f32[104,128]{1,0:T(8,128)S(1)} %get-tuple-element.49.refs_0_, f32[104,128]{1,0:T(8,128)S(1)} %get-tuple-element.62.refs_1_, f32[104,128]{1,0:T(8,128)S(1)} %collective-permute-done.4.refs_2_, f32[80,128]{1,0:T(8,128)S(1)} %get-tuple-element.74.refs_3_, ...), custom_call_target="tpu_custom_call" | custom-call | bytes 3000000 | tf_op jit(solution)/shard_map/pallas_call | solution.py:645
  17.4 0.1 collective-permute-start.5
  17.5 1.3 %collective-permute-done.5.other_ref = f32[192,128]{1,0:T(8,128)S(1)} collective-permute-done((f32[192,128]{1,0:T(8,128)S(1)}, f32[192,128]{1,0:T(8,128)S(1)}, u32[]{:S(2)}, u32[]{:S(2)}) %collective-permute-start.5) | collective-permute-done | bytes 98336 | tf_op jit(solution)/shard_map/ppermute | solution.py:550
  18.8 0.4 %shard_map.83 = (f32[2304,128]{1,0:T(8,128)S(1)}, f32[392,128]{1,0:T(8,128)S(1)}) custom-call(f32[128,128]{1,0:T(8,128)S(1)} %get-tuple-element.82.ends, f32[2512,128]{1,0:T(8,128)S(1)} %get-tuple-element.83.y_ref, f32[2512,128]{1,0:T(8,128)S(1)} %get-tuple-element.71.phi_ref, f32[2512,128]{1,0:T(8,128)S(1)} %get-tuple-element.72.psi_ref, ...), custom_call_target="tpu_custom_call" | custom-call | bytes 3000000 | tf_op jit(solution)/shard_map/pallas_call | solution.py:652
  19.2 0.2 collective-permute-start.7
  19.4 1.5 %collective-permute-start.6 = (f32[200,128]{1,0:T(8,128)S(1)}, f32[200,128]{1,0:T(8,128)S(1)}, u32[]{:S(2)}, u32[]{:S(2)}) collective-permute-start(f32[200,128]{1,0:T(8,128)S(1)} %shard_map.82.refs_2_), channel_id=1, source_target_pairs={{0,24},{8,16},{16,8},{24,0},{1,25},{9,17},{17,9},{25,1},{2,26},{10... | collective-permute-start | bytes 307208 | tf_op jit(solution)/shard_map/ppermute | solution.py:550
  20.9 0.0 collective-permute-done.7.other_ref
  20.9 0.2 shard_map.84
  21.1 3.0 %collective-permute-done.6.refs_3_ = f32[200,128]{1,0:T(8,128)S(1)} collective-permute-done((f32[200,128]{1,0:T(8,128)S(1)}, f32[200,128]{1,0:T(8,128)S(1)}, u32[]{:S(2)}, u32[]{:S(2)}) %collective-permute-start.6) | collective-permute-done | bytes 102432 | tf_op jit(solution)/shard_map/ppermute | solution.py:550
  24.1 1.2 %shard_map.85 = f32[12,192,128]{2,1,0:T(8,128)} custom-call(f32[392,128]{1,0:T(8,128)S(1)} %get-tuple-element.84.mine_ref.refs_0_, f32[576,128]{1,0:T(8,128)S(1)} %get-tuple-element.67.coef_ref.refs_1_, f32[200,128]{1,0:T(8,128)S(1)} %shard_map.82.refs_2_, f32[200,128]{1,0:T(8,128)S(1)} %collective-permute-done.6.refs_3_, ...), custom_call_target="tpu_custom_call" | custom-call | bytes 3000000 | tf_op jit(solution)/shard_map/pallas_call | solution.py:691
  (1 shorter events, 0.0 us)
Async XLA Ops:
  0.0 6.2 %copy-start = (f32[12,48]{1,0:T(8,128)S(1)}, f32[12,48]{1,0:T(8,128)}, u32[]{:S(2)}) copy-start(f32[12,48]{1,0:T(8,128)} %diff_ref.1) | copy-start | bytes 6916
  0.0 14.3 %copy-start.1 = (f32[128]{0:T(128)S(1)}, f32[128]{0:T(128)}, u32[]{:S(2)}) copy-start(f32[128]{0:T(128)} %param.12) | copy-start | bytes 1540
  0.0 14.3 %copy-start.2 = (f32[127]{0:T(128)S(1)}, f32[127]{0:T(128)}, u32[]{:S(2)}) copy-start(f32[127]{0:T(128)} %param.13) | copy-start | bytes 1528
  1.6 6.4 %collective-permute-start = (f32[104,128]{1,0:T(8,128)S(1)}, f32[104,128]{1,0:T(8,128)S(1)}, u32[]{:S(2)}, u32[]{:S(2)}) collective-permute-start(f32[104,128]{1,0:T(8,128)S(1)} %get-tuple-element.49.refs_0_), channel_id=1, source_target_pairs={{0,1},{1,0},{2,3},{3,2},{4,5},{5,4},{6,7},{7,6},{8,9},{9,8},{10,11... | collective-permute-start | bytes 159752 | tf_op jit(solution)/shard_map/ppermute | solution.py:550
  4.6 4.5 %collective-permute-start.1 = (f32[104,128]{1,0:T(8,128)S(1)}, f32[104,128]{1,0:T(8,128)S(1)}, u32[]{:S(2)}, u32[]{:S(2)}) collective-permute-start(f32[104,128]{1,0:T(8,128)S(1)} %get-tuple-element.49.refs_0_), channel_id=1, source_target_pairs={{0,2},{1,3},{2,0},{3,1},{4,6},{5,7},{6,4},{7,5},{8,10},{9,11},{10,... | collective-permute-start | bytes 159752 | tf_op jit(solution)/shard_map/ppermute | solution.py:550
  6.2 5.0 %collective-permute-start.2 = (f32[104,128]{1,0:T(8,128)S(1)}, f32[104,128]{1,0:T(8,128)S(1)}, u32[]{:S(2)}, u32[]{:S(2)}) collective-permute-start(f32[104,128]{1,0:T(8,128)S(1)} %get-tuple-element.49.refs_0_), channel_id=1, source_target_pairs={{0,3},{1,2},{2,1},{3,0},{4,7},{5,6},{6,5},{7,4},{8,11},{9,10},{10,... | collective-permute-start | bytes 159752 | tf_op jit(solution)/shard_map/ppermute | solution.py:550
  6.7 1.2 %collective-permute-start.3 = (f32[8,128]{1,0:T(8,128)S(1)}, f32[8,128]{1,0:T(8,128)S(1)}, u32[]{:S(2)}, u32[]{:S(2)}) collective-permute-start(f32[8,128]{1,0:T(8,128)S(1)} %get-tuple-element.56.small_ref), channel_id=1, source_target_pairs={{0,8},{8,0},{16,24},{24,16},{1,9},{9,1},{17,25},{25,17},{2,10},{10... | collective-permute-start | bytes 12296 | tf_op jit(solution)/shard_map/ppermute | solution.py:550
  11.4 5.6 %collective-permute-start.4 = (f32[104,128]{1,0:T(8,128)S(1)}, f32[104,128]{1,0:T(8,128)S(1)}, u32[]{:S(2)}, u32[]{:S(2)}) collective-permute-start(f32[104,128]{1,0:T(8,128)S(1)} %get-tuple-element.62.refs_1_), channel_id=1, source_target_pairs={{0,4},{1,5},{2,6},{3,7},{4,0},{5,1},{6,2},{7,3},{8,12},{9,13},{10,... | collective-permute-start | bytes 159752 | tf_op jit(solution)/shard_map/ppermute | solution.py:550
  17.4 1.4 %collective-permute-start.5 = (f32[192,128]{1,0:T(8,128)S(1)}, f32[192,128]{1,0:T(8,128)S(1)}, u32[]{:S(2)}, u32[]{:S(2)}) collective-permute-start(f32[192,128]{1,0:T(8,128)S(1)} %get-tuple-element.80.mine_ref), channel_id=1, source_target_pairs={{0,8},{8,0},{16,24},{24,16},{1,9},{9,1},{17,25},{25,17},{2,10},{10... | collective-permute-start | bytes 294920 | tf_op jit(solution)/shard_map/ppermute | solution.py:550
  19.2 1.7 %collective-permute-start.7 = (f32[392,128]{1,0:T(8,128)S(1)}, f32[392,128]{1,0:T(8,128)S(1)}, u32[]{:S(2)}, u32[]{:S(2)}) collective-permute-start(f32[392,128]{1,0:T(8,128)S(1)} %get-tuple-element.84.mine_ref.refs_0_), channel_id=1, source_target_pairs={{0,8},{8,0},{16,24},{24,16},{1,9},{9,1},{17,25},{25,17},{2,10},{10... | collective-permute-start | bytes 602120 | tf_op jit(solution)/shard_map/ppermute | solution.py:550
  19.4 4.6 %collective-permute-start.6 = (f32[200,128]{1,0:T(8,128)S(1)}, f32[200,128]{1,0:T(8,128)S(1)}, u32[]{:S(2)}, u32[]{:S(2)}) collective-permute-start(f32[200,128]{1,0:T(8,128)S(1)} %shard_map.82.refs_2_), channel_id=1, source_target_pairs={{0,24},{8,16},{16,8},{24,0},{1,25},{9,17},{17,9},{25,1},{2,26},{10... | collective-permute-start | bytes 307208 | tf_op jit(solution)/shard_map/ppermute | solution.py:550

commit v8 on v7

--- a/solution.py
+++ b/solution.py
@@ -544,6 +544,48 @@
 
     for k in range(cells // BLOCK):
         chunk_copy(k).wait()
+
+
+def lat_fold_kernel(own_ref, coef_ref, end_ref, back_ref, q_ref, phi_ref, psi_ref, base_ref, gain_ref):
+    cells = coef_ref.shape[0] // 3
+    rows = q_ref.shape[0] // cells
+    right, upper = on_right("lat", 0), on_right("lat", 1)
+    for c in range(0, cells, PART):
+        lo, mid, hi = (slice(k * cells + c, k * cells + c + PART) for k in range(3))
+        one, zero = jnp.ones((PART, LANES), F32), jnp.zeros((PART, LANES), F32)
+        inner, outer = (one, zero), (end_ref[lo, :], -end_ref[mid, :])
+        u_in = [jnp.where(upper, i, o) for i, o in zip(inner, outer)]
+        u_out = [jnp.where(upper, o, i) for i, o in zip(inner, outer)]
+        between = [back_ref[mid, :] * i + back_ref[hi, :] * o for i, o in zip(u_in, u_out)]
+        between[1] = between[1] - back_ref[lo, :]
+        u_in, u_out = (
+            [jnp.where(right, b, i) for b, i in zip(between, u_in)],
+            [jnp.where(right, o, b) for b, o in zip(between, u_out)],
+        )
+        flux = [coef_ref[mid, :] * o - coef_ref[lo, :] * i for i, o in zip(u_in, u_out)]
+        flux[1] = flux[1] - own_ref[lo, :]
+        for j in range(rows):
+            at = slice(j * cells + c, j * cells + c + PART)
+            gain_ref[at, :] = phi_ref[at, :] * u_in[0] + psi_ref[at, :] * flux[0]
+            base_ref[at, :] = q_ref[at, :] + phi_ref[at, :] * u_in[1] + psi_ref[at, :] * flux[1]
+
+
+def finish_pair_kernel(mine_ref, other_ref, base_ref, gain_ref, out_hbm, out, sem, *, memb):
+    cells = mine_ref.shape[0] - 8
+    rows = base_ref.shape[0] // cells
+    soft = 1.0 / (mine_ref[cells:, :] + other_ref[cells:, :])
+    copies = []
+    for k, c in enumerate(range(0, cells, PART)):
+        lo = slice(c, c + PART)
+        middle = -(mine_ref[lo, :] + other_ref[lo, :]) * unpack_small(soft, 0, c, memb)
+        for j in range(rows):
+            at = slice(j * cells + c, j * cells + c + PART)
+            out[j, lo, :] = base_ref[at, :] + gain_ref[at, :] * middle
+        block = pl.ds(c, PART)
+        copies.append(pltpu.make_async_copy(out.at[:, block, :], out_hbm.at[:, block, :], sem.at[k]))
+        copies[-1].start()
+    for copy in copies:
+        copy.wait()
 
 
 def swapped(value, axis, mask):
@@ -669,8 +711,18 @@
             (shape(3 * cells, LANES), shape(2 * cells, LANES)),
             cost=cost(1),
         )(lat_pay, coef, inner)
-        lat_backs = [back]
-        final, group, back, q = lax.optimization_barrier((final, group, back, q))
+        base, gain = call(
+            lat_fold_kernel, (shape(rows * cells, LANES), shape(rows * cells, LANES)), cost=cost(1)
+        )(lat_pay, coef, group, back, q, lat_phi, lat_psi)
+        final, base, gain = lax.optimization_barrier((final, base, gain))
+        out = call(
+            functools.partial(finish_pair_kernel, memb=memb),
+            shape(rows, cells, LANES),
+            scratch=[pltpu.VMEM((rows, cells, LANES), F32), pltpu.SemaphoreType.DMA((cells // PART,))],
+            out_specs=hbm_spec,
+            cost=cost(1),
+        )(pay, final, base, gain)
+        return out.reshape(rows, cols, memb, lev)
     else:
         q, lat_pay = sweep(ends)
         pay, group, lat_backs = lat_pay, coef, []

time: 25.5 us -> 25.5 us (level)
  waiting for transfers between devices: 9.16 us -> 8.76 us
  Pallas kernels: 6.91 us -> 7.27 us
    ppermute x8, waiting for transfers between devices: 9.16 us -> 8.76 us  [swapped(): lax.ppermute(value, axis, [(s, s ^ mask) for s in range(lax.axis_size(axi...]
    pallas_call x1 -> x2, Pallas kernels: 1.22 us -> 1.59 us  [the longest x1 1.19 us: shards(): call(functools.partial(finish_pair_kernel, memb=memb), shape(rows, cells,...]
  transfers between devices with their start and end apart: 8 -> 8, of which waited for: 6 -> 6; matrix products, arithmetic and copies ran while one was open for 0% -> 0% of each run, Pallas kernels for 12% -> 14%
where the time goes in v8:
time: 25.5 us; the launch traced here: 25.3 us
  starting transfers between devices  9.1 us (36%)
  waiting for transfers between devices  8.76 us (34%)
  Pallas kernels  7.27 us (29%)
    ppermute x8, starting transfers between devices, swapped(): lax.ppermute(value, axis, [(s, s ^ mask) for s in range(lax.axis_size(axi...  9.1 us
    ppermute x8, waiting for transfers between devices, swapped(): lax.ppermute(value, axis, [(s, s ^ mask) for s in range(lax.axis_size(axi...  8.76 us
    pallas_call x1, Pallas kernels, shards(): call(lon_sweep_kernel, (shape(cells, 16, LANES), shape(cols, 16, LANES),...  1.57 us
    pallas_call x1, Pallas kernels, shards(): call(functools.partial(vertical_kernel, stride=stride, rows=rows), (shape...  1.22 us
    pallas_call x1, Pallas kernels, shards(): call(functools.partial(finish_pair_kernel, memb=memb), shape(rows, cells,...  1.19 us
  transfers between devices with their start and end apart: 8, of which 6 were waited for; matrix products, arithmetic and copies ran while one was open for 0% of the time, Pallas kernels for 14%

profile of v8, /device:TPU:0, one launch (start us, length us, event | category | flops | bytes accessed | tf_op | source)
XLA Modules:
  0.0 25.3 jit_solution(15859814972921660568)
XLA Ops:
  0.0 0.0 copy-start
  0.0 0.0 copy-start.1
  0.0 0.0 copy-start.2
  0.0 1.6 %shard_map.73 = (f32[192,16,128]{2,1,0:T(8,128)S(1)}, f32[48,16,128]{2,1,0:T(8,128)S(1)}, f32[48,16,128]{2,1,0:T(8,128)S(1)}, f32[104,128]{1,0:T(8,128)S(1)}) custom-call(f32[12,192,128]{2,1,0:T(8,128)} %bitcast.6, f32[12,48,128]{2,1,0:T(8,128)} %grad_hbm.1, f32[12,48]{1,0:T(8,128)} %norm_hbm.1, f32[12,48]{1,0:T(8,128)} %diff_hbm.1), custom_call_target="tpu_custom_call" | custom-call | bytes 6000000 | tf_op jit(solution)/shard_map/pallas_call | solution.py:608
  1.6 3.1 %collective-permute-start = (f32[104,128]{1,0:T(8,128)S(1)}, f32[104,128]{1,0:T(8,128)S(1)}, u32[]{:S(2)}, u32[]{:S(2)}) collective-permute-start(f32[104,128]{1,0:T(8,128)S(1)} %get-tuple-element.51.refs_0_), channel_id=1, source_target_pairs={{0,1},{1,0},{2,3},{3,2},{4,5},{5,4},{6,7},{7,6},{8,9},{9,8},{10,11... | collective-permute-start | bytes 159752 | tf_op jit(solution)/shard_map/ppermute | solution.py:592
  4.6 1.6 %collective-permute-start.1 = (f32[104,128]{1,0:T(8,128)S(1)}, f32[104,128]{1,0:T(8,128)S(1)}, u32[]{:S(2)}, u32[]{:S(2)}) collective-permute-start(f32[104,128]{1,0:T(8,128)S(1)} %get-tuple-element.51.refs_0_), channel_id=1, source_target_pairs={{0,2},{1,3},{2,0},{3,1},{4,6},{5,7},{6,4},{7,5},{8,10},{9,11},{10,... | collective-permute-start | bytes 159752 | tf_op jit(solution)/shard_map/ppermute | solution.py:592
  6.2 0.0 collective-permute-start.2
  6.2 0.0 copy-done
  6.2 0.5 %shard_map.75 = (f32[2512,128]{1,0:T(8,128)S(1)}, f32[2304,128]{1,0:T(8,128)S(1)}, f32[2304,128]{1,0:T(8,128)S(1)}, f32[576,128]{1,0:T(8,128)S(1)}, f32[8,128]{1,0:T(8,128)S(1)}, /*index=5*/f32[16,128]{1,0:T(8,128)S(1)}) custom-call(f32[12,48]{1,0:T(8,128)S(1)} %copy-done), custom_call_target="tpu_custom_call" | custom-call | bytes 3000000 | tf_op jit(solution)/shard_map/pallas_call | solution.py:632
  6.7 0.1 collective-permute-start.3
  6.8 0.2 shard_map.74
  7.0 0.9 %collective-permute-done.3.other_ref = f32[8,128]{1,0:T(8,128)S(1)} collective-permute-done((f32[8,128]{1,0:T(8,128)S(1)}, f32[8,128]{1,0:T(8,128)S(1)}, u32[]{:S(2)}, u32[]{:S(2)}) %collective-permute-start.3) | collective-permute-done | bytes 4128 | tf_op jit(solution)/shard_map/ppermute | solution.py:592
  8.0 0.0 collective-permute-done.refs_1_
  8.0 1.2 %collective-permute-done.1.refs_2_ = f32[104,128]{1,0:T(8,128)S(1)} collective-permute-done((f32[104,128]{1,0:T(8,128)S(1)}, f32[104,128]{1,0:T(8,128)S(1)}, u32[]{:S(2)}, u32[]{:S(2)}) %collective-permute-start.1) | collective-permute-done | bytes 53280 | tf_op jit(solution)/shard_map/ppermute | solution.py:592
  9.2 2.1 %collective-permute-done.2.refs_3_ = f32[104,128]{1,0:T(8,128)S(1)} collective-permute-done((f32[104,128]{1,0:T(8,128)S(1)}, f32[104,128]{1,0:T(8,128)S(1)}, u32[]{:S(2)}, u32[]{:S(2)}) %collective-permute-start.2) | collective-permute-done | bytes 53280 | tf_op jit(solution)/shard_map/ppermute | solution.py:592
  11.3 0.1 shard_map.76
  11.4 2.7 %collective-permute-start.4 = (f32[104,128]{1,0:T(8,128)S(1)}, f32[104,128]{1,0:T(8,128)S(1)}, u32[]{:S(2)}, u32[]{:S(2)}) collective-permute-start(f32[104,128]{1,0:T(8,128)S(1)} %get-tuple-element.64.refs_1_), channel_id=1, source_target_pairs={{0,4},{1,5},{2,6},{3,7},{4,0},{5,1},{6,2},{7,3},{8,12},{9,13},{10,... | collective-permute-start | bytes 159752 | tf_op jit(solution)/shard_map/ppermute | solution.py:592
  14.0 0.2 shard_map.78
  14.3 0.0 copy-done.1
  14.3 0.0 copy-done.2
  14.3 1.2 %shard_map.77 = (f32[2512,128]{1,0:T(8,128)S(1)}, bf16[256,256]{1,0:T(8,128)(2,1)S(1)}) custom-call(f32[1,128]{1,0:T(1,128)S(1)} %bitcast.4, f32[1,127]{1,0:T(1,128)S(1)} %bitcast.5, f32[192,16,128]{2,1,0:T(8,128)S(1)} %get-tuple-element.65.part_ref), custom_call_target="tpu_custom_call" | custom-call | bytes 6000000 | tf_op jit(solution)/shard_map/pallas_call | solution.py:655
  15.5 0.3 %shard_map.79.refs_7_ = f32[192,128]{1,0:T(8,128)S(1)} custom-call(f32[2512,128]{1,0:T(8,128)S(1)} %get-tuple-element.85.y_ref, f32[2512,128]{1,0:T(8,128)S(1)} %get-tuple-element.68.step_ref, f32[576,128]{1,0:T(8,128)S(1)} %get-tuple-element.69.coef_ref, f32[16,128]{1,0:T(8,128)S(1)} %get-tuple-element.70.cos_ref, f32[384,128]{1,0:T(8,128)S(1)} %get-tuple-element.72.weight_ref), custom_call_target="tpu_custom_call" | custom-call | bytes 3000000 | tf_op jit(solution)/shard_map/pallas_call | solution.py:676
  15.8 0.5 %shard_map.80.refs_6_ = bf16[192,256]{1,0:T(8,128)(2,1)S(1)} custom-call(f32[2512,128]{1,0:T(8,128)S(1)} %get-tuple-element.68.step_ref, f32[2512,128]{1,0:T(8,128)S(1)} %get-tuple-element.73.phi_ref, f32[2512,128]{1,0:T(8,128)S(1)} %get-tuple-element.74.psi_ref, f32[576,128]{1,0:T(8,128)S(1)} %get-tuple-element.69.coef_ref, ...), custom_call_target="tpu_custom_call" | custom-call | bytes 3000000 | tf_op jit(solution)/shard_map/pallas_call | solution.py:667
  16.3 0.7 %collective-permute-done.4.refs_2_ = f32[104,128]{1,0:T(8,128)S(1)} collective-permute-done((f32[104,128]{1,0:T(8,128)S(1)}, f32[104,128]{1,0:T(8,128)S(1)}, u32[]{:S(2)}, u32[]{:S(2)}) %collective-permute-start.4) | collective-permute-done | bytes 53280 | tf_op jit(solution)/shard_map/ppermute | solution.py:592
  16.9 0.4 %shard_map.81 = (f32[128,128]{1,0:T(8,128)S(1)}, f32[192,128]{1,0:T(8,128)S(1)}) custom-call(f32[104,128]{1,0:T(8,128)S(1)} %get-tuple-element.51.refs_0_, f32[104,128]{1,0:T(8,128)S(1)} %get-tuple-element.64.refs_1_, f32[104,128]{1,0:T(8,128)S(1)} %collective-permute-done.4.refs_2_, f32[80,128]{1,0:T(8,128)S(1)} %get-tuple-element.76.refs_3_, ...), custom_call_target="tpu_custom_call" | custom-call | bytes 3000000 | tf_op jit(solution)/shard_map/pallas_call | solution.py:687
  17.4 0.1 collective-permute-start.5
  17.5 1.3 %collective-permute-done.5.other_ref = f32[192,128]{1,0:T(8,128)S(1)} collective-permute-done((f32[192,128]{1,0:T(8,128)S(1)}, f32[192,128]{1,0:T(8,128)S(1)}, u32[]{:S(2)}, u32[]{:S(2)}) %collective-permute-start.5) | collective-permute-done | bytes 98336 | tf_op jit(solution)/shard_map/ppermute | solution.py:592
  18.8 0.4 %shard_map.83 = (f32[2304,128]{1,0:T(8,128)S(1)}, f32[392,128]{1,0:T(8,128)S(1)}) custom-call(f32[128,128]{1,0:T(8,128)S(1)} %get-tuple-element.84.ends, f32[2512,128]{1,0:T(8,128)S(1)} %get-tuple-element.85.y_ref, f32[2512,128]{1,0:T(8,128)S(1)} %get-tuple-element.73.phi_ref, f32[2512,128]{1,0:T(8,128)S(1)} %get-tuple-element.74.psi_ref, ...), custom_call_target="tpu_custom_call" | custom-call | bytes 3000000 | tf_op jit(solution)/shard_map/pallas_call | solution.py:694
  19.2 0.2 collective-permute-start.7
  19.4 1.5 %collective-permute-start.6 = (f32[200,128]{1,0:T(8,128)S(1)}, f32[200,128]{1,0:T(8,128)S(1)}, u32[]{:S(2)}, u32[]{:S(2)}) collective-permute-start(f32[200,128]{1,0:T(8,128)S(1)} %shard_map.82.mine_ref), channel_id=1, source_target_pairs={{0,24},{8,16},{16,8},{24,0},{1,25},{9,17},{17,9},{25,1},{2,26},{10... | collective-permute-start | bytes 307208 | tf_op jit(solution)/shard_map/ppermute | solution.py:592
  20.9 0.0 collective-permute-done.7.other_ref
  20.9 0.2 shard_map.84
  21.1 0.4 %shard_map.85 = (f32[2304,128]{1,0:T(8,128)S(1)}, f32[2304,128]{1,0:T(8,128)S(1)}) custom-call(f32[392,128]{1,0:T(8,128)S(1)} %get-tuple-element.86.mine_ref.own_ref, f32[576,128]{1,0:T(8,128)S(1)} %get-tuple-element.69.coef_ref, f32[384,128]{1,0:T(8,128)S(1)} %get-tuple-element.87.end_ref, f32[576,128]{1,0:T(8,128)S(1)} %get-tuple-element.88.back_ref, ...), custom_call_target="tpu_custom_call" | custom-call | bytes 3000000 | tf_op jit(solution)/shard_map/pallas_call | solution.py:714
  21.5 2.6 %collective-permute-done.6.other_ref = f32[200,128]{1,0:T(8,128)S(1)} collective-permute-done((f32[200,128]{1,0:T(8,128)S(1)}, f32[200,128]{1,0:T(8,128)S(1)}, u32[]{:S(2)}, u32[]{:S(2)}) %collective-permute-start.6) | collective-permute-done | bytes 102432 | tf_op jit(solution)/shard_map/ppermute | solution.py:592
  24.1 1.2 %shard_map.86 = f32[12,192,128]{2,1,0:T(8,128)} custom-call(f32[200,128]{1,0:T(8,128)S(1)} %shard_map.82.mine_ref, f32[200,128]{1,0:T(8,128)S(1)} %collective-permute-done.6.other_ref, f32[2304,128]{1,0:T(8,128)S(1)} %get-tuple-element.95.base_ref, f32[2304,128]{1,0:T(8,128)S(1)} %get-tuple-element.96.gain_ref), custom_call_target="tpu_custom_call" | custom-call | bytes 3000000 | tf_op jit(solution)/shard_map/pallas_call | solution.py:718
  (1 shorter events, 0.0 us)
Async XLA Ops:
  0.0 6.2 %copy-start = (f32[12,48]{1,0:T(8,128)S(1)}, f32[12,48]{1,0:T(8,128)}, u32[]{:S(2)}) copy-start(f32[12,48]{1,0:T(8,128)} %diff_ref.1) | copy-start | bytes 6916
  0.0 14.3 %copy-start.1 = (f32[128]{0:T(128)S(1)}, f32[128]{0:T(128)}, u32[]{:S(2)}) copy-start(f32[128]{0:T(128)} %param.12) | copy-start | bytes 1540
  0.0 14.3 %copy-start.2 = (f32[127]{0:T(128)S(1)}, f32[127]{0:T(128)}, u32[]{:S(2)}) copy-start(f32[127]{0:T(128)} %param.13) | copy-start | bytes 1528
  1.6 6.4 %collective-permute-start = (f32[104,128]{1,0:T(8,128)S(1)}, f32[104,128]{1,0:T(8,128)S(1)}, u32[]{:S(2)}, u32[]{:S(2)}) collective-permute-start(f32[104,128]{1,0:T(8,128)S(1)} %get-tuple-element.51.refs_0_), channel_id=1, source_target_pairs={{0,1},{1,0},{2,3},{3,2},{4,5},{5,4},{6,7},{7,6},{8,9},{9,8},{10,11... | collective-permute-start | bytes 159752 | tf_op jit(solution)/shard_map/ppermute | solution.py:592
  4.6 4.5 %collective-permute-start.1 = (f32[104,128]{1,0:T(8,128)S(1)}, f32[104,128]{1,0:T(8,128)S(1)}, u32[]{:S(2)}, u32[]{:S(2)}) collective-permute-start(f32[104,128]{1,0:T(8,128)S(1)} %get-tuple-element.51.refs_0_), channel_id=1, source_target_pairs={{0,2},{1,3},{2,0},{3,1},{4,6},{5,7},{6,4},{7,5},{8,10},{9,11},{10,... | collective-permute-start | bytes 159752 | tf_op jit(solution)/shard_map/ppermute | solution.py:592
  6.2 5.0 %collective-permute-start.2 = (f32[104,128]{1,0:T(8,128)S(1)}, f32[104,128]{1,0:T(8,128)S(1)}, u32[]{:S(2)}, u32[]{:S(2)}) collective-permute-start(f32[104,128]{1,0:T(8,128)S(1)} %get-tuple-element.51.refs_0_), channel_id=1, source_target_pairs={{0,3},{1,2},{2,1},{3,0},{4,7},{5,6},{6,5},{7,4},{8,11},{9,10},{10,... | collective-permute-start | bytes 159752 | tf_op jit(solution)/shard_map/ppermute | solution.py:592
  6.7 1.2 %collective-permute-start.3 = (f32[8,128]{1,0:T(8,128)S(1)}, f32[8,128]{1,0:T(8,128)S(1)}, u32[]{:S(2)}, u32[]{:S(2)}) collective-permute-start(f32[8,128]{1,0:T(8,128)S(1)} %get-tuple-element.58.small_ref), channel_id=1, source_target_pairs={{0,8},{8,0},{16,24},{24,16},{1,9},{9,1},{17,25},{25,17},{2,10},{10... | collective-permute-start | bytes 12296 | tf_op jit(solution)/shard_map/ppermute | solution.py:592
  11.4 5.6 %collective-permute-start.4 = (f32[104,128]{1,0:T(8,128)S(1)}, f32[104,128]{1,0:T(8,128)S(1)}, u32[]{:S(2)}, u32[]{:S(2)}) collective-permute-start(f32[104,128]{1,0:T(8,128)S(1)} %get-tuple-element.64.refs_1_), channel_id=1, source_target_pairs={{0,4},{1,5},{2,6},{3,7},{4,0},{5,1},{6,2},{7,3},{8,12},{9,13},{10,... | collective-permute-start | bytes 159752 | tf_op jit(solution)/shard_map/ppermute | solution.py:592
  17.4 1.4 %collective-permute-start.5 = (f32[192,128]{1,0:T(8,128)S(1)}, f32[192,128]{1,0:T(8,128)S(1)}, u32[]{:S(2)}, u32[]{:S(2)}) collective-permute-start(f32[192,128]{1,0:T(8,128)S(1)} %get-tuple-element.81.mine_ref), channel_id=1, source_target_pairs={{0,8},{8,0},{16,24},{24,16},{1,9},{9,1},{17,25},{25,17},{2,10},{10... | collective-permute-start | bytes 294920 | tf_op jit(solution)/shard_map/ppermute | solution.py:592
  19.2 1.7 %collective-permute-start.7 = (f32[392,128]{1,0:T(8,128)S(1)}, f32[392,128]{1,0:T(8,128)S(1)}, u32[]{:S(2)}, u32[]{:S(2)}) collective-permute-start(f32[392,128]{1,0:T(8,128)S(1)} %get-tuple-element.86.mine_ref.own_ref), channel_id=1, source_target_pairs={{0,8},{8,0},{16,24},{24,16},{1,9},{9,1},{17,25},{25,17},{2,10},{10... | collective-permute-start | bytes 602120 | tf_op jit(solution)/shard_map/ppermute | solution.py:592
  19.4 4.6 %collective-permute-start.6 = (f32[200,128]{1,0:T(8,128)S(1)}, f32[200,128]{1,0:T(8,128)S(1)}, u32[]{:S(2)}, u32[]{:S(2)}) collective-permute-start(f32[200,128]{1,0:T(8,128)S(1)} %shard_map.82.mine_ref), channel_id=1, source_target_pairs={{0,24},{8,16},{16,8},{24,0},{1,25},{9,17},{17,9},{25,1},{2,26},{10... | collective-permute-start | bytes 307208 | tf_op jit(solution)/shard_map/ppermute | solution.py:592
